TPU v7x, 32 devices: a whole 2x2x4 slice. The times are simulated.
32 devices in a mesh: dp: 4 (over z), ctx: 8 (over y, x, core).
Axes of the slice: x: 2, y: 2, z: 4, core: 2. Of those that a mesh axis runs over, the one named last changes fastest.
Arguments:
- head_inputs: bfloat16 [4, 1024, 2048], P('dp', 'ctx'), may hold values from -11 to 11
- entry_operator: bfloat16 [4, 1024, 128], P('dp', 'ctx'), may hold values from -3 to 3
- memory_readout: bfloat16 [4, 1024, 128], P('dp', 'ctx'), may hold values from -0.1796875 to 0.1796875
- unshifted_strides: float32 [4, 64, 1024], P('dp', None, 'ctx'), may hold values from -1.5 to 5.5, as said below
- log_decay_rates: float32 [64], P('dp'), may hold values from -11 to -2
- stride_shift: float32 [64], P('dp'), may hold values from -0.5 to 0.5
- bypass_coefficients: float32 [64], P('dp'), may hold values from 0.5 to 1.5
- result_cotangent: bfloat16 [4, 1024, 2048], P('dp', 'ctx'), may hold values from -26 to 26
Outputs:
- output: bfloat16 [4, 1024, 2048], P('dp', 'ctx')
- channels_grad: bfloat16 [4, 1024, 2048], P('dp', 'ctx')
- input_map_grad: float32 [4, 1024, 128], P('dp', 'ctx')
- output_map_grad: float32 [4, 1024, 128], P('dp', 'ctx')
- timestep_raw_gradient: float32 [4, 64, 1024], P('dp', None, 'ctx')
- a_log_grad: float32 [64], P('dp')
- bias_grad: float32 [64], P('dp')
- skip_grad: float32 [64], P('dp')
Inputs may be any that keep to these rules, and one draw needn't show every extreme that they name: `unshifted_strides`: step sizes are moderate at most positions, with a few large ones in each sequence.
All inputs are finite; a program needn't handle non-finite values.
Results may differ from a plain program's by a relative error of at most 0.001.
Values sent between devices are 32-bit elements; how exact they have to be, the bound alone decides.
No kernel may reach another device: no remote copies, remote signals or barrier semaphores. Data moves between devices by JAX's collectives and lax.ppermute only.
A program may use at most 128 MiB of HBM per device.

v0:
```python
import jax
import jax.numpy as jnp
from jax import lax
from jax.sharding import PartitionSpec as P

maximal_accuracy = lax.Precision.HIGHEST


def carried_in(array, axis, combine, identity, reverse):
    devices, position = (lax.axis_size(axis), lax.axis_index(axis))
    everything = jax.tree.map(lambda part: lax.all_gather(part, axis), array)
    start = jax.tree.map(
        lambda part, zero: jnp.broadcast_to(jnp.asarray(zero, part.dtype), part.shape),
        array,
        identity,
    )

    def hop(k, before):
        at = devices - 1 - k if reverse else k
        reached = at > position if reverse else at < position
        new = combine(before, jax.tree.map(lambda part: part[at], everything))
        return jax.tree.map(lambda a, b: jnp.where(reached, a, b), new, before)

    return lax.fori_loop(0, devices, hop, start)


def local_part(xg, write_operator, gram, dtr, rate_log, bias, skip):
    count = xg.shape[0]
    heads = dtr.shape[0]
    xg3 = xg.reshape(count, heads, -1)
    step = jax.nn.softplus(dtr + bias[:, None])
    logdecay = -jnp.exp(rate_log)[:, None] * step
    cum = jnp.cumsum(logdecay, axis=1)
    rows = lax.broadcasted_iota(jnp.int32, (count, count), 0)
    cols = lax.broadcasted_iota(jnp.int32, (count, count), 1)
    diff = cum[:, :, None] - cum[:, None, :]
    seg = jnp.exp(jnp.where((rows >= cols)[None], diff, -jnp.inf))
    weights = gram[None] * seg * step[:, None, :]
    inner = jnp.einsum("hts,shp->thp", weights, xg3, precision=maximal_accuracy)
    y_part = inner + skip[None, :, None] * xg3
    tail = jnp.exp(cum[:, -1:] - cum) * step
    scaled = xg3 * tail.T[:, :, None]
    state = jnp.einsum("shp,sn->hpn", scaled, write_operator, precision=maximal_accuracy)
    return (y_part, state, jnp.exp(cum))


def combine(earlier, later):
    return (earlier[0] * later[0], later[0][:, None, None] * earlier[1] + later[1])


def local(
    head_inputs,
    entry_operator,
    memory_readout,
    unshifted_strides,
    log_decay_rates,
    stride_shift,
    bypass_coefficients,
    result_cotangent,
):
    rate_all, full_bias_vector, skip_all = (
        lax.all_gather(log_decay_rates, "dp", axis=0, tiled=True),
        lax.all_gather(stride_shift, "dp", axis=0, tiled=True),
        lax.all_gather(bypass_coefficients, "dp", axis=0, tiled=True),
    )
    tokens = head_inputs[0].astype(jnp.float32)
    write_operator = entry_operator[0].astype(jnp.float32)
    cmat = memory_readout[0].astype(jnp.float32)
    gram = lax.dot_general(
        memory_readout[0],
        entry_operator[0],
        (((1,), (1,)), ((), ())),
        preferred_element_type=jnp.float32,
    )
    raw = unshifted_strides[0]
    upstream = result_cotangent[0].astype(jnp.float32)
    heads = raw.shape[0]
    width = tokens.shape[1] // heads
    count = tokens.shape[0]
    parts = 1
    per = heads // parts
    output_pieces, dx_list, dt_list, rate_list, bias_list, skip_list = ([], [], [], [], [], [])
    cmat_grad = jnp.zeros_like(cmat)
    (y_part, state, growth_factor), backward = jax.vjp(
        local_part, tokens, write_operator, gram, raw, rate_all, full_bias_vector, skip_all
    )
    ends = growth_factor[:, -1]
    identity = (jnp.ones_like(ends), jnp.zeros_like(state))
    _, carried = carried_in((ends, state), "ctx", combine, identity, False)
    readout = jnp.einsum("tn,hpn->thp", cmat, carried, precision=maximal_accuracy)
    output_pieces.append(y_part + growth_factor.T[:, :, None] * readout)
    g_group = upstream.reshape(count, per, width)
    dread = growth_factor.T[:, :, None] * g_group
    growth_grad = jnp.einsum("thp,thp->ht", g_group, readout, precision=maximal_accuracy)
    local_grad = jnp.einsum("thp,tn->hpn", dread, cmat, precision=maximal_accuracy)
    cmat_grad = cmat_grad + jnp.einsum("thp,hpn->tn", dread, carried, precision=maximal_accuracy)
    _, later = carried_in((ends, local_grad), "ctx", combine, identity, True)
    end_grad = jnp.sum(later * carried, axis=(1, 2))
    growth_grad = growth_grad.at[:, -1].add(end_grad)
    grads = backward((g_group, later, growth_grad))
    dx_list.append(grads[0])
    bmat_grad = grads[1]
    gram_grad = grads[2]
    dt_list.append(grads[3])
    rate_list.append(grads[4])
    bias_list.append(grads[5])
    skip_list.append(grads[6])
    cmat_grad = cmat_grad + jnp.dot(gram_grad, write_operator, precision=maximal_accuracy)
    bmat_grad = bmat_grad + jnp.dot(gram_grad.T, cmat, precision=maximal_accuracy)
    core = output_pieces[0].reshape(count, heads * width)
    channels_grad = dx_list[0]
    timestep_raw_gradient = dt_list[0]
    rate_grad = rate_list[0]
    bias_grad = bias_list[0]
    skip_grad = skip_list[0]
    totals = lax.psum((rate_grad, bias_grad, skip_grad), "ctx")
    owned = (
        lax.psum_scatter(totals[0], "dp", scatter_dimension=0, tiled=True),
        lax.psum_scatter(totals[1], "dp", scatter_dimension=0, tiled=True),
        lax.psum_scatter(totals[2], "dp", scatter_dimension=0, tiled=True),
    )
    return (
        core.astype(jnp.bfloat16)[None],
        channels_grad.astype(jnp.bfloat16)[None],
        bmat_grad[None],
        cmat_grad[None],
        timestep_raw_gradient[None],
        owned[0],
        owned[1],
        owned[2],
    )


def solution(mesh):
    placed = (
        P("dp", "ctx", None),
        P("dp", "ctx", None),
        P("dp", "ctx", None),
        P("dp", None, "ctx"),
        P("dp"),
        P("dp"),
        P("dp"),
        P("dp", "ctx", None),
    )
    return jax.shard_map(
        local,
        mesh=mesh,
        in_specs=placed,
        out_specs=(
            P("dp", "ctx", None),
            P("dp", "ctx", None),
            P("dp", "ctx", None),
            P("dp", "ctx", None),
            P("dp", None, "ctx"),
            P("dp"),
            P("dp"),
            P("dp"),
        ),
        check_vma=False,
    )
```

profile of v0, /device:TPU:0, one launch (start us, length us, event | category | flops | bytes accessed | tf_op | source)
XLA Modules:
  0.0 215.4 jit_solution(5517105314016589985)
XLA Ops:
  10.9 13.5 %all-reduce.10 = (f32[64]{0:T(128)S(1)}, f32[64]{0:T(128)S(1)}) all-reduce(f32[64]{0:T(128)S(1)} %dynamic-update-slice.4, f32[64]{0:T(128)S(1)} %dynamic-update-slice.3), channel_id=1, replica_groups=mesh['dp'=4,'ctx'=8] {'dp'}, use_global_device_ids=true, to_apply=%add.2 | all-reduce | flops 128 | bytes 1024
  30.2 1.6 fusion.57
  31.9 1.6 fusion.62
  35.2 12.4 %all-reduce.4 = f32[512]{0:T(512)S(1)} all-reduce(f32[512]{0:T(512)S(1)} %dynamic-update-slice.6), channel_id=2, replica_groups=mesh['dp'=4,'ctx'=8] {'ctx'}, use_global_device_ids=true, to_apply=%add.4 | all-reduce | flops 512 | bytes 4096
  50.1 34.4 %all-gather.8.cloned.1.call-done = f32[512,32,128]{2,1,0:T(8,128)} async-done(((f32[64,32,128]{2,1,0:T(8,128)}), f32[512,32,128]{2,1,0:T(8,128)}) %all-gather.8.cloned.1.call-update) | async-done | bytes 8388624 | tf_op jit(solution)/shard_map/all_gather | solution.py:11
  84.5 12.6 %while.32 = (s32[]{:T(128)}, f32[64,32,128]{2,1,0:T(8,128)S(1)}, s32[]{:T(128)}, f32[8,64]{1,0:T(8,128)S(1)}, f32[8,64,32,128]{3,2,1,0:T(8,128)}, /*index=5*/s32[]{:T(128)}, s32[]{:T(128)}, s32[]{:T(128)}, s32[]{:T(128)}) while((s32[]{:T(128)}, f32[64,32,128]{2,1,0:T(8,128)S(1)}, s32[]{:T(128)}, f32[8,64]{1,0:T(8,128)S(1)}, ...), condition=%wide.region_4.5_spmd.clone, body=%wide.region_3.4_spmd.clone.sunk | while | flops 1048584 | bytes 3146663 | solution.py:24
  86.0 1.5 fusion.91
  87.6 1.5 fusion.91
  89.1 1.5 fusion.91
  90.7 1.5 fusion.91
  92.2 1.6 fusion.91
  93.9 1.6 fusion.91
  95.5 1.6 fusion.91
  97.1 2.5 %convolution_bitcast_fusion.2 = f32[128,128]{1,0:T(8,128)} fusion(f32[64,32,128]{2,1,0:T(8,128)S(1)} %get-tuple-element.247, bf16[128,64,32]{0,2,1:T(8,128)(2,1)S(1)} %bitcast.147, f32[128,64]{0,1:T(8,128)S(1)} %get-tuple-element.351), kind=kOutput, calls=%fused_computation.49 | convolution fusion | flops 403177472 | bytes 1671168 | tf_op jit(solution)/shard_map/transpose(jvp(shp,sn->hpn))/dot_general | solution.py:43
  99.5 1.7 fusion.47
  101.2 39.4 %all-gather.6.cloned.1.call-done = f32[512,32,128]{2,1,0:T(8,128)} async-done(((f32[64,32,128]{2,1,0:T(8,128)}), f32[512,32,128]{2,1,0:T(8,128)}) %all-gather.6.cloned.1.call-update) | async-done | bytes 8388624 | tf_op jit(solution)/shard_map/all_gather | solution.py:11
  140.7 12.2 %while.31 = (s32[]{:T(128)}, f32[64,32,128]{2,1,0:T(8,128)S(1)}, s32[]{:T(128)}, f32[8,64]{1,0:T(8,128)S(1)}, f32[8,64,32,128]{3,2,1,0:T(8,128)}, /*index=5*/s32[]{:T(128)}, s32[]{:T(128)}) while((s32[]{:T(128)}, f32[64,32,128]{2,1,0:T(8,128)S(1)}, s32[]{:T(128)}, f32[8,64]{1,0:T(8,128)S(1)}, f32[8,64,32,128]{3,2,1,0:T(8,128)}, ...), condition=%wide.region_2.3_spmd.clone, body=%wide.region_1.2_spmd.clone.sunk | while | flops 1048580 | bytes 3146601 | solution.py:24
  143.7 1.5 fusion.90
  146.8 1.5 fusion.90
  149.8 1.5 fusion.90
  151.4 1.5 fusion.90
  153.5 1.6 fusion.48
  156.4 5.5 %fusion.9 = (f32[64,128]{1,0:T(8,128)S(1)}, f32[64,128]{1,0:T(8,128)S(1)}, f32[64,128]{1,0:T(8,128)}, f32[128,128]{1,0:T(8,128)S(1)}) fusion(f32[64,128]{1,0:T(8,128)} %get-tuple-element.349, f32[64,128]{1,0:T(8,128)S(1)} %reduce_window_sum.22, f32[128,128]{1,0:T(8,128)} %fusion.65, pred[128,128]{1,0:T(8,128)(4,1)S(1)} %iota_compare_fusion, ...), kind=kOutput, calls=%fused_computation.15 | convolution fusion | flops 80699392 | bytes 1359872 | tf_op jit(solution)/shard_map/transpose(jvp(hts,shp->thp))/dot_general | solution.py:39
  162.6 2.0 reduce_window_sum.23
  164.6 1.6 fusion.71
  166.9 12.0 %all-reduce.9 = (f32[64]{0:T(128)S(1)}, f32[64]{0:T(128)S(1)}, f32[64]{0:T(128)S(1)}, f32[64]{0:T(128)S(1)}) all-reduce(f32[64]{0:T(128)} %copy-done.10, f32[64]{0:T(128)S(1)} %negate_multiply_fusion, f32[64]{0:T(128)S(1)} %get-tuple-element.341, f32[64]{0:T(128)} %reduce_sum.119), channel_id=1, replica_groups=mesh['dp'=4,'ctx'=8] {'dp'}, use_global_device_ids=true, to_apply=%add.3 | all-reduce | flops 256 | bytes 2048
  179.1 1.8 convolution_bitcast_fusion.1
  181.7 1.7 fusion.44
  183.4 5.2 %fusion.37 = bf16[128,64,32]{0,2,1:T(8,128)(2,1)} fusion(bf16[64,32,128]{2,1,0:T(8,128)(2,1)S(1)} %bitcast.154, f32[64,128]{1,0:T(8,128)} %get-tuple-element.349, f32[64,128]{1,0:T(8,128)S(1)} %reduce_window_sum.22, f32[128,128]{1,0:T(8,128)} %fusion.65, pred[128,128]{1,0:T(8,128)(4,1)S(1)} %iota_compare_fusion, bf16[128,64,32]{0,2,1:T(8,128)(2,1)S(1)} %bitcast.155, ...), kind=kOutput, calls=%fused_computation.42 | convolution fusion | flops 408420352 | bytes 2801920 | tf_op jit(solution)/shard_map/transpose(jvp(hts,shp->thp))/dot_general | solution.py:39
  188.6 2.0 copy.49
  190.6 4.6 %fusion.40 = bf16[128,64,32]{0,2,1:T(8,128)(2,1)S(1)} fusion(bf16[128,64,32]{0,2,1:T(8,128)(2,1)S(1)} %bitcast.150, f32[64,128]{1,0:T(8,128)S(1)} %copy-done.6, f32[64,128]{1,0:T(8,128)S(1)} %reduce_window_sum.22, f32[128,128]{1,0:T(8,128)S(1)} %copy-done.5, pred[128,128]{1,0:T(8,128)(4,1)S(1)} %iota_compare_fusion, f32[64,32,128]{2,1,0:T(8,128)S(1)} %copy-done.2, ...), kind=kOutput, calls=%fused_computation.43 | convolution fusion | flops 408420352 | bytes 2277632 | tf_op jit(solution)/shard_map/jvp(hts,shp->thp)/dot_general | solution.py:39
  196.2 12.3 %all-reduce.8 = (f32[16]{0:T(128)}, f32[16]{0:T(128)}, f32[16]{0:T(128)}) all-reduce(f32[16]{0:T(128)S(1)} %dynamic-slice.13, f32[16]{0:T(128)S(1)} %dynamic-slice.15, f32[16]{0:T(128)S(1)} %dynamic-slice.17), channel_id=1, replica_groups=mesh['dp'=4,'ctx'=8] {'ctx'}, use_global_device_ids=true, to_apply=%region_14.15 | all-reduce | flops 48 | bytes 384 | tf_op jit(solution)/shard_map/psum | solution.py:116
  (92 shorter events, 24.5 us)
Async XLA Ops:
  7.2 24.7 %copy-start = (bf16[1,128,128]{2,1,0:T(8,128)(2,1)S(1)}, bf16[1,128,128]{2,1,0:T(8,128)(2,1)}, u32[]{:S(2)}) copy-start(bf16[1,128,128]{2,1,0:T(8,128)(2,1)} %param.15) | copy-start | bytes 98308
  7.2 23.0 %copy-start.3 = (bf16[1,128,128]{2,1,0:T(8,128)(2,1)S(1)}, bf16[1,128,128]{2,1,0:T(8,128)(2,1)}, u32[]{:S(2)}) copy-start(bf16[1,128,128]{2,1,0:T(8,128)(2,1)} %param.16) | copy-start | bytes 98308
  7.2 77.3 %all-gather.8.cloned.1.call-start = ((), (), s32[]{:S(2)}) async-start(), calls=%async_computation.1 | async-start | bytes 9437184 | tf_op jit(solution)/shard_map/all_gather | solution.py:11
  24.4 7.4 %copy-start.12 = (f32[64]{0:T(128)}, f32[64]{0:T(128)S(1)}, u32[]{:S(2)}) copy-start(f32[64]{0:T(128)S(1)} %get-tuple-element.340) | copy-start | bytes 772
  24.4 130.8 %copy-start.7 = (f32[64]{0:T(128)}, f32[64]{0:T(128)S(1)}, u32[]{:S(2)}) copy-start(f32[64]{0:T(128)S(1)} %get-tuple-element.339) | copy-start | bytes 772
  24.4 0.5 copy-start.9
  26.2 128.9 %copy-start.8 = (f32[64]{0:T(128)}, f32[64]{0:T(128)S(1)}, u32[]{:S(2)}) copy-start(f32[64]{0:T(128)S(1)} %slice_reduce_fusion) | copy-start | bytes 772
  29.8 3.8 %copy-start.13 = (u32[32]{0:T(128)S(1)}, u32[32]{0:T(128)}, u32[]{:S(2)}) copy-start(u32[32]{0:T(128)} %constant.141) | copy-start | bytes 388
  29.8 18.7 %copy-start.11 = (f32[16]{0:T(128)S(1)}, f32[16]{0:T(128)}, u32[]{:S(2)}) copy-start(f32[16]{0:T(128)} %param.20) | copy-start | bytes 196
  31.8 108.8 %all-gather.6.cloned.1.call-start = ((), (), s32[]{:S(2)}) async-start(), calls=%async_computation | async-start | bytes 9437184 | tf_op jit(solution)/shard_map/all_gather | solution.py:11
  48.6 35.9 %copy-start.10 = (f32[64]{0:T(128)}, f32[64]{0:T(128)S(1)}, u32[]{:S(2)}) copy-start(f32[64]{0:T(128)S(1)} %dynamic-update-slice.5) | copy-start | bytes 772
  152.9 2.3 %copy-start.4 = (f32[1,64,128]{2,1,0:T(8,128)S(1)}, f32[1,64,128]{2,1,0:T(8,128)}, u32[]{:S(2)}) copy-start(f32[1,64,128]{2,1,0:T(8,128)} %param.17) | copy-start | bytes 98308
  156.4 27.1 %copy-start.1 = (f32[128,64,32]{0,2,1:T(8,128)S(1)}, f32[128,64,32]{0,2,1:T(8,128)}, u32[]{:S(2)}) copy-start(f32[128,64,32]{0,2,1:T(8,128)} %get-tuple-element.356) | copy-start | bytes 3145732
  183.4 7.2 %copy-start.2 = (f32[64,32,128]{2,1,0:T(8,128)S(1)}, f32[64,32,128]{2,1,0:T(8,128)}, u32[]{:S(2)}) copy-start(f32[64,32,128]{2,1,0:T(8,128)} %get-tuple-element.358) | copy-start | bytes 3145732
  183.4 7.2 %copy-start.5 = (f32[128,128]{1,0:T(8,128)S(1)}, f32[128,128]{1,0:T(8,128)}, u32[]{:S(2)}) copy-start(f32[128,128]{1,0:T(8,128)} %fusion.65) | copy-start | bytes 196612
  183.4 7.2 %copy-start.6 = (f32[64,128]{1,0:T(8,128)S(1)}, f32[64,128]{1,0:T(8,128)}, u32[]{:S(2)}) copy-start(f32[64,128]{1,0:T(8,128)} %get-tuple-element.349) | copy-start | bytes 98308
Sparse Core Ops, SparseCore 0:
  31.9 52.5 all-gather.7
  86.4 54.2 all-gather.5
where the time goes:
time: 217 us; the launch traced here: 215 us
  waiting for transfers between devices  73.9 us (34%)
  blocking collectives  50.1 us (23%)
  other arithmetic  33.5 us (15%)
  matrix products  29.4 us (14%)
  between operations  16.3 us (8%)
  local copies, waits for them, and re-layouts  11.5 us (5%)
    all_gather x2, waiting for transfers between devices, carried_in(): everything = jax.tree.map(lambda part: lax.all_gather(part, axis), array)  73.8 us
    unnamed x3, blocking collectives  37.8 us
    select_n x16, other arithmetic, hop(): return jax.tree.map(lambda a, b: jnp.where(reached, a, b), new, before)  24.1 us
    dot_general x3, matrix products, local_part(): inner = jnp.einsum('hts,shp->thp', weights, xg3, precision=maximal_accuracy)  15.3 us
    psum x1, blocking collectives, local(): totals = lax.psum((rate_grad, bias_grad, skip_grad), 'ctx')  12.3 us
    unnamed x45, local copies, waits for them, and re-layouts  10.5 us
    dot_general x3, matrix products, local_part(): jnp.einsum('shp,sn->hpn', scaled, write_operator, precision=maximal_accur...  5.77 us
  transfers between devices with their start and end apart: 2, of which 2 were waited for; matrix products, arithmetic and copies ran while one was open for 10% of the time, Pallas kernels for 0%

commit v1 on v0

v1 whole, which is shorter than its diff:
```python
import functools

import jax
import jax.numpy as jnp
from jax import lax
from jax.experimental import pallas as pl
from jax.experimental.pallas import tpu as pltpu
from jax.sharding import PartitionSpec as P

F32, BF16 = jnp.float32, jnp.bfloat16
EXACT = lax.Precision.HIGHEST
NT = (((1,), (1,)), ((), ()))
NN = (((1,), (0,)), ((), ()))
LANES = 128
PAD = 8


def mm(a, b, dims=NN):
    return lax.dot_general(a, b, dims, preferred_element_type=F32)


def exact_mm(a, b, dims=NN):
    return lax.dot_general(a, b, dims, precision=EXACT, preferred_element_type=F32)


def split(v):
    hi = v.astype(BF16)
    return hi, (v - hi.astype(F32)).astype(BF16)


def spread(heads, width, first, lanes, rows=None):
    head = lax.broadcasted_iota(jnp.int32, (heads, lanes), 0)
    lane = lax.broadcasted_iota(jnp.int32, (heads, lanes), 1) + first
    inside = jnp.logical_and(lane >= head * width, lane < head * width + width)
    return jnp.where(inside, 1.0, 0.0).astype(BF16)


def expand(per_head, hot):
    hi, lo = split(per_head)
    return mm(jnp.concatenate([hi, lo], axis=1), jnp.concatenate([hot, hot], axis=0))


def scans(raw, par):
    rate, bias = par[:, 0:1], par[:, 1:2]
    z = raw + bias
    step = jnp.maximum(z, 0.0) + jnp.log1p(jnp.exp(-jnp.abs(z)))
    scale = -jnp.exp(rate)
    logdecay = scale * step
    count = raw.shape[1]
    early = lax.broadcasted_iota(jnp.int32, (count, count), 0)
    late = lax.broadcasted_iota(jnp.int32, (count, count), 1)
    upper = jnp.where(early <= late, 1.0, 0.0)
    cum = exact_mm(logdecay, upper)
    return z, step, scale, logdecay, cum, upper


def ends_kernel(c_ref, x_ref, g_ref, b_ref, r_ref, raw_ref, par_ref, own_ref, oth_ref, cum_ref, step_ref):
    heads, count = raw_ref.shape
    total = x_ref.shape[1]
    half = total // 2
    width = total // heads
    chunk = min(half, 512)
    _, step, _, _, cum, _ = scans(raw_ref[...], par_ref[...])
    cum_ref[...] = cum
    step_ref[...] = step
    tail = (jnp.exp(cum[:, -1:] - cum) * step).T
    grow = jnp.exp(cum).T
    bt = b_ref[...].astype(F32).T.astype(BF16)
    ct = r_ref[...].astype(F32).T.astype(BF16)
    bt2 = jnp.concatenate([bt, bt], axis=1)
    ct2 = jnp.concatenate([ct, ct], axis=1)
    c = c_ref[0]
    size = b_ref.shape[1]
    for which, out in ((c, own_ref), (1 - c, oth_ref)):
        for k in range(half // chunk):
            first = pl.multiple_of(which * half + k * chunk, chunk)
            hot = spread(heads, width, first, chunk)
            here = pl.ds(first, chunk)
            there = pl.ds(k * chunk, chunk)
            grow_x = expand(grow, hot)
            xt = expand(tail, hot) * x_ref[:, here].astype(F32)
            out[0, :size, there] = mm(bt2, jnp.concatenate(split(xt), axis=0))
            gt = grow_x * g_ref[:, here].astype(F32)
            out[1, :size, there] = mm(ct2, jnp.concatenate(split(gt), axis=0))
            last = jnp.broadcast_to(grow_x[count - 1 :, :], (PAD, chunk))
            out[0, size:, there] = last
            out[1, size:, there] = last


def inside_kernel(x_ref, g_ref, b_ref, r_ref, cum_ref, step_ref, inner_ref, dxin_ref, db_ref, dc_ref, cumt_ref, dgram_ref):
    heads, count = cum_ref.shape
    total = x_ref.shape[1]
    width = total // heads
    pack = LANES // width
    t_row = lax.broadcasted_iota(jnp.int32, (count, count), 0)
    t_col = lax.broadcasted_iota(jnp.int32, (count, count), 1)
    b, r = b_ref[...], r_ref[...]
    gram = jnp.where(t_row >= t_col, mm(r, b, NT), 0.0)
    gram_t = jnp.where(t_row <= t_col, mm(b, r, NT), 0.0)
    cum_all = cum_ref[...]
    cumt_ref[...] = jnp.concatenate([cum_all, jnp.zeros((LANES - heads, count), F32)], axis=0).T
    step_t = step_ref[...].T
    dgram_ref[...] = jnp.zeros_like(dgram_ref)
    lane = lax.broadcasted_iota(jnp.int32, (count, LANES), 1)

    def group(j, _):
        at = pl.multiple_of(j * LANES, LANES)
        x4 = x_ref[:, pl.ds(at, LANES)]
        g4 = g_ref[:, pl.ds(at, LANES)]
        cols = pltpu.roll(cumt_ref[...], LANES - j * pack, 1)
        his, los, thi, tlo, xs, gs = [], [], [], [], [], []
        dgram = dgram_ref[...]
        for i in range(pack):
            head = j * pack + i
            row = cum_ref[pl.ds(head, 1), :]
            step_row = step_ref[pl.ds(head, 1), :]
            diff = cols[:, i : i + 1] - row
            seg = jnp.exp(jnp.minimum(diff, 0.0)) * step_row
            seg_t = jnp.exp(jnp.minimum(-diff, 0.0))
            mine = jnp.logical_and(lane >= i * width, lane < (i + 1) * width)
            xm = jnp.where(mine, x4.astype(F32), 0.0).astype(BF16)
            gm = jnp.where(mine, g4.astype(F32), 0.0).astype(BF16)
            dgram = dgram + mm(gm, x4, NT) * seg
            hi, lo = split(gram * seg)
            his.append(hi)
            los.append(lo)
            hi, lo = split(gram_t * seg_t)
            thi.append(hi)
            tlo.append(lo)
            xs.append(xm)
            gs.append(gm)
        dgram_ref[...] = dgram
        inner_ref[:, pl.ds(at, LANES)] = mm(jnp.concatenate(his + los, axis=1), jnp.concatenate(xs + xs, axis=0))
        hot = spread(heads, width, at, LANES)
        back = mm(jnp.concatenate(thi + tlo, axis=1), jnp.concatenate(gs + gs, axis=0))
        dxin_ref[:, pl.ds(at, LANES)] = back * expand(step_t, hot)
        return 0

    lax.fori_loop(0, heads // pack, group, 0)
    dgram = jnp.where(t_row >= t_col, dgram_ref[...], 0.0)
    hi, lo = split(dgram)
    dc_ref[...] = mm(jnp.concatenate([hi, lo], axis=1), jnp.concatenate([b, b], axis=0))
    hi, lo = split(dgram.T)
    db_ref[...] = mm(jnp.concatenate([hi, lo], axis=1), jnp.concatenate([r, r], axis=0))


def after_kernel(
    c_ref, x_ref, g_ref, b_ref, r_ref, raw_ref, par_ref, inner_ref, dxin_ref, db0_ref, dc0_ref,
    own_ref, oth_ref, y_ref, dx_ref, db_ref, dc_ref, draw_ref, tot_ref,
):
    heads, count = raw_ref.shape
    total = x_ref.shape[1]
    half = total // 2
    width = total // heads
    chunk = min(half, 512)
    z, step, scale, logdecay, cum, upper = scans(raw_ref[...], par_ref[...])
    tail = (jnp.exp(cum[:, -1:] - cum) * step).T
    grow = jnp.exp(cum).T
    skip = jnp.broadcast_to(par_ref[:, 2:3], (heads, LANES)).T[:PAD]
    b, r = b_ref[...], r_ref[...]
    b2 = jnp.concatenate([b, b], axis=1)
    r2 = jnp.concatenate([r, r], axis=1)
    c = c_ref[0]
    db, dc = db0_ref[...], dc0_ref[...]
    uv = jnp.zeros((2 * count, heads), F32)
    sums = jnp.zeros((3 * PAD, heads), F32)
    for which, src in ((c, own_ref), (1 - c, oth_ref)):
        for k in range(half // chunk):
            first = pl.multiple_of(which * half + k * chunk, chunk)
            hot = spread(heads, width, first, chunk)
            here = pl.ds(first, chunk)
            there = pl.ds(k * chunk, chunk)
            x = x_ref[:, here].astype(F32)
            g = g_ref[:, here].astype(F32)
            grow_x, tail_x, skip_x = expand(grow, hot), expand(tail, hot), expand(skip, hot)[0:1]
            before, later = src[0, :, there], src[1, :, there]
            h_hi, h_lo = split(before)
            d_hi, d_lo = split(later)
            flow = inner_ref[:, here] + grow_x * mm(r2, jnp.concatenate([h_hi, h_lo], axis=0))
            y_ref[:, here] = (flow + skip_x * x).astype(BF16)
            reach = tail_x * mm(b2, jnp.concatenate([d_hi, d_lo], axis=0))
            back = dxin_ref[:, here] + reach
            dx_ref[:, here] = (back + skip_x * g).astype(BF16)
            uv_hi, uv_lo = split(jnp.concatenate([g * flow, x * back], axis=0))
            uv = uv + mm(uv_hi, hot, NT) + mm(uv_lo, hot, NT)
            parts = jnp.concatenate(
                [
                    jnp.sum((v).reshape(-1, PAD, chunk), axis=0)
                    for v in (x * reach, before * later, g * x)
                ],
                axis=0,
            )
            s_hi, s_lo = split(parts)
            sums = sums + mm(s_hi, hot, NT) + mm(s_lo, hot, NT)
            e_hi, e_lo = split(grow_x * g)
            dc = dc + mm(e_hi, h_hi, NT) + mm(e_hi, h_lo, NT) + mm(e_lo, h_hi, NT)
            t_hi, t_lo = split(tail_x * x)
            db = db + mm(t_hi, d_hi, NT) + mm(t_hi, d_lo, NT) + mm(t_lo, d_hi, NT)
    db_ref[...] = db
    dc_ref[...] = dc
    u = uv[:count].T
    v = uv[count:].T
    sums_t = sums.T
    reach_sum = jnp.sum(sums_t[:, :PAD], axis=1, keepdims=True)
    meet_sum = jnp.sum(sums_t[:, PAD : 2 * PAD], axis=1, keepdims=True)
    skip_sum = jnp.sum(sums_t[:, 2 * PAD :], axis=1, keepdims=True)
    end = reach_sum + jnp.exp(cum[:, -1:]) * meet_sum
    dlog = exact_mm(u - v, upper, NT) + end
    draw = (scale * dlog + v / step) * jax.nn.sigmoid(z)
    draw_ref[...] = draw
    column = lax.broadcasted_iota(jnp.int32, (heads, LANES), 1)
    rate_sum = jnp.sum(dlog * logdecay, axis=1, keepdims=True)
    bias_sum = jnp.sum(draw, axis=1, keepdims=True)
    tot_ref[...] = jnp.where(column == 0, rate_sum, jnp.where(column == 1, bias_sum, jnp.where(column == 2, skip_sum, 0.0)))


def call(kernel, outs, args, scratch=(), flops=0, scalar=False):
    vmem = pl.BlockSpec(memory_space=pltpu.VMEM)
    specs = [vmem] * len(args)
    if scalar:
        specs[0] = pl.BlockSpec(memory_space=pltpu.SMEM)
    size = sum(a.size * a.dtype.itemsize for a in (*args, *outs))
    return pl.pallas_call(
        kernel,
        out_shape=outs,
        in_specs=specs,
        out_specs=tuple([vmem] * len(outs)),
        scratch_shapes=list(scratch),
        cost_estimate=pl.CostEstimate(flops=flops, bytes_accessed=size, transcendentals=0),
        compiler_params=pltpu.CompilerParams(vmem_limit_bytes=48 << 20),
    )(*args)


def swap(value, axis, bit):
    return lax.ppermute(value, axis, [(i, i ^ bit) for i in range(lax.axis_size(axis))])


def gathered(value, axis):
    place, bit = lax.axis_index(axis), 1
    while bit < lax.axis_size(axis):
        other = swap(value, axis, bit)
        low = (place & bit) == 0
        value = jnp.concatenate([jnp.where(low, value, other), jnp.where(low, other, value)], axis=0)
        bit *= 2
    return value


def owned_sum(value, axis):
    place, bit = lax.axis_index(axis), lax.axis_size(axis) // 2
    while bit:
        lower, upper = jnp.split(value, 2, axis=0)
        low = (place & bit) == 0
        value = jnp.where(low, lower, upper) + swap(jnp.where(low, upper, lower), axis, bit)
        bit //= 2
    return value


def total_sum(value, axis):
    bit = 1
    while bit < lax.axis_size(axis):
        value = value + swap(value, axis, bit)
        bit *= 2
    return value


def chip_carries(total, size):
    n = lax.axis_size("ctx")
    place = lax.axis_index("ctx")
    zero = jnp.zeros_like(total[0, :size])

    def act(first, second, forward):
        if forward:
            return second[:size] + second[size : size + 1] * first[:size]
        return first[:size] + first[size : size + 1] * second[:size]

    if n == 8:
        x1, y1 = (place & 2) != 0, (place & 4) != 0
        from_y = swap(jnp.where(y1, total[1], total[0]), "ctx", 4)
        from_x = swap(jnp.where(x1, total[1], total[0]), "ctx", 2)
        far = swap(from_y, "ctx", 2)
        first, second = jnp.where(x1, far, from_y), jnp.where(x1, from_y, far)
        row = jnp.where(y1, act(first, second, True), act(first, second, False))
        ahead, behind = jnp.where(y1, row, zero), jnp.where(y1, zero, row)
        step = from_x[:size] + from_x[size : size + 1] * jnp.where(x1, ahead, behind)
        return jnp.where(x1, step, ahead), jnp.where(x1, behind, step)
    ahead, behind = zero, zero
    ahead_decay = behind_decay = jnp.ones_like(total[0, size : size + 1])
    fwd, bwd = total[0], total[1]
    bit = 2
    while bit < n:
        o_fwd, o_bwd = swap(fwd, "ctx", bit), swap(bwd, "ctx", bit)
        up = (place & bit) != 0
        ahead = jnp.where(up, ahead + ahead_decay * o_fwd[:size], ahead)
        ahead_decay = jnp.where(up, ahead_decay * o_fwd[size : size + 1], ahead_decay)
        behind = jnp.where(up, behind, behind + behind_decay * o_bwd[:size])
        behind_decay = jnp.where(up, behind_decay, behind_decay * o_bwd[size : size + 1])
        decay = fwd[size:] * o_fwd[size:]
        f1, f2 = jnp.where(up, o_fwd, fwd), jnp.where(up, fwd, o_fwd)
        b1, b2 = jnp.where(up, o_bwd, bwd), jnp.where(up, bwd, o_bwd)
        fwd = jnp.concatenate([act(f1, f2, True), decay], axis=0)
        bwd = jnp.concatenate([act(b1, b2, False), decay], axis=0)
        bit *= 2
    return ahead, behind


def local(x, b, r, raw, rate, bias, skip, g):
    x, b, r, raw, g = x[0], b[0], r[0], raw[0], g[0]
    heads, count = raw.shape
    total, size = x.shape[1], b.shape[1]
    half = total // 2
    par = gathered(jnp.stack([rate, bias, skip], axis=1), "dp")
    core = lax.axis_index("ctx") & 1
    odd = core == 1
    c = core.astype(jnp.int32).reshape(1)
    shape = jax.ShapeDtypeStruct
    message = shape((2, size + PAD, half), F32)
    small = shape((heads, count), F32)
    wide = shape((count, total), F32)
    square = shape((count, size), F32)
    own, oth, cum, step = call(
        ends_kernel, (message, message, small, small), (c, x, g, b, r, raw, par), flops=10**9, scalar=True
    )
    mate = swap(oth, "ctx", 1)
    s_o, g_o, a_o = own[0, :size], own[1, :size], own[0, size:]
    s_p, g_p, a_p = mate[0, :size], mate[1, :size], mate[0, size:]
    fwd = jnp.where(odd, a_o[0:1] * s_p + s_o, a_p[0:1] * s_o + s_p)
    bwd = jnp.where(odd, g_p + a_p[0:1] * g_o, g_o + a_o[0:1] * g_p)
    decay = a_o * a_p
    chip = jnp.stack([jnp.concatenate([fwd, decay], axis=0), jnp.concatenate([bwd, decay], axis=0)])
    ahead, behind = chip_carries(chip, size)
    inner, dxin, db0, dc0 = call(
        inside_kernel,
        (wide, wide, square, square),
        (x, g, b, r, cum, step),
        scratch=[pltpu.VMEM((count, LANES), F32), pltpu.VMEM((count, count), F32)],
        flops=10**9,
    )
    through = jnp.where(odd, a_p[0:1], a_o[0:1]) * ahead + jnp.where(odd, s_p, s_o)
    mine = jnp.where(odd, through, ahead), jnp.where(odd, behind, g_p + a_p[0:1] * behind)
    theirs = jnp.where(odd, ahead, through), jnp.where(odd, g_o + a_o[0:1] * behind, behind)
    mine, theirs = jnp.stack(mine), jnp.stack(theirs)
    rest = swap(theirs, "ctx", 1)
    outs = (shape((count, total), BF16), shape((count, total), BF16), square, square, small, shape((heads, LANES), F32))
    y, dx, db, dc, draw, tot = call(
        after_kernel, outs, (c, x, g, b, r, raw, par, inner, dxin, db0, dc0, mine, rest), flops=10**9, scalar=True
    )
    sums = owned_sum(total_sum(tot[:, :3], "ctx"), "dp")
    return (y[None], dx[None], db[None], dc[None], draw[None], sums[:, 0], sums[:, 1], sums[:, 2])


def solution(mesh):
    wide = P("dp", "ctx", None)
    strides = P("dp", None, "ctx")
    return jax.shard_map(
        local,
        mesh=mesh,
        in_specs=(wide, wide, wide, strides, P("dp"), P("dp"), P("dp"), wide),
        out_specs=(wide, wide, wide, wide, strides, P("dp"), P("dp"), P("dp")),
        check_vma=False,
    )
```

time: 217 us -> 83.9 us (0.39)
  blocking collectives: 50.1 us -> 0 us
  waiting for transfers between devices: 73.9 us -> 39.4 us
  other arithmetic: 33.5 us -> 2.11 us
  matrix products: 29.4 us -> 0 us
  starting transfers between devices: 0.08 us -> 19.2 us
  between operations: 16.3 us -> 0.83 us
  Pallas kernels: 0 us -> 15.1 us
  local copies, waits for them, and re-layouts: 11.5 us -> 6.82 us
    all_gather x2 -> x0, waiting for transfers between devices: 73.8 us -> none  [carried_in(): everything = jax.tree.map(lambda part: lax.all_gather(part, axis), array)]
    ppermute x0 -> x12, waiting for transfers between devices: none -> 39.4 us  [swap(): lax.ppermute(value, axis, [(i, i ^ bit) for i in range(lax.axis_size(axis...]
    unnamed x3 -> x0, blocking collectives: 37.8 us -> none
    dot_general x12 -> x0, matrix products: 29.4 us -> none  [the longest x3 15.3 us: local_part(): inner = jnp.einsum('hts,shp->thp', weights, xg3, precision=maximal_accuracy)]
    select_n x16 -> x8, other arithmetic: 24.1 us -> 0.5 us  [the longest x1 0.3 us: local(): fwd = jnp.where(odd, a_o[0:1] * s_p + s_o, a_p[0:1] * s_o + s_p)]
    ppermute x0 -> x12, starting transfers between devices: none -> 19.2 us  [swap(): lax.ppermute(value, axis, [(i, i ^ bit) for i in range(lax.axis_size(axis...]
    pallas_call x0 -> x3, Pallas kernels: none -> 15.1 us  [call(): pl.pallas_call(kernel, out_shape=outs, in_specs=specs, out_specs=tuple([v...]
    psum x1 -> x0, blocking collectives: 12.3 us -> none  [local(): totals = lax.psum((rate_grad, bias_grad, skip_grad), 'ctx')]
  transfers between devices with their start and end apart: 2 -> 12, of which waited for: 2 -> 10; matrix products, arithmetic and copies ran while one was open for 10% -> 0% of each run, Pallas kernels for 0% -> 10%
where the time goes in v1:
time: 83.9 us; the launch traced here: 83.4 us
  waiting for transfers between devices  39.4 us (47%)
  starting transfers between devices  19.2 us (23%)
  Pallas kernels  15.1 us (18%)
  local copies, waits for them, and re-layouts  6.82 us (8%)
  other arithmetic  2.11 us (3%)
    ppermute x12, waiting for transfers between devices, swap(): lax.ppermute(value, axis, [(i, i ^ bit) for i in range(lax.axis_size(axis...  39.4 us
    ppermute x12, starting transfers between devices, swap(): lax.ppermute(value, axis, [(i, i ^ bit) for i in range(lax.axis_size(axis...  19.2 us
    pallas_call x3, Pallas kernels, call(): pl.pallas_call(kernel, out_shape=outs, in_specs=specs, out_specs=tuple([v...  15.1 us
    unnamed x20, local copies, waits for them, and re-layouts  5.98 us
  transfers between devices with their start and end apart: 12, of which 10 were waited for; matrix products, arithmetic and copies ran while one was open for 0% of the time, Pallas kernels for 10%

profile of v1, /device:TPU:0, one launch (start us, length us, event | category | flops | bytes accessed | tf_op | source)
XLA Modules:
  0.0 83.4 jit_solution(3123012858380917091)
XLA Ops:
  0.6 0.7 pad_maximum_fusion.6
  1.4 3.1 %collective-permute-start = (f32[16,3]{1,0:T(8,128)S(1)}, f32[16,3]{1,0:T(8,128)S(1)}, u32[]{:S(2)}, u32[]{:S(2)}) collective-permute-start(f32[16,3]{1,0:T(8,128)S(1)} %copy.35), channel_id=1, source_target_pairs={{0,8},{8,0},{16,24},{24,16},{1,9},{9,1},{17,25},{25,17},{2,10},{10... | collective-permute-start | bytes 584 | tf_op jit(solution)/shard_map/ppermute | solution.py:235
  4.5 1.6 %collective-permute-done = f32[16,3]{1,0:T(8,128)S(1)} collective-permute-done((f32[16,3]{1,0:T(8,128)S(1)}, f32[16,3]{1,0:T(8,128)S(1)}, u32[]{:S(2)}, u32[]{:S(2)}) %collective-permute-start) | collective-permute-done | bytes 224 | tf_op jit(solution)/shard_map/ppermute | solution.py:235
  6.1 3.1 %collective-permute-start.1 = (f32[32,3]{1,0:T(8,128)S(1)}, f32[32,3]{1,0:T(8,128)S(1)}, u32[]{:S(2)}, u32[]{:S(2)}) collective-permute-start(f32[32,3]{1,0:T(8,128)S(1)} %pad_maximum_fusion.5), channel_id=1, source_target_pairs={{0,16},{8,24},{16,0},{24,8},{1,17},{9,25},{17,1},{25,9},{2,18},{10... | collective-permute-start | bytes 1160 | tf_op jit(solution)/shard_map/ppermute | solution.py:235
  9.2 1.7 %collective-permute-done.1 = f32[32,3]{1,0:T(8,128)S(1)} collective-permute-done((f32[32,3]{1,0:T(8,128)S(1)}, f32[32,3]{1,0:T(8,128)S(1)}, u32[]{:S(2)}, u32[]{:S(2)}) %collective-permute-start.1) | collective-permute-done | bytes 416 | tf_op jit(solution)/shard_map/ppermute | solution.py:235
  11.0 1.0 %copy-done = bf16[1,128,2048]{2,1,0:T(8,128)(2,1)S(1)} copy-done((bf16[1,128,2048]{2,1,0:T(8,128)(2,1)S(1)}, bf16[1,128,2048]{2,1,0:T(8,128)(2,1)}, u32[]{:S(2)}) %copy-start) | copy-done | bytes 524312
  12.0 1.0 %copy-done.2 = bf16[1,128,2048]{2,1,0:T(8,128)(2,1)S(1)} copy-done((bf16[1,128,2048]{2,1,0:T(8,128)(2,1)S(1)}, bf16[1,128,2048]{2,1,0:T(8,128)(2,1)}, u32[]{:S(2)}) %copy-start.2) | copy-done | bytes 524312
  13.0 0.8 copy-done.4
  13.8 0.8 copy-done.6
  14.6 0.8 copy-done.8
  15.3 1.9 %shard_map.143 = (f32[2,136,1024]{2,1,0:T(8,128)S(1)}, f32[2,136,1024]{2,1,0:T(8,128)S(1)}, f32[64,128]{1,0:T(8,128)S(1)}, f32[64,128]{1,0:T(8,128)S(1)}) custom-call(s32[1]{0:T(128)} %bitcast.c_ref, bf16[128,2048]{1,0:T(8,128)(2,1)S(1)} %bitcast.76, bf16[128,2048]{1,0:T(8,128)(2,1)S(1)} %bitcast.79, bf16[128,128]{1,0:T(8,128)(2,1)S(1)} %bitcast.82, ...), custom_call_target="tpu_custom_call" | custom-call | flops 1000000000 | bytes 3441412 | tf_op jit(solution)/shard_map/pallas_call | solution.py:223
  17.3 2.7 %collective-permute-done.2 = f32[2,136,1024]{2,1,0:T(8,128)S(1)} collective-permute-done((f32[2,136,1024]{2,1,0:T(8,128)S(1)}, f32[2,136,1024]{2,1,0:T(8,128)S(1)}, u32[]{:S(2)}, u32[]{:S(2)}) %collective-permute-start.2) | collective-permute-done | bytes 1114144 | tf_op jit(solution)/shard_map/ppermute | solution.py:235
  20.4 1.9 %collective-permute-start.4 = (f32[136,1024]{1,0:T(8,128)S(1)}, f32[136,1024]{1,0:T(8,128)S(1)}, u32[]{:S(2)}, u32[]{:S(2)}) collective-permute-start(f32[136,1024]{1,0:T(8,128)S(1)} %get-tuple-element.51), channel_id=1, source_target_pairs={{0,4},{1,5},{2,6},{3,7},{4,0},{5,1},{6,2},{7,3},{8,12},{9,13},{10,... | collective-permute-start | bytes 1671176 | tf_op jit(solution)/shard_map/ppermute | solution.py:235
  22.3 1.5 %collective-permute-start.3 = (f32[136,1024]{1,0:T(8,128)S(1)}, f32[136,1024]{1,0:T(8,128)S(1)}, u32[]{:S(2)}, u32[]{:S(2)}) collective-permute-start(f32[136,1024]{1,0:T(8,128)S(1)} %get-tuple-element.52), channel_id=1, source_target_pairs={{0,2},{1,3},{2,0},{3,1},{4,6},{5,7},{6,4},{7,5},{8,10},{9,11},{10,... | collective-permute-start | bytes 1671176 | tf_op jit(solution)/shard_map/ppermute | solution.py:235
  23.8 11.4 %collective-permute-done.4 = f32[136,1024]{1,0:T(8,128)S(1)} collective-permute-done((f32[136,1024]{1,0:T(8,128)S(1)}, f32[136,1024]{1,0:T(8,128)S(1)}, u32[]{:S(2)}, u32[]{:S(2)}) %collective-permute-start.4) | collective-permute-done | bytes 557088 | tf_op jit(solution)/shard_map/ppermute | solution.py:235
  35.2 1.7 %collective-permute-start.5 = (f32[136,1024]{1,0:T(8,128)S(1)}, f32[136,1024]{1,0:T(8,128)S(1)}, u32[]{:S(2)}, u32[]{:S(2)}) collective-permute-start(f32[136,1024]{1,0:T(8,128)S(1)} %collective-permute-done.4), channel_id=1, source_target_pairs={{0,2},{1,3},{2,0},{3,1},{4,6},{5,7},{6,4},{7,5},{8,10},{9,11},{10,... | collective-permute-start | bytes 1671176 | tf_op jit(solution)/shard_map/ppermute | solution.py:235
  37.0 12.2 %collective-permute-done.5 = f32[136,1024]{1,0:T(8,128)S(1)} collective-permute-done((f32[136,1024]{1,0:T(8,128)S(1)}, f32[136,1024]{1,0:T(8,128)S(1)}, u32[]{:S(2)}, u32[]{:S(2)}) %collective-permute-start.5) | collective-permute-done | bytes 557088 | tf_op jit(solution)/shard_map/ppermute | solution.py:235
  49.3 0.4 select_bitcast_fusion
  49.9 0.8 copy-done.1
  50.9 8.7 %shard_map.144 = (f32[128,2048]{1,0:T(8,128)S(1)}, f32[128,2048]{1,0:T(8,128)S(1)}, f32[128,128]{1,0:T(8,128)S(1)}, f32[128,128]{1,0:T(8,128)S(1)}) custom-call(bf16[128,2048]{1,0:T(8,128)(2,1)S(1)} %bitcast.77, bf16[128,2048]{1,0:T(8,128)(2,1)S(1)} %bitcast.80, bf16[128,128]{1,0:T(8,128)(2,1)S(1)} %bitcast.83, bf16[128,128]{1,0:T(8,128)(2,1)S(1)} %bitcast.86, ...), custom_call_target="tpu_custom_call" | custom-call | flops 1000000000 | bytes 3407872 | tf_op jit(solution)/shard_map/pallas_call | solution.py:223
  60.0 0.6 copy-done.9
  60.7 4.5 %shard_map.145 = (bf16[128,2048]{1,0:T(8,128)(2,1)}, bf16[128,2048]{1,0:T(8,128)(2,1)}, f32[128,128]{1,0:T(8,128)}, f32[128,128]{1,0:T(8,128)}, f32[64,128]{1,0:T(8,128)}, /*index=5*/f32[64,128]{1,0:T(8,128)S(1)}) custom-call(s32[1]{0:T(128)} %bitcast.c_ref, bf16[128,2048]{1,0:T(8,128)(2,1)S(1)} %bitcast.78, bf16[128,2048]{1,0:T(8,128)(2,1)S(1)} %bitcast.81, ...), custom_call_target="tpu_custom_call" | custom-call | flops 1000000000 | bytes 6718212 | tf_op jit(solution)/shard_map/pallas_call | solution.py:223
  65.2 1.2 %collective-permute-done.7 = f32[64,3]{1,0:T(8,128)S(1)} collective-permute-done((f32[64,3]{1,0:T(8,128)S(1)}, f32[64,3]{1,0:T(8,128)S(1)}, u32[]{:S(2)}, u32[]{:S(2)}) %collective-permute-start.7) | collective-permute-done | bytes 800 | tf_op jit(solution)/shard_map/ppermute | solution.py:235
  66.4 1.6 %collective-permute-start.8 = (f32[64,3]{1,0:T(8,128)S(1)}, f32[64,3]{1,0:T(8,128)S(1)}, u32[]{:S(2)}, u32[]{:S(2)}) collective-permute-start(f32[64,3]{1,0:T(8,128)S(1)} %slice_add_fusion.1), channel_id=1, source_target_pairs={{0,2},{1,3},{2,0},{3,1},{4,6},{5,7},{6,4},{7,5},{8,10},{9,11},{10,... | collective-permute-start | bytes 2312 | tf_op jit(solution)/shard_map/ppermute | solution.py:235
  68.0 2.3 %collective-permute-done.8 = f32[64,3]{1,0:T(8,128)S(1)} collective-permute-done((f32[64,3]{1,0:T(8,128)S(1)}, f32[64,3]{1,0:T(8,128)S(1)}, u32[]{:S(2)}, u32[]{:S(2)}) %collective-permute-start.8) | collective-permute-done | bytes 800 | tf_op jit(solution)/shard_map/ppermute | solution.py:235
  70.3 1.6 %collective-permute-start.9 = (f32[64,3]{1,0:T(8,128)S(1)}, f32[64,3]{1,0:T(8,128)S(1)}, u32[]{:S(2)}, u32[]{:S(2)}) collective-permute-start(f32[64,3]{1,0:T(8,128)S(1)} %add.56), channel_id=1, source_target_pairs={{0,4},{1,5},{2,6},{3,7},{4,0},{5,1},{6,2},{7,3},{8,12},{9,13},{10,... | collective-permute-start | bytes 2312 | tf_op jit(solution)/shard_map/ppermute | solution.py:235
  71.9 2.3 %collective-permute-done.9 = f32[64,3]{1,0:T(8,128)S(1)} collective-permute-done((f32[64,3]{1,0:T(8,128)S(1)}, f32[64,3]{1,0:T(8,128)S(1)}, u32[]{:S(2)}, u32[]{:S(2)}) %collective-permute-start.9) | collective-permute-done | bytes 800 | tf_op jit(solution)/shard_map/ppermute | solution.py:235
  74.2 2.8 %collective-permute-start.10 = (f32[32,3]{1,0:T(8,128)S(1)}, f32[32,3]{1,0:T(8,128)S(1)}, u32[]{:S(2)}, u32[]{:S(2)}) collective-permute-start(f32[32,3]{1,0:T(8,128)S(1)} %slice_select_fusion), channel_id=1, source_target_pairs={{0,16},{8,24},{16,0},{24,8},{1,17},{9,25},{17,1},{25,9},{2,18},{10... | collective-permute-start | bytes 1160 | tf_op jit(solution)/shard_map/ppermute | solution.py:235
  77.0 1.9 %collective-permute-done.10 = f32[32,3]{1,0:T(8,128)S(1)} collective-permute-done((f32[32,3]{1,0:T(8,128)S(1)}, f32[32,3]{1,0:T(8,128)S(1)}, u32[]{:S(2)}, u32[]{:S(2)}) %collective-permute-start.10) | collective-permute-done | bytes 416 | tf_op jit(solution)/shard_map/ppermute | solution.py:235
  78.9 1.8 %collective-permute-start.11 = (f32[16,3]{1,0:T(8,128)S(1)}, f32[16,3]{1,0:T(8,128)S(1)}, u32[]{:S(2)}, u32[]{:S(2)}) collective-permute-start(f32[16,3]{1,0:T(8,128)S(1)} %slice_select_fusion.1), channel_id=1, source_target_pairs={{0,8},{8,0},{16,24},{24,16},{1,9},{9,1},{17,25},{25,17},{2,10},{10... | collective-permute-start | bytes 584 | tf_op jit(solution)/shard_map/ppermute | solution.py:235
  80.7 2.0 %collective-permute-done.11 = f32[16,3]{1,0:T(8,128)S(1)} collective-permute-done((f32[16,3]{1,0:T(8,128)S(1)}, f32[16,3]{1,0:T(8,128)S(1)}, u32[]{:S(2)}, u32[]{:S(2)}) %collective-permute-start.11) | collective-permute-done | bytes 224 | tf_op jit(solution)/shard_map/ppermute | solution.py:235
  82.7 0.7 slice_reduce_fusion
  (43 shorter events, 1.5 us)
Async XLA Ops:
  1.4 4.7 %collective-permute-start = (f32[16,3]{1,0:T(8,128)S(1)}, f32[16,3]{1,0:T(8,128)S(1)}, u32[]{:S(2)}, u32[]{:S(2)}) collective-permute-start(f32[16,3]{1,0:T(8,128)S(1)} %copy.35), channel_id=1, source_target_pairs={{0,8},{8,0},{16,24},{24,16},{1,9},{9,1},{17,25},{25,17},{2,10},{10... | collective-permute-start | bytes 584 | tf_op jit(solution)/shard_map/ppermute | solution.py:235
  6.1 4.8 %collective-permute-start.1 = (f32[32,3]{1,0:T(8,128)S(1)}, f32[32,3]{1,0:T(8,128)S(1)}, u32[]{:S(2)}, u32[]{:S(2)}) collective-permute-start(f32[32,3]{1,0:T(8,128)S(1)} %pad_maximum_fusion.5), channel_id=1, source_target_pairs={{0,16},{8,24},{16,0},{24,8},{1,17},{9,25},{17,1},{25,9},{2,18},{10... | collective-permute-start | bytes 1160 | tf_op jit(solution)/shard_map/ppermute | solution.py:235
  10.9 1.0 %copy-start = (bf16[1,128,2048]{2,1,0:T(8,128)(2,1)S(1)}, bf16[1,128,2048]{2,1,0:T(8,128)(2,1)}, u32[]{:S(2)}) copy-start(bf16[1,128,2048]{2,1,0:T(8,128)(2,1)} %param.8) | copy-start | bytes 1572868
  12.0 1.0 %copy-start.2 = (bf16[1,128,2048]{2,1,0:T(8,128)(2,1)S(1)}, bf16[1,128,2048]{2,1,0:T(8,128)(2,1)}, u32[]{:S(2)}) copy-start(bf16[1,128,2048]{2,1,0:T(8,128)(2,1)} %param.15) | copy-start | bytes 1572868
  13.0 0.8 copy-start.4
  13.8 0.8 copy-start.6
  14.6 0.8 copy-start.8
  17.2 2.8 %collective-permute-start.2 = (f32[2,136,1024]{2,1,0:T(8,128)S(1)}, f32[2,136,1024]{2,1,0:T(8,128)S(1)}, u32[]{:S(2)}, u32[]{:S(2)}) collective-permute-start(f32[2,136,1024]{2,1,0:T(8,128)S(1)} %get-tuple-element.28), channel_id=1, source_target_pairs={{0,1},{1,0},{2,3},{3,2},{4,5},{5,4},{6,7},{7,6},{8,9},{9,8},{10,11... | collective-permute-start | bytes 3342344 | tf_op jit(solution)/shard_map/ppermute | solution.py:235
  20.4 14.8 %collective-permute-start.4 = (f32[136,1024]{1,0:T(8,128)S(1)}, f32[136,1024]{1,0:T(8,128)S(1)}, u32[]{:S(2)}, u32[]{:S(2)}) collective-permute-start(f32[136,1024]{1,0:T(8,128)S(1)} %get-tuple-element.51), channel_id=1, source_target_pairs={{0,4},{1,5},{2,6},{3,7},{4,0},{5,1},{6,2},{7,3},{8,12},{9,13},{10,... | collective-permute-start | bytes 1671176 | tf_op jit(solution)/shard_map/ppermute | solution.py:235
  22.3 14.6 %collective-permute-start.3 = (f32[136,1024]{1,0:T(8,128)S(1)}, f32[136,1024]{1,0:T(8,128)S(1)}, u32[]{:S(2)}, u32[]{:S(2)}) collective-permute-start(f32[136,1024]{1,0:T(8,128)S(1)} %get-tuple-element.52), channel_id=1, source_target_pairs={{0,2},{1,3},{2,0},{3,1},{4,6},{5,7},{6,4},{7,5},{8,10},{9,11},{10,... | collective-permute-start | bytes 1671176 | tf_op jit(solution)/shard_map/ppermute | solution.py:235
  35.2 13.9 %collective-permute-start.5 = (f32[136,1024]{1,0:T(8,128)S(1)}, f32[136,1024]{1,0:T(8,128)S(1)}, u32[]{:S(2)}, u32[]{:S(2)}) collective-permute-start(f32[136,1024]{1,0:T(8,128)S(1)} %collective-permute-done.4), channel_id=1, source_target_pairs={{0,2},{1,3},{2,0},{3,1},{4,6},{5,7},{6,4},{7,5},{8,10},{9,11},{10,... | collective-permute-start | bytes 1671176 | tf_op jit(solution)/shard_map/ppermute | solution.py:235
  49.7 1.0 %copy-start.1 = (bf16[1,128,2048]{2,1,0:T(8,128)(2,1)S(1)}, bf16[1,128,2048]{2,1,0:T(8,128)(2,1)}, u32[]{:S(2)}) copy-start(bf16[1,128,2048]{2,1,0:T(8,128)(2,1)} %param.8) | copy-start | bytes 1572868
  49.7 1.2 %copy-start.3 = (bf16[1,128,2048]{2,1,0:T(8,128)(2,1)S(1)}, bf16[1,128,2048]{2,1,0:T(8,128)(2,1)}, u32[]{:S(2)}) copy-start(bf16[1,128,2048]{2,1,0:T(8,128)(2,1)} %param.15) | copy-start | bytes 1572868
  49.7 1.2 %copy-start.5 = (bf16[1,128,128]{2,1,0:T(8,128)(2,1)S(1)}, bf16[1,128,128]{2,1,0:T(8,128)(2,1)}, u32[]{:S(2)}) copy-start(bf16[1,128,128]{2,1,0:T(8,128)(2,1)} %param.9) | copy-start | bytes 98308
  49.7 1.2 %copy-start.7 = (bf16[1,128,128]{2,1,0:T(8,128)(2,1)S(1)}, bf16[1,128,128]{2,1,0:T(8,128)(2,1)}, u32[]{:S(2)}) copy-start(bf16[1,128,128]{2,1,0:T(8,128)(2,1)} %param.10) | copy-start | bytes 98308
  49.8 10.2 %collective-permute-start.6 = (f32[2,128,1024]{2,1,0:T(8,128)S(1)}, f32[2,128,1024]{2,1,0:T(8,128)S(1)}, u32[]{:S(2)}, u32[]{:S(2)}) collective-permute-start(f32[2,128,1024]{2,1,0:T(8,128)S(1)} %pad_maximum_fusion.1), channel_id=1, source_target_pairs={{0,1},{1,0},{2,3},{3,2},{4,5},{5,4},{6,7},{7,6},{8,9},{9,8},{10,11... | collective-permute-start | bytes 3145736 | tf_op jit(solution)/shard_map/ppermute | solution.py:235
  59.9 0.8 copy-start.9
  65.2 1.2 %collective-permute-start.7 = (f32[64,3]{1,0:T(8,128)S(1)}, f32[64,3]{1,0:T(8,128)S(1)}, u32[]{:S(2)}, u32[]{:S(2)}) collective-permute-start(f32[64,3]{1,0:T(8,128)S(1)} %bitcast.90), channel_id=1, source_target_pairs={{0,1},{1,0},{2,3},{3,2},{4,5},{5,4},{6,7},{7,6},{8,9},{9,8},{10,11... | collective-permute-start | bytes 2312 | tf_op jit(solution)/shard_map/ppermute | solution.py:235
  66.4 3.9 %collective-permute-start.8 = (f32[64,3]{1,0:T(8,128)S(1)}, f32[64,3]{1,0:T(8,128)S(1)}, u32[]{:S(2)}, u32[]{:S(2)}) collective-permute-start(f32[64,3]{1,0:T(8,128)S(1)} %slice_add_fusion.1), channel_id=1, source_target_pairs={{0,2},{1,3},{2,0},{3,1},{4,6},{5,7},{6,4},{7,5},{8,10},{9,11},{10,... | collective-permute-start | bytes 2312 | tf_op jit(solution)/shard_map/ppermute | solution.py:235
  70.3 3.9 %collective-permute-start.9 = (f32[64,3]{1,0:T(8,128)S(1)}, f32[64,3]{1,0:T(8,128)S(1)}, u32[]{:S(2)}, u32[]{:S(2)}) collective-permute-start(f32[64,3]{1,0:T(8,128)S(1)} %add.56), channel_id=1, source_target_pairs={{0,4},{1,5},{2,6},{3,7},{4,0},{5,1},{6,2},{7,3},{8,12},{9,13},{10,... | collective-permute-start | bytes 2312 | tf_op jit(solution)/shard_map/ppermute | solution.py:235
  74.2 4.7 %collective-permute-start.10 = (f32[32,3]{1,0:T(8,128)S(1)}, f32[32,3]{1,0:T(8,128)S(1)}, u32[]{:S(2)}, u32[]{:S(2)}) collective-permute-start(f32[32,3]{1,0:T(8,128)S(1)} %slice_select_fusion), channel_id=1, source_target_pairs={{0,16},{8,24},{16,0},{24,8},{1,17},{9,25},{17,1},{25,9},{2,18},{10... | collective-permute-start | bytes 1160 | tf_op jit(solution)/shard_map/ppermute | solution.py:235
  78.9 3.7 %collective-permute-start.11 = (f32[16,3]{1,0:T(8,128)S(1)}, f32[16,3]{1,0:T(8,128)S(1)}, u32[]{:S(2)}, u32[]{:S(2)}) collective-permute-start(f32[16,3]{1,0:T(8,128)S(1)} %slice_select_fusion.1), channel_id=1, source_target_pairs={{0,8},{8,0},{16,24},{24,16},{1,9},{9,1},{17,25},{25,17},{2,10},{10... | collective-permute-start | bytes 584 | tf_op jit(solution)/shard_map/ppermute | solution.py:235

commit v2 on v1

v2 whole, which is shorter than its diff:
```python
import jax
import jax.numpy as jnp
from jax import lax
from jax.experimental import pallas as pl
from jax.experimental.pallas import tpu as pltpu
from jax.sharding import PartitionSpec as P


F32, BF16 = jnp.float32, jnp.bfloat16
EXACT = lax.Precision.HIGHEST
NT = (((1,), (1,)), ((), ()))
NN = (((1,), (0,)), ((), ()))
LANES = 128
PAD = 8


def mm(a, b, dims=NN):
    return lax.dot_general(a, b, dims, preferred_element_type=F32)


def exact_mm(a, b, dims=NN):
    return lax.dot_general(a, b, dims, precision=EXACT, preferred_element_type=F32)


def split(v):
    hi = v.astype(BF16)
    return hi, (v - hi.astype(F32)).astype(BF16)


def spread(heads, width, first, lanes):
    head = lax.broadcasted_iota(jnp.int32, (heads, lanes), 0)
    lane = lax.broadcasted_iota(jnp.int32, (heads, lanes), 1) + first
    inside = jnp.logical_and(lane >= head * width, lane < head * width + width)
    return jnp.where(inside, 1.0, 0.0).astype(BF16)


def expand(per_head, hot):
    hi, lo = split(per_head)
    return mm(jnp.concatenate([hi, lo], axis=1), jnp.concatenate([hot, hot], axis=0))


def scans(raw, par):
    rate, bias = par[:, 0:1], par[:, 1:2]
    z = raw + bias
    step = jnp.maximum(z, 0.0) + jnp.log1p(jnp.exp(-jnp.abs(z)))
    scale = -jnp.exp(rate)
    logdecay = scale * step
    count = raw.shape[1]
    early = lax.broadcasted_iota(jnp.int32, (count, count), 0)
    late = lax.broadcasted_iota(jnp.int32, (count, count), 1)
    upper = jnp.where(early <= late, 1.0, 0.0)
    cum = exact_mm(logdecay, upper)
    return z, step, scale, logdecay, cum, upper


def prep_kernel(x_ref, g_ref, b_ref, r_ref, raw_ref, *rest):
    outs, sems = rest[:5], rest[5]
    copies = [
        pltpu.make_async_copy(src, dst, sems.at[k])
        for k, (src, dst) in enumerate(zip((x_ref, g_ref, b_ref, r_ref, raw_ref), outs))
    ]
    for copy in copies:
        copy.start()
    for copy in copies:
        copy.wait()


def ends_kernel(c_ref, x_ref, g_ref, b_ref, r_ref, raw_ref, par_ref, own_ref, oth_ref, cum_ref, step_ref):
    heads, count = raw_ref.shape
    total = x_ref.shape[1]
    half = total // 2
    width = total // heads
    part = half // 2
    _, step, _, _, cum, _ = scans(raw_ref[...], par_ref[...])
    cum_ref[...] = cum
    step_ref[...] = step
    tail = (jnp.exp(cum[:, -1:] - cum) * step).T
    grow = jnp.exp(cum).T
    bt = b_ref[...].astype(F32).T.astype(BF16)
    ct = r_ref[...].astype(F32).T.astype(BF16)
    bt2 = jnp.concatenate([bt, bt], axis=1)
    ct2 = jnp.concatenate([ct, ct], axis=1)
    c = c_ref[0]
    size = b_ref.shape[1]
    for which, out in ((1 - c, oth_ref), (c, own_ref)):
        for k in range(2):
            first = pl.multiple_of(which * half + k * part, part)
            hot = spread(heads, width, first, part)
            here = pl.ds(first, part)
            grow_x = expand(grow, hot)
            xt = expand(tail, hot) * x_ref[:, here].astype(F32)
            out[0, k, :size] = mm(bt2, jnp.concatenate(split(xt), axis=0))
            gt = grow_x * g_ref[:, here].astype(F32)
            out[1, k, :size] = mm(ct2, jnp.concatenate(split(gt), axis=0))
            last = jnp.broadcast_to(grow_x[count - 1 :, :], (PAD, part))
            out[0, k, size:] = last
            out[1, k, size:] = last


def gram_kernel(b_ref, r_ref, gram_ref, gram_t_ref):
    b, r = b_ref[...], r_ref[...]
    row = lax.broadcasted_iota(jnp.int32, gram_ref.shape, 0)
    col = lax.broadcasted_iota(jnp.int32, gram_ref.shape, 1)
    gram_ref[...] = jnp.where(row >= col, mm(r, b, NT), 0.0)
    gram_t_ref[...] = jnp.where(row <= col, mm(b, r, NT), 0.0)


def inside_kernel(x_ref, g_ref, b_ref, r_ref, cum_ref, step_ref, gram_ref, gram_t_ref, inner_ref, dxin_ref, db_ref, dc_ref, cumt_ref, dgram_ref):
    heads, count = cum_ref.shape
    total = x_ref.shape[1]
    width = total // heads
    pack = LANES // width
    t_row = lax.broadcasted_iota(jnp.int32, (count, count), 0)
    t_col = lax.broadcasted_iota(jnp.int32, (count, count), 1)
    b, r = b_ref[...], r_ref[...]
    gram, gram_t = gram_ref[...], gram_t_ref[...]
    cum_all = cum_ref[...]
    cumt_ref[...] = jnp.concatenate([cum_all, jnp.zeros((LANES - heads, count), F32)], axis=0).T
    step_t = step_ref[...].T
    dgram_ref[...] = jnp.zeros_like(dgram_ref)
    lane = lax.broadcasted_iota(jnp.int32, (count, LANES), 1)

    def group(j, _):
        at = pl.multiple_of(j * LANES, LANES)
        x4 = x_ref[:, pl.ds(at, LANES)]
        g4 = g_ref[:, pl.ds(at, LANES)]
        cols = pltpu.roll(cumt_ref[...], LANES - j * pack, 1)
        his, los, thi, tlo, xs, gs = [], [], [], [], [], []
        dgram = dgram_ref[...]
        for i in range(pack):
            head = j * pack + i
            row = cum_ref[pl.ds(head, 1), :]
            step_row = step_ref[pl.ds(head, 1), :]
            diff = cols[:, i : i + 1] - row
            seg = jnp.exp(jnp.minimum(diff, 0.0)) * step_row
            seg_t = jnp.exp(jnp.minimum(-diff, 0.0))
            mine = jnp.logical_and(lane >= i * width, lane < (i + 1) * width)
            xm = jnp.where(mine, x4.astype(F32), 0.0).astype(BF16)
            gm = jnp.where(mine, g4.astype(F32), 0.0).astype(BF16)
            dgram = dgram + mm(gm, x4, NT) * seg
            hi, lo = split(gram * seg)
            his.append(hi)
            los.append(lo)
            hi, lo = split(gram_t * seg_t)
            thi.append(hi)
            tlo.append(lo)
            xs.append(xm)
            gs.append(gm)
        dgram_ref[...] = dgram
        inner_ref[:, pl.ds(at, LANES)] = mm(jnp.concatenate(his + los, axis=1), jnp.concatenate(xs + xs, axis=0))
        hot = spread(heads, width, at, LANES)
        back = mm(jnp.concatenate(thi + tlo, axis=1), jnp.concatenate(gs + gs, axis=0))
        dxin_ref[:, pl.ds(at, LANES)] = back * expand(step_t, hot)
        return 0

    lax.fori_loop(0, heads // pack, group, 0)
    dgram = jnp.where(t_row >= t_col, dgram_ref[...], 0.0)
    hi, lo = split(dgram)
    dc_ref[...] = mm(jnp.concatenate([hi, lo], axis=1), jnp.concatenate([b, b], axis=0))
    hi, lo = split(dgram.T)
    db_ref[...] = mm(jnp.concatenate([hi, lo], axis=1), jnp.concatenate([r, r], axis=0))


def carried(which, src, x_ref, g_ref, b_ref, r_ref, raw, par, inner_ref, dxin_ref, db, dc, uv, sums, y_ref, dx_ref, offset):
    heads, _ = raw.shape
    total = x_ref.shape[1]
    half = total // 2
    width = total // heads
    part = half // 2
    z, step, scale, logdecay, cum, upper = scans(raw, par)
    tail = (jnp.exp(cum[:, -1:] - cum) * step).T
    grow = jnp.exp(cum).T
    skip = jnp.broadcast_to(par[:, 2:3], (heads, LANES)).T[:PAD]
    b, r = b_ref[...], r_ref[...]
    b2 = jnp.concatenate([b, b], axis=1)
    r2 = jnp.concatenate([r, r], axis=1)
    for k in range(2):
        first = pl.multiple_of(which * half + k * part, part)
        hot = spread(heads, width, first, part)
        here = pl.ds(first, part)
        out = pl.ds(pl.multiple_of(offset + k * part, part), part)
        x = x_ref[:, here].astype(F32)
        g = g_ref[:, here].astype(F32)
        grow_x, tail_x, skip_x = expand(grow, hot), expand(tail, hot), expand(skip, hot)[0:1]
        before, later = src[0, k], src[1, k]
        h_hi, h_lo = split(before)
        d_hi, d_lo = split(later)
        flow = inner_ref[:, here] + grow_x * mm(r2, jnp.concatenate([h_hi, h_lo], axis=0))
        y_ref[:, out] = (flow + skip_x * x).astype(BF16)
        reach = tail_x * mm(b2, jnp.concatenate([d_hi, d_lo], axis=0))
        back = dxin_ref[:, here] + reach
        dx_ref[:, out] = (back + skip_x * g).astype(BF16)
        uv_hi, uv_lo = split(jnp.concatenate([g * flow, x * back], axis=0))
        uv = uv + mm(uv_hi, hot, NT) + mm(uv_lo, hot, NT)
        parts = jnp.concatenate(
            [jnp.sum(v.reshape(-1, PAD, part), axis=0) for v in (x * reach, before * later, g * x)], axis=0
        )
        s_hi, s_lo = split(parts)
        sums = sums + mm(s_hi, hot, NT) + mm(s_lo, hot, NT)
        e_hi, e_lo = split(grow_x * g)
        dc = dc + mm(e_hi, h_hi, NT) + mm(e_hi, h_lo, NT) + mm(e_lo, h_hi, NT)
        t_hi, t_lo = split(tail_x * x)
        db = db + mm(t_hi, d_hi, NT) + mm(t_hi, d_lo, NT) + mm(t_lo, d_hi, NT)
    return db, dc, uv, sums, (z, step, scale, logdecay, cum, upper)


def first_kernel(
    c_ref, x_ref, g_ref, b_ref, r_ref, raw_ref, par_ref, inner_ref, dxin_ref, db0_ref, dc0_ref, src_ref,
    y_ref, dx_ref, db_ref, dc_ref, uv_ref, sums_ref,
):
    uv, sums = jnp.zeros(uv_ref.shape, F32), jnp.zeros(sums_ref.shape, F32)
    db_ref[...], dc_ref[...], uv_ref[...], sums_ref[...], _ = carried(
        c_ref[0], src_ref, x_ref, g_ref, b_ref, r_ref, raw_ref[...], par_ref[...], inner_ref, dxin_ref,
        db0_ref[...], dc0_ref[...], uv, sums, y_ref, dx_ref, 0,
    )


def second_kernel(
    c_ref, x_ref, g_ref, b_ref, r_ref, raw_ref, par_ref, inner_ref, dxin_ref, db0_ref, dc0_ref, src_ref,
    y0_ref, dx0_ref, uv0_ref, sums0_ref, y_ref, dx_ref, db_ref, dc_ref, draw_ref, tot_ref,
):
    heads, count = raw_ref.shape
    half = x_ref.shape[1] // 2
    c = c_ref[0]
    other = (1 - c) * half
    db_ref[...], dc_ref[...], uv, sums, (z, step, scale, logdecay, cum, upper) = carried(
        1 - c, src_ref, x_ref, g_ref, b_ref, r_ref, raw_ref[...], par_ref[...], inner_ref, dxin_ref,
        db0_ref[...], dc0_ref[...], uv0_ref[...], sums0_ref[...], y_ref, dx_ref, other,
    )
    mine = pl.ds(pl.multiple_of(c * half, half), half)
    y_ref[:, mine] = y0_ref[...]
    dx_ref[:, mine] = dx0_ref[...]
    u = uv[:count].T
    v = uv[count:].T
    sums_t = sums.T
    reach_sum = jnp.sum(sums_t[:, :PAD], axis=1, keepdims=True)
    meet_sum = jnp.sum(sums_t[:, PAD : 2 * PAD], axis=1, keepdims=True)
    skip_sum = jnp.sum(sums_t[:, 2 * PAD :], axis=1, keepdims=True)
    end = reach_sum + jnp.exp(cum[:, -1:]) * meet_sum
    dlog = exact_mm(u - v, upper, NT) + end
    draw = (scale * dlog + v / step) * jax.nn.sigmoid(z)
    draw_ref[...] = draw
    column = lax.broadcasted_iota(jnp.int32, (heads, LANES), 1)
    rate_sum = jnp.sum(dlog * logdecay, axis=1, keepdims=True)
    bias_sum = jnp.sum(draw, axis=1, keepdims=True)
    tot_ref[...] = jnp.where(column == 0, rate_sum, jnp.where(column == 1, bias_sum, jnp.where(column == 2, skip_sum, 0.0)))


def call(kernel, outs, args, scratch=(), flops=0, scalar=False, off_chip=False):
    if off_chip:
        args = tuple(pltpu.with_memory_space_constraint(a, pltpu.HBM) for a in args)
    vmem = pl.BlockSpec(memory_space=pltpu.VMEM)
    specs = [pl.BlockSpec(memory_space=pltpu.HBM) if off_chip else vmem] * len(args)
    if scalar:
        specs[0] = pl.BlockSpec(memory_space=pltpu.SMEM)
    size = sum(a.size * a.dtype.itemsize for a in (*args, *outs))
    return pl.pallas_call(
        kernel,
        out_shape=outs,
        in_specs=specs,
        out_specs=tuple([vmem] * len(outs)),
        scratch_shapes=list(scratch),
        cost_estimate=pl.CostEstimate(flops=flops, bytes_accessed=size, transcendentals=0),
        compiler_params=pltpu.CompilerParams(vmem_limit_bytes=32 << 20),
    )(*args)


def swap(value, axis, bit):
    return lax.ppermute(value, axis, [(i, i ^ bit) for i in range(lax.axis_size(axis))])


def gathered(value, axis):
    place, bit = lax.axis_index(axis), 1
    while bit < lax.axis_size(axis):
        other = swap(value, axis, bit)
        low = (place & bit) == 0
        value = jnp.concatenate([jnp.where(low, value, other), jnp.where(low, other, value)], axis=0)
        bit *= 2
    return value


def owned_sum(value, axis):
    place, bit = lax.axis_index(axis), lax.axis_size(axis) // 2
    while bit:
        lower, upper = jnp.split(value, 2, axis=0)
        low = (place & bit) == 0
        value = jnp.where(low, lower, upper) + swap(jnp.where(low, upper, lower), axis, bit)
        bit //= 2
    return value


def total_sum(value, axis):
    bit = 1
    while bit < lax.axis_size(axis):
        value = value + swap(value, axis, bit)
        bit *= 2
    return value


def planned(mesh_size):
    return mesh_size == 8


def chip_carries(total, size):
    n = lax.axis_size("ctx")
    place = lax.axis_index("ctx")

    def state(v):
        return v[..., :size, :]

    def decay(v):
        return v[..., size : size + 1, :]

    if planned(n):
        x1, y1 = (place & 2) != 0, (place & 4) != 0
        bent = x1 != y1
        (f_a, f_b), (r_a, r_b) = total[0], total[1]
        own_a, own_b = jnp.where(y1, r_a, f_a), jnp.where(y1, f_b, r_b)
        xa = swap(own_a, "ctx", 2)
        yb = swap(jnp.where(y1, r_b, f_b), "ctx", 4)
        late = swap(jnp.where(y1, jnp.where(x1, r_b, f_a), jnp.where(x1, r_a, f_b)), "ctx", 2)
        diag = swap(f_b[size:], "ctx", 6)
        first, second = jnp.where(x1, xa, own_a), jnp.where(x1, own_a, xa)
        row = jnp.where(y1, state(first) + decay(first) * state(second), state(second) + decay(second) * state(first))
        ya = swap(row, "ctx", 4)
        both = state(own_b) + decay(own_b) * diag[:1] * state(yb)
        onward = jnp.concatenate([jnp.where(bent, both, state(yb)), jnp.where(bent, own_b[size:], yb[size:])], axis=0)
        xb = swap(onward, "ctx", 2)
        far = jnp.stack([jnp.where(bent, ya, state(late) + decay(late) * ya), state(xb) + decay(xb) * state(yb)])
        near = jnp.where(bent, jnp.stack([state(xa), state(late)]), 0.0)
        return jnp.where(y1, far, near), jnp.where(y1, near, far)
    fwd, bwd = total[0], total[1]
    ahead = behind = jnp.zeros_like(state(fwd))
    ahead_decay = behind_decay = jnp.ones_like(decay(fwd))
    bit = 2
    while bit < n:
        o_fwd, o_bwd = swap(fwd, "ctx", bit), swap(bwd, "ctx", bit)
        up = (place & bit) != 0
        ahead = jnp.where(up, ahead + ahead_decay * state(o_fwd), ahead)
        ahead_decay = jnp.where(up, ahead_decay * decay(o_fwd), ahead_decay)
        behind = jnp.where(up, behind, behind + behind_decay * state(o_bwd))
        behind_decay = jnp.where(up, behind_decay, behind_decay * decay(o_bwd))
        both = fwd[..., size:, :] * o_fwd[..., size:, :]
        f1, f2 = jnp.where(up, o_fwd, fwd), jnp.where(up, fwd, o_fwd)
        b1, b2 = jnp.where(up, o_bwd, bwd), jnp.where(up, bwd, o_bwd)
        fwd = jnp.concatenate([state(f2) + decay(f2) * state(f1), both], axis=-2)
        bwd = jnp.concatenate([state(b1) + decay(b1) * state(b2), both], axis=-2)
        bit *= 2
    return ahead, behind


def local(x, b, r, raw, rate, bias, skip, g):
    return layer(x[0], b[0], r[0], raw[0], rate, bias, skip, g[0])


def layer(x, b, r, raw, rate, bias, skip, g):
    heads, count = raw.shape
    total, size = x.shape[1], b.shape[1]
    half = total // 2
    part = half // 2
    shape = jax.ShapeDtypeStruct
    par = gathered(jnp.stack([rate, bias, skip], axis=1), "dp")
    core = lax.axis_index("ctx") & 1
    odd = core == 1
    c = core.astype(jnp.int32).reshape(1)
    message = shape((2, 2, size + PAD, part), F32)
    small = shape((heads, count), F32)
    wide = shape((count, total), F32)
    square = shape((count, size), F32)
    mixed = shape((count, count), F32)
    args = (x, g, b, r, raw)
    x, g, b, r, raw = call(
        prep_kernel, tuple(shape(v.shape, v.dtype) for v in args), args,
        scratch=[pltpu.SemaphoreType.DMA((len(args),))], off_chip=True,
    )
    own, oth, cum, step = call(
        ends_kernel, (message, message, small, small), (c, x, g, b, r, raw, par), flops=10**9, scalar=True
    )
    mate = swap(oth, "ctx", 1)
    s_o, g_o, a_o = own[0, :, :size], own[1, :, :size], own[0, :, size:]
    s_p, g_p, a_p = mate[0, :, :size], mate[1, :, :size], mate[0, :, size:]
    fwd = jnp.where(odd, a_o[:, :1] * s_p + s_o, a_p[:, :1] * s_o + s_p)
    bwd = jnp.where(odd, g_p + a_p[:, :1] * g_o, g_o + a_o[:, :1] * g_p)
    decay = a_o * a_p
    chip = jnp.stack([jnp.concatenate([fwd, decay], axis=1), jnp.concatenate([bwd, decay], axis=1)])
    ahead, behind = chip_carries(chip, size)
    gram, gram_t = call(gram_kernel, (mixed, mixed), (b, r), flops=10**7)
    inner, dxin, db0, dc0 = call(
        inside_kernel,
        (wide, wide, square, square),
        (x, g, b, r, cum, step, gram, gram_t),
        scratch=[pltpu.VMEM((count, LANES), F32), pltpu.VMEM((count, count), F32)],
        flops=10**9,
    )
    through = jnp.where(odd, a_p[:, :1], a_o[:, :1]) * ahead + jnp.where(odd, s_p, s_o)
    theirs = jnp.where(odd, ahead, through), jnp.where(odd, g_o + a_o[:, :1] * behind, behind)
    rest = swap(jnp.stack(theirs), "ctx", 1)
    mine = jnp.stack([jnp.where(odd, through, ahead), jnp.where(odd, behind, g_p + a_p[:, :1] * behind)])
    ready = (c, x, g, b, r, raw, par, inner, dxin)
    halved = shape((count, half), BF16)
    whole = shape((count, total), BF16)
    y0, dx0, db1, dc1, uv, sums = call(
        first_kernel,
        (halved, halved, square, square, shape((2 * count, heads), F32), shape((3 * PAD, heads), F32)),
        (*ready, db0, dc0, mine), flops=10**9, scalar=True,
    )
    y, dx, db, dc, draw, tot = call(
        second_kernel, (whole, whole, square, square, small, shape((heads, LANES), F32)),
        (*ready, db1, dc1, rest, y0, dx0, uv, sums), flops=10**9, scalar=True,
    )
    owned = owned_sum(total_sum(tot[:, :3], "ctx"), "dp")
    return (y[None], dx[None], db[None], dc[None], draw[None], owned[:, 0], owned[:, 1], owned[:, 2])


def solution(mesh):
    wide = P("dp", "ctx", None)
    strides = P("dp", None, "ctx")
    return jax.shard_map(
        local,
        mesh=mesh,
        in_specs=(wide, wide, wide, strides, P("dp"), P("dp"), P("dp"), wide),
        out_specs=(wide, wide, wide, wide, strides, P("dp"), P("dp"), P("dp")),
        check_vma=False,
    )
```

time: 83.9 us -> 76.7 us (0.914)
  waiting for transfers between devices: 39.4 us -> 28.9 us
  local copies, waits for them, and re-layouts: 6.82 us -> 1.62 us
  other arithmetic: 2.11 us -> 6.91 us
  Pallas kernels: 15.1 us -> 17.3 us
  starting transfers between devices: 19.2 us -> 20.7 us
    ppermute x12 -> x15, waiting for transfers between devices: 39.4 us -> 28.9 us  [swap(): lax.ppermute(value, axis, [(i, i ^ bit) for i in range(lax.axis_size(axis...]
    unnamed x20 -> x2, local copies, waits for them, and re-layouts: 5.98 us -> 0.01 us
    select_n x4 -> x9, other arithmetic: 0.47 us -> 5.09 us  [the longest x1 1.45 us: layer(): fwd = jnp.where(odd, a_o[:, :1] * s_p + s_o, a_p[:, :1] * s_o + s_p)]
    pallas_call x3 -> x6, Pallas kernels: 15.1 us -> 17.3 us  [call(): pl.pallas_call(kernel, out_shape=outs, in_specs=specs, out_specs=tuple([v...]
    ppermute x12 -> x15, starting transfers between devices: 19.2 us -> 20.7 us  [swap(): lax.ppermute(value, axis, [(i, i ^ bit) for i in range(lax.axis_size(axis...]
  transfers between devices with their start and end apart: 12 -> 15, of which waited for: 10 -> 13; matrix products, arithmetic and copies ran while one was open for 0% -> 0% of each run, Pallas kernels for 10% -> 16%
where the time goes in v2:
time: 76.7 us; the launch traced here: 76.3 us
  waiting for transfers between devices  28.9 us (38%)
  starting transfers between devices  20.7 us (27%)
  Pallas kernels  17.3 us (23%)
  other arithmetic  6.91 us (9%)
  local copies, waits for them, and re-layouts  1.62 us (2%)
  between operations  0.83 us (1%)
    ppermute x15, waiting for transfers between devices, swap(): lax.ppermute(value, axis, [(i, i ^ bit) for i in range(lax.axis_size(axis...  28.9 us
    ppermute x15, starting transfers between devices, swap(): lax.ppermute(value, axis, [(i, i ^ bit) for i in range(lax.axis_size(axis...  20.7 us
    pallas_call x6, Pallas kernels, call(): pl.pallas_call(kernel, out_shape=outs, in_specs=specs, out_specs=tuple([v...  17.3 us
  transfers between devices with their start and end apart: 15, of which 13 were waited for; matrix products, arithmetic and copies ran while one was open for 0% of the time, Pallas kernels for 16%

profile of v2, /device:TPU:0, one launch (start us, length us, event | category | flops | bytes accessed | tf_op | source)
XLA Modules:
  0.0 76.3 jit_solution(3564102996193169767)
XLA Ops:
  1.4 3.1 %collective-permute-start = (f32[16,3]{1,0:T(8,128)S(1)}, f32[16,3]{1,0:T(8,128)S(1)}, u32[]{:S(2)}, u32[]{:S(2)}) collective-permute-start(f32[16,3]{1,0:T(8,128)S(1)} %copy.36), channel_id=1, source_target_pairs={{0,8},{8,0},{16,24},{24,16},{1,9},{9,1},{17,25},{25,17},{2,10},{10... | collective-permute-start | bytes 584 | tf_op jit(solution)/shard_map/ppermute | solution.py:269
  4.5 1.6 %collective-permute-done = f32[16,3]{1,0:T(8,128)S(1)} collective-permute-done((f32[16,3]{1,0:T(8,128)S(1)}, f32[16,3]{1,0:T(8,128)S(1)}, u32[]{:S(2)}, u32[]{:S(2)}) %collective-permute-start) | collective-permute-done | bytes 224 | tf_op jit(solution)/shard_map/ppermute | solution.py:269
  6.1 3.1 %collective-permute-start.1 = (f32[32,3]{1,0:T(8,128)S(1)}, f32[32,3]{1,0:T(8,128)S(1)}, u32[]{:S(2)}, u32[]{:S(2)}) collective-permute-start(f32[32,3]{1,0:T(8,128)S(1)} %pad_maximum_fusion.7), channel_id=1, source_target_pairs={{0,16},{8,24},{16,0},{24,8},{1,17},{9,25},{17,1},{25,9},{2,18},{10... | collective-permute-start | bytes 1160 | tf_op jit(solution)/shard_map/ppermute | solution.py:269
  9.2 1.2 %shard_map.143 = (bf16[128,2048]{1,0:T(8,128)(2,1)S(1)}, bf16[128,2048]{1,0:T(8,128)(2,1)S(1)}, bf16[128,128]{1,0:T(8,128)(2,1)S(1)}, bf16[128,128]{1,0:T(8,128)(2,1)S(1)}, f32[64,128]{1,0:T(8,128)S(1)}) custom-call(bf16[128,2048]{1,0:T(8,128)(2,1)} %bitcast.94, bf16[128,2048]{1,0:T(8,128)(2,1)} %bitcast.95, bf16[128,128]{1,0:T(8,128)(2,1)} %bitcast.96, ...), custom_call_target="tpu_custom_call" | custom-call | bytes 2293760 | tf_op jit(solution)/shard_map/pallas_call | solution.py:257
  10.9 1.9 %shard_map.144 = (f32[2,2,136,512]{3,2,1,0:T(8,128)S(1)}, f32[2,2,136,512]{3,2,1,0:T(8,128)S(1)}, f32[64,128]{1,0:T(8,128)S(1)}, f32[64,128]{1,0:T(8,128)S(1)}) custom-call(s32[1]{0:T(128)} %bitcast.c_ref, bf16[128,2048]{1,0:T(8,128)(2,1)S(1)} %get-tuple-element.35.x_ref, bf16[128,2048]{1,0:T(8,128)(2,1)S(1)} %get-tuple-element.36.g_ref, ...), custom_call_target="tpu_custom_call" | custom-call | flops 1000000000 | bytes 3441412 | tf_op jit(solution)/shard_map/pallas_call | solution.py:257
  12.9 2.9 %collective-permute-done.2 = f32[2,2,136,512]{3,2,1,0:T(8,128)} collective-permute-done((f32[2,2,136,512]{3,2,1,0:T(8,128)S(1)}, f32[2,2,136,512]{3,2,1,0:T(8,128)}, u32[]{:S(2)}, u32[]{:S(2)}) %collective-permute-start.2) | collective-permute-done | bytes 1114144 | tf_op jit(solution)/shard_map/ppermute | solution.py:269
  15.8 0.8 slice_bitcast_fusion.3
  16.6 0.8 %fusion.13 = f32[2,8,512]{2,1,0:T(8,128)S(1)} fusion(f32[2,2,136,512]{3,2,1,0:T(8,128)S(1)} %get-tuple-element.49, f32[2,2,136,512]{3,2,1,0:T(8,128)} %collective-permute-done.2), kind=kLoop, calls=%fused_computation.69 | loop fusion | flops 8192 | bytes 98304 | tf_op jit(solution)/shard_map/mul | solution.py:384
  17.3 1.5 %fusion = (f32[2,128,512]{2,1,0:T(8,128)S(1)}, f32[2,128,512]{2,1,0:T(8,128)S(1)}) fusion(f32[2,2,136,512]{3,2,1,0:T(8,128)} %collective-permute-done.2, f32[2,2,136,512]{3,2,1,0:T(8,128)S(1)} %get-tuple-element.49, f32[2,512]{1,0:T(2,128)S(1)} %get-tuple-element.86, f32[2,512]{1,0:T(2,128)S(1)} %get-tuple-element.87, pred[]{:T(512)S(6)} %eq.13), kind=kLoop, calls=%fused_computation.9 | loop fusion | flops 1310720 | bytes 3153921 | tf_op jit(solution)/shard_map/jit(_where)/select_n | solution.py:382
  18.8 0.9 %select_bitcast_fusion.1 = (f32[136,512]{1,0:T(8,128)S(1)}, f32[1,136,512]{2,1,0:T(8,128)S(1)}, f32[136,512]{1,0:T(8,128)}, f32[136,512]{1,0:T(8,128)S(1)}) fusion(pred[]{:T(512)S(6)} %ne.10, pred[]{:T(512)S(6)} %ne.9, f32[2,8,512]{2,1,0:T(8,128)S(1)} %fusion.13, f32[2,128,512]{2,1,0:T(8,128)S(1)} %get-tuple-element.68, f32[2,128,512]{2,1,0:T(8,128)S(1)} %get-tuple-element.67), kind=kLoop, calls=%fused_computation.30 | loop fusion | flops 835584 | bytes 2195458 | tf_op jit(solution)/shard_map/jit(_where)/select_n | solution.py:321
  19.6 1.8 %collective-permute-start.3 = (f32[136,512]{1,0:T(8,128)S(1)}, f32[136,512]{1,0:T(8,128)S(1)}, u32[]{:S(2)}, u32[]{:S(2)}) collective-permute-start(f32[136,512]{1,0:T(8,128)S(1)} %get-tuple-element.72), channel_id=1, source_target_pairs={{0,2},{1,3},{2,0},{3,1},{4,6},{5,7},{6,4},{7,5},{8,10},{9,11},{10,... | collective-permute-start | bytes 835592 | tf_op jit(solution)/shard_map/ppermute | solution.py:269
  21.5 1.5 %collective-permute-start.6 = (f32[8,512]{1,0:T(8,128)S(1)}, f32[8,512]{1,0:T(8,128)S(1)}, u32[]{:S(2)}, u32[]{:S(2)}) collective-permute-start(f32[8,512]{1,0:T(8,128)S(1)} %slice_bitcast_fusion.6), channel_id=1, source_target_pairs={{0,6},{1,7},{2,4},{3,5},{4,2},{5,3},{6,0},{7,1},{8,14},{9,15},{10,... | collective-permute-start | bytes 49160 | tf_op jit(solution)/shard_map/ppermute | solution.py:269
  23.0 1.5 %collective-permute-start.5 = (f32[136,512]{1,0:T(8,128)S(1)}, f32[136,512]{1,0:T(8,128)S(1)}, u32[]{:S(2)}, u32[]{:S(2)}) collective-permute-start(f32[136,512]{1,0:T(8,128)S(1)} %get-tuple-element.69), channel_id=1, source_target_pairs={{0,2},{1,3},{2,0},{3,1},{4,6},{5,7},{6,4},{7,5},{8,10},{9,11},{10,... | collective-permute-start | bytes 835592 | tf_op jit(solution)/shard_map/ppermute | solution.py:269
  25.0 5.8 %collective-permute-done.6 = f32[8,512]{1,0:T(8,128)S(1)} collective-permute-done((f32[8,512]{1,0:T(8,128)S(1)}, f32[8,512]{1,0:T(8,128)S(1)}, u32[]{:S(2)}, u32[]{:S(2)}) %collective-permute-start.6) | collective-permute-done | bytes 16416 | tf_op jit(solution)/shard_map/ppermute | solution.py:269
  31.2 2.7 %collective-permute-done.7 = f32[136,512]{1,0:T(8,128)S(1)} collective-permute-done((f32[136,512]{1,0:T(8,128)}, f32[136,512]{1,0:T(8,128)S(1)}, u32[]{:S(2)}, u32[]{:S(2)}) %collective-permute-start.7) | collective-permute-done | bytes 278560 | tf_op jit(solution)/shard_map/ppermute | solution.py:269
  34.2 1.3 %collective-permute-done.5 = f32[136,512]{1,0:T(8,128)S(1)} collective-permute-done((f32[136,512]{1,0:T(8,128)S(1)}, f32[136,512]{1,0:T(8,128)S(1)}, u32[]{:S(2)}, u32[]{:S(2)}) %collective-permute-start.5) | collective-permute-done | bytes 278560 | tf_op jit(solution)/shard_map/ppermute | solution.py:269
  35.4 3.1 %collective-permute-done.4 = f32[128,512]{1,0:T(8,128)S(1)} collective-permute-done((f32[128,512]{1,0:T(8,128)S(1)}, f32[128,512]{1,0:T(8,128)S(1)}, u32[]{:S(2)}, u32[]{:S(2)}) %collective-permute-start.4) | collective-permute-done | bytes 262176 | tf_op jit(solution)/shard_map/ppermute | solution.py:269
  38.5 2.2 %collective-permute-done.8 = f32[136,512]{1,0:T(8,128)S(1)} collective-permute-done((f32[136,512]{1,0:T(8,128)S(1)}, f32[136,512]{1,0:T(8,128)S(1)}, u32[]{:S(2)}, u32[]{:S(2)}) %collective-permute-start.8) | collective-permute-done | bytes 278560 | tf_op jit(solution)/shard_map/ppermute | solution.py:269
  40.8 1.3 %add_select_fusion = (f32[1,2,128,512]{3,2,1,0:T(8,128)S(1)}, f32[1,2,128,512]{3,2,1,0:T(8,128)S(1)}) fusion(f32[2,2,136,512]{3,2,1,0:T(8,128)S(1)} %get-tuple-element.49, f32[2,512]{1,0:T(2,128)S(1)} %get-tuple-element.86, pred[]{:T(512)S(6)} %eq.13, f32[1,1,128,512]{3,2,1,0:T(8,128)S(1)} %fusion.10, f32[1,1,128,512]{3,2,1,0:T(8,128)S(1)} %get-tuple-element.78, ...), kind=kLoop, calls=%fused_computation.17 | loop fusion | flops 1310720 | bytes 3153923 | tf_op jit(solution)/shard_map/jit(_where)/select_n | solution.py:396
  42.1 1.3 %fusion.6 = (f32[1,2,128,512]{3,2,1,0:T(8,128)S(1)}, f32[1,2,128,512]{3,2,1,0:T(8,128)S(1)}) fusion(f32[2,2,136,512]{3,2,1,0:T(8,128)S(1)} %get-tuple-element.49, f32[2,2,136,512]{3,2,1,0:T(8,128)} %collective-permute-done.2, f32[2,512]{1,0:T(2,128)S(1)} %bitcast.99, pred[]{:T(512)S(6)} %eq.13, f32[1,1,128,512]{3,2,1,0:T(8,128)S(1)} %get-tuple-element.77, ...), kind=kLoop, calls=%fused_computation.24 | loop fusion | flops 1179648 | bytes 3149827 | tf_op jit(solution)/shard_map/jit(_where)/select_n | solution.py:396
  43.7 8.6 %shard_map.146 = (f32[128,2048]{1,0:T(8,128)S(1)}, f32[128,2048]{1,0:T(8,128)S(1)}, f32[128,128]{1,0:T(8,128)S(1)}, f32[128,128]{1,0:T(8,128)S(1)}) custom-call(bf16[128,2048]{1,0:T(8,128)(2,1)S(1)} %get-tuple-element.35.x_ref, bf16[128,2048]{1,0:T(8,128)(2,1)S(1)} %get-tuple-element.36.g_ref, bf16[128,128]{1,0:T(8,128)(2,1)S(1)} %get-tuple-element.37.b_ref, ...), custom_call_target="tpu_custom_call" | custom-call | flops 1000000000 | bytes 3538944 | tf_op jit(solution)/shard_map/pallas_call | solution.py:257
  52.4 2.1 %shard_map.147 = (bf16[128,1024]{1,0:T(8,128)(2,1)S(1)}, bf16[128,1024]{1,0:T(8,128)(2,1)S(1)}, f32[128,128]{1,0:T(8,128)S(1)}, f32[128,128]{1,0:T(8,128)S(1)}, ...) custom-call(s32[1]{0:T(128)} %bitcast.c_ref, bf16[128,2048]{1,0:T(8,128)(2,1)S(1)} %get-tuple-element.35.x_ref, ...), custom_call_target="tpu_custom_call" | custom-call | flops 1000000000 | bytes 5151492 | tf_op jit(solution)/shard_map/pallas_call | solution.py:257
  54.6 3.3 %shard_map.148 = (bf16[128,2048]{1,0:T(8,128)(2,1)}, bf16[128,2048]{1,0:T(8,128)(2,1)}, f32[128,128]{1,0:T(8,128)}, f32[128,128]{1,0:T(8,128)}, f32[64,128]{1,0:T(8,128)}, /*index=5*/f32[64,128]{1,0:T(8,128)S(1)}) custom-call(s32[1]{0:T(128)} %bitcast.c_ref, bf16[128,2048]{1,0:T(8,128)(2,1)S(1)} %get-tuple-element.35.x_ref, ...), custom_call_target="tpu_custom_call" | custom-call | flops 1000000000 | bytes 6265604 | tf_op jit(solution)/shard_map/pallas_call | solution.py:257
  58.3 0.9 %collective-permute-done.10 = f32[64,3]{1,0:T(8,128)S(1)} collective-permute-done((f32[64,3]{1,0:T(8,128)S(1)}, f32[64,3]{1,0:T(8,128)S(1)}, u32[]{:S(2)}, u32[]{:S(2)}) %collective-permute-start.10) | collective-permute-done | bytes 800 | tf_op jit(solution)/shard_map/ppermute | solution.py:269
  59.2 1.8 %collective-permute-start.11 = (f32[64,3]{1,0:T(8,128)S(1)}, f32[64,3]{1,0:T(8,128)S(1)}, u32[]{:S(2)}, u32[]{:S(2)}) collective-permute-start(f32[64,3]{1,0:T(8,128)S(1)} %slice_add_fusion.1), channel_id=1, source_target_pairs={{0,2},{1,3},{2,0},{3,1},{4,6},{5,7},{6,4},{7,5},{8,10},{9,11},{10,... | collective-permute-start | bytes 2312 | tf_op jit(solution)/shard_map/ppermute | solution.py:269
  61.0 2.2 %collective-permute-done.11 = f32[64,3]{1,0:T(8,128)S(1)} collective-permute-done((f32[64,3]{1,0:T(8,128)S(1)}, f32[64,3]{1,0:T(8,128)S(1)}, u32[]{:S(2)}, u32[]{:S(2)}) %collective-permute-start.11) | collective-permute-done | bytes 800 | tf_op jit(solution)/shard_map/ppermute | solution.py:269
  63.1 1.8 %collective-permute-start.12 = (f32[64,3]{1,0:T(8,128)S(1)}, f32[64,3]{1,0:T(8,128)S(1)}, u32[]{:S(2)}, u32[]{:S(2)}) collective-permute-start(f32[64,3]{1,0:T(8,128)S(1)} %add.68), channel_id=1, source_target_pairs={{0,4},{1,5},{2,6},{3,7},{4,0},{5,1},{6,2},{7,3},{8,12},{9,13},{10,... | collective-permute-start | bytes 2312 | tf_op jit(solution)/shard_map/ppermute | solution.py:269
  64.9 2.1 %collective-permute-done.12 = f32[64,3]{1,0:T(8,128)S(1)} collective-permute-done((f32[64,3]{1,0:T(8,128)S(1)}, f32[64,3]{1,0:T(8,128)S(1)}, u32[]{:S(2)}, u32[]{:S(2)}) %collective-permute-start.12) | collective-permute-done | bytes 800 | tf_op jit(solution)/shard_map/ppermute | solution.py:269
  67.1 2.9 %collective-permute-start.13 = (f32[32,3]{1,0:T(8,128)S(1)}, f32[32,3]{1,0:T(8,128)S(1)}, u32[]{:S(2)}, u32[]{:S(2)}) collective-permute-start(f32[32,3]{1,0:T(8,128)S(1)} %slice_select_fusion.1), channel_id=1, source_target_pairs={{0,16},{8,24},{16,0},{24,8},{1,17},{9,25},{17,1},{25,9},{2,18},{10... | collective-permute-start | bytes 1160 | tf_op jit(solution)/shard_map/ppermute | solution.py:269
  70.0 1.8 %collective-permute-done.13 = f32[32,3]{1,0:T(8,128)S(1)} collective-permute-done((f32[32,3]{1,0:T(8,128)S(1)}, f32[32,3]{1,0:T(8,128)S(1)}, u32[]{:S(2)}, u32[]{:S(2)}) %collective-permute-start.13) | collective-permute-done | bytes 416 | tf_op jit(solution)/shard_map/ppermute | solution.py:269
  71.8 1.8 %collective-permute-start.14 = (f32[16,3]{1,0:T(8,128)S(1)}, f32[16,3]{1,0:T(8,128)S(1)}, u32[]{:S(2)}, u32[]{:S(2)}) collective-permute-start(f32[16,3]{1,0:T(8,128)S(1)} %slice_select_fusion.2), channel_id=1, source_target_pairs={{0,8},{8,0},{16,24},{24,16},{1,9},{9,1},{17,25},{25,17},{2,10},{10... | collective-permute-start | bytes 584 | tf_op jit(solution)/shard_map/ppermute | solution.py:269
  73.7 1.9 %collective-permute-done.14 = f32[16,3]{1,0:T(8,128)S(1)} collective-permute-done((f32[16,3]{1,0:T(8,128)S(1)}, f32[16,3]{1,0:T(8,128)S(1)}, u32[]{:S(2)}, u32[]{:S(2)}) %collective-permute-start.14) | collective-permute-done | bytes 224 | tf_op jit(solution)/shard_map/ppermute | solution.py:269
  (44 shorter events, 4.2 us)
Async XLA Ops:
  1.4 4.7 %collective-permute-start = (f32[16,3]{1,0:T(8,128)S(1)}, f32[16,3]{1,0:T(8,128)S(1)}, u32[]{:S(2)}, u32[]{:S(2)}) collective-permute-start(f32[16,3]{1,0:T(8,128)S(1)} %copy.36), channel_id=1, source_target_pairs={{0,8},{8,0},{16,24},{24,16},{1,9},{9,1},{17,25},{25,17},{2,10},{10... | collective-permute-start | bytes 584 | tf_op jit(solution)/shard_map/ppermute | solution.py:269
  6.1 4.8 %collective-permute-start.1 = (f32[32,3]{1,0:T(8,128)S(1)}, f32[32,3]{1,0:T(8,128)S(1)}, u32[]{:S(2)}, u32[]{:S(2)}) collective-permute-start(f32[32,3]{1,0:T(8,128)S(1)} %pad_maximum_fusion.7), channel_id=1, source_target_pairs={{0,16},{8,24},{16,0},{24,8},{1,17},{9,25},{17,1},{25,9},{2,18},{10... | collective-permute-start | bytes 1160 | tf_op jit(solution)/shard_map/ppermute | solution.py:269
  12.8 3.0 %collective-permute-start.2 = (f32[2,2,136,512]{3,2,1,0:T(8,128)S(1)}, f32[2,2,136,512]{3,2,1,0:T(8,128)}, u32[]{:S(2)}, u32[]{:S(2)}) collective-permute-start(f32[2,2,136,512]{3,2,1,0:T(8,128)S(1)} %get-tuple-element.48), channel_id=1, source_target_pairs={{0,1},{1,0},{2,3},{3,2},{4,5},{5,4},{6,7},{7,6},{8,9},{9,8},{10,11... | collective-permute-start | bytes 3342344 | tf_op jit(solution)/shard_map/ppermute | solution.py:269
  19.6 11.2 %collective-permute-start.3 = (f32[136,512]{1,0:T(8,128)S(1)}, f32[136,512]{1,0:T(8,128)S(1)}, u32[]{:S(2)}, u32[]{:S(2)}) collective-permute-start(f32[136,512]{1,0:T(8,128)S(1)} %get-tuple-element.72), channel_id=1, source_target_pairs={{0,2},{1,3},{2,0},{3,1},{4,6},{5,7},{6,4},{7,5},{8,10},{9,11},{10,... | collective-permute-start | bytes 835592 | tf_op jit(solution)/shard_map/ppermute | solution.py:269
  21.5 9.3 %collective-permute-start.6 = (f32[8,512]{1,0:T(8,128)S(1)}, f32[8,512]{1,0:T(8,128)S(1)}, u32[]{:S(2)}, u32[]{:S(2)}) collective-permute-start(f32[8,512]{1,0:T(8,128)S(1)} %slice_bitcast_fusion.6), channel_id=1, source_target_pairs={{0,6},{1,7},{2,4},{3,5},{4,2},{5,3},{6,0},{7,1},{8,14},{9,15},{10,... | collective-permute-start | bytes 49160 | tf_op jit(solution)/shard_map/ppermute | solution.py:269
  23.0 12.5 %collective-permute-start.5 = (f32[136,512]{1,0:T(8,128)S(1)}, f32[136,512]{1,0:T(8,128)S(1)}, u32[]{:S(2)}, u32[]{:S(2)}) collective-permute-start(f32[136,512]{1,0:T(8,128)S(1)} %get-tuple-element.69), channel_id=1, source_target_pairs={{0,2},{1,3},{2,0},{3,1},{4,6},{5,7},{6,4},{7,5},{8,10},{9,11},{10,... | collective-permute-start | bytes 835592 | tf_op jit(solution)/shard_map/ppermute | solution.py:269
  24.4 9.5 %collective-permute-start.7 = (f32[136,512]{1,0:T(8,128)}, f32[136,512]{1,0:T(8,128)S(1)}, u32[]{:S(2)}, u32[]{:S(2)}) collective-permute-start(f32[136,512]{1,0:T(8,128)} %get-tuple-element.71), channel_id=1, source_target_pairs={{0,4},{1,5},{2,6},{3,7},{4,0},{5,1},{6,2},{7,3},{8,12},{9,13},{10,... | collective-permute-start | bytes 835592 | tf_op jit(solution)/shard_map/ppermute | solution.py:269
  31.0 7.5 %collective-permute-start.4 = (f32[128,512]{1,0:T(8,128)S(1)}, f32[128,512]{1,0:T(8,128)S(1)}, u32[]{:S(2)}, u32[]{:S(2)}) collective-permute-start(f32[128,512]{1,0:T(8,128)S(1)} %add_select_fusion.2), channel_id=1, source_target_pairs={{0,4},{1,5},{2,6},{3,7},{4,0},{5,1},{6,2},{7,3},{8,12},{9,13},{10,... | collective-permute-start | bytes 786440 | tf_op jit(solution)/shard_map/ppermute | solution.py:269
  34.0 6.7 %collective-permute-start.8 = (f32[136,512]{1,0:T(8,128)S(1)}, f32[136,512]{1,0:T(8,128)S(1)}, u32[]{:S(2)}, u32[]{:S(2)}) collective-permute-start(f32[136,512]{1,0:T(8,128)S(1)} %pad_maximum_fusion.5), channel_id=1, source_target_pairs={{0,2},{1,3},{2,0},{3,1},{4,6},{5,7},{6,4},{7,5},{8,10},{9,11},{10,... | collective-permute-start | bytes 835592 | tf_op jit(solution)/shard_map/ppermute | solution.py:269
  43.5 11.1 %collective-permute-start.9 = (f32[2,2,128,512]{3,2,1,0:T(8,128)S(1)}, f32[2,2,128,512]{3,2,1,0:T(8,128)S(1)}, u32[]{:S(2)}, u32[]{:S(2)}) collective-permute-start(f32[2,2,128,512]{3,2,1,0:T(8,128)S(1)} %pad_maximum_fusion.1), channel_id=1, source_target_pairs={{0,1},{1,0},{2,3},{3,2},{4,5},{5,4},{6,7},{7,6},{8,9},{9,8},{10,11... | collective-permute-start | bytes 3145736 | tf_op jit(solution)/shard_map/ppermute | solution.py:269
  57.9 1.4 %collective-permute-start.10 = (f32[64,3]{1,0:T(8,128)S(1)}, f32[64,3]{1,0:T(8,128)S(1)}, u32[]{:S(2)}, u32[]{:S(2)}) collective-permute-start(f32[64,3]{1,0:T(8,128)S(1)} %bitcast.93), channel_id=1, source_target_pairs={{0,1},{1,0},{2,3},{3,2},{4,5},{5,4},{6,7},{7,6},{8,9},{9,8},{10,11... | collective-permute-start | bytes 2312 | tf_op jit(solution)/shard_map/ppermute | solution.py:269
  59.2 3.9 %collective-permute-start.11 = (f32[64,3]{1,0:T(8,128)S(1)}, f32[64,3]{1,0:T(8,128)S(1)}, u32[]{:S(2)}, u32[]{:S(2)}) collective-permute-start(f32[64,3]{1,0:T(8,128)S(1)} %slice_add_fusion.1), channel_id=1, source_target_pairs={{0,2},{1,3},{2,0},{3,1},{4,6},{5,7},{6,4},{7,5},{8,10},{9,11},{10,... | collective-permute-start | bytes 2312 | tf_op jit(solution)/shard_map/ppermute | solution.py:269
  63.1 3.9 %collective-permute-start.12 = (f32[64,3]{1,0:T(8,128)S(1)}, f32[64,3]{1,0:T(8,128)S(1)}, u32[]{:S(2)}, u32[]{:S(2)}) collective-permute-start(f32[64,3]{1,0:T(8,128)S(1)} %add.68), channel_id=1, source_target_pairs={{0,4},{1,5},{2,6},{3,7},{4,0},{5,1},{6,2},{7,3},{8,12},{9,13},{10,... | collective-permute-start | bytes 2312 | tf_op jit(solution)/shard_map/ppermute | solution.py:269
  67.1 4.8 %collective-permute-start.13 = (f32[32,3]{1,0:T(8,128)S(1)}, f32[32,3]{1,0:T(8,128)S(1)}, u32[]{:S(2)}, u32[]{:S(2)}) collective-permute-start(f32[32,3]{1,0:T(8,128)S(1)} %slice_select_fusion.1), channel_id=1, source_target_pairs={{0,16},{8,24},{16,0},{24,8},{1,17},{9,25},{17,1},{25,9},{2,18},{10... | collective-permute-start | bytes 1160 | tf_op jit(solution)/shard_map/ppermute | solution.py:269
  71.8 3.7 %collective-permute-start.14 = (f32[16,3]{1,0:T(8,128)S(1)}, f32[16,3]{1,0:T(8,128)S(1)}, u32[]{:S(2)}, u32[]{:S(2)}) collective-permute-start(f32[16,3]{1,0:T(8,128)S(1)} %slice_select_fusion.2), channel_id=1, source_target_pairs={{0,8},{8,0},{16,24},{24,16},{1,9},{9,1},{17,25},{25,17},{2,10},{10... | collective-permute-start | bytes 584 | tf_op jit(solution)/shard_map/ppermute | solution.py:269

commit v3 on v2

--- a/solution.py
+++ b/solution.py
@@ -1,3 +1,5 @@
+import functools
+
 import jax
 import jax.numpy as jnp
 from jax import lax
@@ -37,6 +39,11 @@
 def expand(per_head, hot):
     hi, lo = split(per_head)
     return mm(jnp.concatenate([hi, lo], axis=1), jnp.concatenate([hot, hot], axis=0))
+
+
+def relative(n, place, block, src_ref, dst_ref):
+    for i in range(n):
+        dst_ref[pl.ds(i * block, block), :] = src_ref[pl.ds(pl.multiple_of((place ^ i) * block, block), block), :]
 
 
 def scans(raw, par):
@@ -65,8 +72,13 @@
         copy.wait()
 
 
-def ends_kernel(c_ref, x_ref, g_ref, b_ref, r_ref, raw_ref, par_ref, own_ref, oth_ref, cum_ref, step_ref):
+def ends_kernel(
+    groups, place_ref, x_ref, g_ref, b_ref, r_ref, raw_ref, got_ref, own_ref, oth_ref, cum_ref, step_ref, par_ref, mixed_ref,
+):
     heads, count = raw_ref.shape
+    rows = got_ref.shape[0]
+    mixed_ref[...] = jnp.concatenate([got_ref[...], jnp.zeros((LANES - rows, heads), F32)], axis=0).T
+    relative(groups, place_ref[1], heads // groups, mixed_ref, par_ref)
     total = x_ref.shape[1]
     half = total // 2
     width = total // heads
@@ -80,7 +92,7 @@
     ct = r_ref[...].astype(F32).T.astype(BF16)
     bt2 = jnp.concatenate([bt, bt], axis=1)
     ct2 = jnp.concatenate([ct, ct], axis=1)
-    c = c_ref[0]
+    c = place_ref[0] & 1
     size = b_ref.shape[1]
     for which, out in ((1 - c, oth_ref), (c, own_ref)):
         for k in range(2):
@@ -103,6 +115,104 @@
     col = lax.broadcasted_iota(jnp.int32, gram_ref.shape, 1)
     gram_ref[...] = jnp.where(row >= col, mm(r, b, NT), 0.0)
     gram_t_ref[...] = jnp.where(row <= col, mm(b, r, NT), 0.0)
+
+
+def totals_kernel(place_ref, own_ref, mate_ref, xa_ref, yb_ref, late_ref, diag_ref, kept_ref):
+    place = place_ref[0]
+    odd, x1, y1 = (place & 1) != 0, (place >> 1) & 1, (place >> 2) & 1
+    size = own_ref.shape[2] - PAD
+
+    def total(way, part, first, second, out):
+        f, l = first[way, part, :size], second[way, part, :size]
+        fd, ld = first[way, part, size:], second[way, part, size:]
+        lead = jnp.broadcast_to((way == 0).astype(F32), fd[:1].shape)
+        keep = jnp.where(lead > 0.0, ld[:1], 1.0)
+        onto = jnp.where(lead > 0.0, 1.0, fd[:1])
+        out[:size] = keep * f + onto * l
+        out[size:] = fd * ld
+
+    def all_totals(first, second):
+        total(y1, 0, first, second, xa_ref)
+        total(y1, 1, first, second, yb_ref)
+        total(1 - y1, 1, first, second, kept_ref)
+
+        @pl.when(x1 != y1)
+        def _():
+            total(1 - y1, 0, first, second, late_ref)
+
+        @pl.when(x1 == y1)
+        def _():
+            late_ref[...] = yb_ref[...]
+
+        diag_ref[...] = kept_ref[size:]
+
+    @pl.when(odd)
+    def _():
+        all_totals(mate_ref, own_ref)
+
+    @pl.when(jnp.logical_not(odd))
+    def _():
+        all_totals(own_ref, mate_ref)
+
+
+def row_kernel(place_ref, sent_ref, xa_ref, row_ref):
+    place = place_ref[0]
+    x1, y1 = (place >> 1) & 1, (place >> 2) & 1
+    size = row_ref.shape[0]
+
+    @pl.when(x1 != y1)
+    def _():
+        row_ref[...] = sent_ref[:size] + sent_ref[size : size + 1] * xa_ref[:size]
+
+    @pl.when(x1 == y1)
+    def _():
+        row_ref[...] = xa_ref[:size] + xa_ref[size : size + 1] * sent_ref[:size]
+
+
+def onward_kernel(place_ref, kept_ref, diag_ref, yb_ref, xb_ref):
+    place = place_ref[0]
+    x1, y1 = (place >> 1) & 1, (place >> 2) & 1
+    size = xb_ref.shape[0] - PAD
+
+    @pl.when(x1 != y1)
+    def _():
+        xb_ref[:size] = kept_ref[:size] + kept_ref[size : size + 1] * diag_ref[:1] * yb_ref[:size]
+        xb_ref[size:] = kept_ref[size:]
+
+    @pl.when(x1 == y1)
+    def _():
+        xb_ref[...] = yb_ref[...]
+
+
+def reach_kernel(place_ref, own_ref, mate_ref, xa_ref, yb_ref, late_ref, ya_ref, xb_ref, mine_ref, rest_ref):
+    place = place_ref[0]
+    odd, x1, y1 = (place & 1) != 0, (place >> 1) & 1, (place >> 2) & 1
+    size = ya_ref.shape[0]
+
+    def spread_to(first, second, to_first, to_second):
+        for part in range(2):
+            if part == 0:
+                bent_far, near = ya_ref[...], xa_ref
+                flat_far = late_ref[:size] + late_ref[size : size + 1] * ya_ref[...]
+                far = jnp.where(jnp.broadcast_to(x1 != y1, flat_far.shape), bent_far, flat_far)
+            else:
+                near = late_ref
+                far = xb_ref[:size] + xb_ref[size : size + 1] * yb_ref[:size]
+            near = jnp.where(jnp.broadcast_to(x1 != y1, far.shape), near[:size], 0.0)
+            forward = jnp.broadcast_to(y1 == 1, far.shape)
+            ahead, behind = jnp.where(forward, far, near), jnp.where(forward, near, far)
+            to_first[0, part] = ahead
+            to_second[0, part] = first[0, part, size : size + 1] * ahead + first[0, part, :size]
+            to_second[1, part] = behind
+            to_first[1, part] = second[1, part, size : size + 1] * behind + second[1, part, :size]
+
+    @pl.when(odd)
+    def _():
+        spread_to(mate_ref, own_ref, rest_ref, mine_ref)
+
+    @pl.when(jnp.logical_not(odd))
+    def _():
+        spread_to(own_ref, mate_ref, mine_ref, rest_ref)
 
 
 def inside_kernel(x_ref, g_ref, b_ref, r_ref, cum_ref, step_ref, gram_ref, gram_t_ref, inner_ref, dxin_ref, db_ref, dc_ref, cumt_ref, dgram_ref):
@@ -161,75 +271,81 @@
     db_ref[...] = mm(jnp.concatenate([hi, lo], axis=1), jnp.concatenate([r, r], axis=0))
 
 
-def carried(which, src, x_ref, g_ref, b_ref, r_ref, raw, par, inner_ref, dxin_ref, db, dc, uv, sums, y_ref, dx_ref, offset):
+def lanes_of(heads, total, which):
+    half = total // 2
+    part = half // 2
+    for k in range(2):
+        first = pl.multiple_of(which * half + k * part, part)
+        yield k, pl.ds(first, part), pl.ds(k * part, part), spread(heads, total // heads, first, part)
+
+
+def carried(which, src, x_ref, g_ref, b_ref, r_ref, raw, par, inner_ref, dxin_ref, uv, sums, y_ref, dx_ref):
     heads, _ = raw.shape
-    total = x_ref.shape[1]
-    half = total // 2
-    width = total // heads
-    part = half // 2
-    z, step, scale, logdecay, cum, upper = scans(raw, par)
+    scanned = scans(raw, par)
+    _, step, _, _, cum, _ = scanned
     tail = (jnp.exp(cum[:, -1:] - cum) * step).T
     grow = jnp.exp(cum).T
     skip = jnp.broadcast_to(par[:, 2:3], (heads, LANES)).T[:PAD]
     b, r = b_ref[...], r_ref[...]
     b2 = jnp.concatenate([b, b], axis=1)
     r2 = jnp.concatenate([r, r], axis=1)
-    for k in range(2):
-        first = pl.multiple_of(which * half + k * part, part)
-        hot = spread(heads, width, first, part)
-        here = pl.ds(first, part)
-        out = pl.ds(pl.multiple_of(offset + k * part, part), part)
+    for k, here, out, hot in lanes_of(heads, x_ref.shape[1], which):
         x = x_ref[:, here].astype(F32)
         g = g_ref[:, here].astype(F32)
         grow_x, tail_x, skip_x = expand(grow, hot), expand(tail, hot), expand(skip, hot)[0:1]
         before, later = src[0, k], src[1, k]
-        h_hi, h_lo = split(before)
-        d_hi, d_lo = split(later)
-        flow = inner_ref[:, here] + grow_x * mm(r2, jnp.concatenate([h_hi, h_lo], axis=0))
+        flow = inner_ref[:, here] + grow_x * mm(r2, jnp.concatenate(split(before), axis=0))
         y_ref[:, out] = (flow + skip_x * x).astype(BF16)
-        reach = tail_x * mm(b2, jnp.concatenate([d_hi, d_lo], axis=0))
+        reach = tail_x * mm(b2, jnp.concatenate(split(later), axis=0))
         back = dxin_ref[:, here] + reach
         dx_ref[:, out] = (back + skip_x * g).astype(BF16)
         uv_hi, uv_lo = split(jnp.concatenate([g * flow, x * back], axis=0))
         uv = uv + mm(uv_hi, hot, NT) + mm(uv_lo, hot, NT)
         parts = jnp.concatenate(
-            [jnp.sum(v.reshape(-1, PAD, part), axis=0) for v in (x * reach, before * later, g * x)], axis=0
+            [jnp.sum(v.reshape(-1, PAD, v.shape[1]), axis=0) for v in (x * reach, before * later, g * x)], axis=0
         )
         s_hi, s_lo = split(parts)
         sums = sums + mm(s_hi, hot, NT) + mm(s_lo, hot, NT)
-        e_hi, e_lo = split(grow_x * g)
+    return uv, sums, scanned
+
+
+def projected(which, src, x_ref, g_ref, cum, step, db, dc):
+    tail = (jnp.exp(cum[:, -1:] - cum) * step).T
+    grow = jnp.exp(cum).T
+    for k, here, _, hot in lanes_of(cum.shape[0], x_ref.shape[1], which):
+        h_hi, h_lo = split(src[0, k])
+        d_hi, d_lo = split(src[1, k])
+        e_hi, e_lo = split(expand(grow, hot) * g_ref[:, here].astype(F32))
         dc = dc + mm(e_hi, h_hi, NT) + mm(e_hi, h_lo, NT) + mm(e_lo, h_hi, NT)
-        t_hi, t_lo = split(tail_x * x)
+        t_hi, t_lo = split(expand(tail, hot) * x_ref[:, here].astype(F32))
         db = db + mm(t_hi, d_hi, NT) + mm(t_hi, d_lo, NT) + mm(t_lo, d_hi, NT)
-    return db, dc, uv, sums, (z, step, scale, logdecay, cum, upper)
+    return db, dc
 
 
 def first_kernel(
-    c_ref, x_ref, g_ref, b_ref, r_ref, raw_ref, par_ref, inner_ref, dxin_ref, db0_ref, dc0_ref, src_ref,
-    y_ref, dx_ref, db_ref, dc_ref, uv_ref, sums_ref,
+    place_ref, x_ref, g_ref, b_ref, r_ref, raw_ref, par_ref, inner_ref, dxin_ref, src_ref, cum_ref, step_ref,
+    db0_ref, dc0_ref, y_ref, dx_ref, uv_ref, sums_ref, db_ref, dc_ref,
 ):
+    c = place_ref[0] & 1
     uv, sums = jnp.zeros(uv_ref.shape, F32), jnp.zeros(sums_ref.shape, F32)
-    db_ref[...], dc_ref[...], uv_ref[...], sums_ref[...], _ = carried(
-        c_ref[0], src_ref, x_ref, g_ref, b_ref, r_ref, raw_ref[...], par_ref[...], inner_ref, dxin_ref,
-        db0_ref[...], dc0_ref[...], uv, sums, y_ref, dx_ref, 0,
+    uv_ref[...], sums_ref[...], _ = carried(
+        c, src_ref, x_ref, g_ref, b_ref, r_ref, raw_ref[...], par_ref[...], inner_ref, dxin_ref, uv, sums, y_ref, dx_ref
+    )
+    db_ref[...], dc_ref[...] = projected(
+        c, src_ref, x_ref, g_ref, cum_ref[...], step_ref[...], db0_ref[...], dc0_ref[...]
     )
 
 
 def second_kernel(
-    c_ref, x_ref, g_ref, b_ref, r_ref, raw_ref, par_ref, inner_ref, dxin_ref, db0_ref, dc0_ref, src_ref,
-    y0_ref, dx0_ref, uv0_ref, sums0_ref, y_ref, dx_ref, db_ref, dc_ref, draw_ref, tot_ref,
+    groups, place_ref, x_ref, g_ref, b_ref, r_ref, raw_ref, par_ref, inner_ref, dxin_ref, src_ref,
+    uv0_ref, sums0_ref, y_ref, dx_ref, draw_ref, tot_ref, col_ref, rel_ref,
 ):
     heads, count = raw_ref.shape
-    half = x_ref.shape[1] // 2
-    c = c_ref[0]
-    other = (1 - c) * half
-    db_ref[...], dc_ref[...], uv, sums, (z, step, scale, logdecay, cum, upper) = carried(
-        1 - c, src_ref, x_ref, g_ref, b_ref, r_ref, raw_ref[...], par_ref[...], inner_ref, dxin_ref,
-        db0_ref[...], dc0_ref[...], uv0_ref[...], sums0_ref[...], y_ref, dx_ref, other,
-    )
-    mine = pl.ds(pl.multiple_of(c * half, half), half)
-    y_ref[:, mine] = y0_ref[...]
-    dx_ref[:, mine] = dx0_ref[...]
+    other = 1 - (place_ref[0] & 1)
+    uv, sums, (z, step, scale, logdecay, cum, upper) = carried(
+        other, src_ref, x_ref, g_ref, b_ref, r_ref, raw_ref[...], par_ref[...], inner_ref, dxin_ref,
+        uv0_ref[...], sums0_ref[...], y_ref, dx_ref,
+    )
     u = uv[:count].T
     v = uv[count:].T
     sums_t = sums.T
@@ -243,7 +359,24 @@
     column = lax.broadcasted_iota(jnp.int32, (heads, LANES), 1)
     rate_sum = jnp.sum(dlog * logdecay, axis=1, keepdims=True)
     bias_sum = jnp.sum(draw, axis=1, keepdims=True)
-    tot_ref[...] = jnp.where(column == 0, rate_sum, jnp.where(column == 1, bias_sum, jnp.where(column == 2, skip_sum, 0.0)))
+    col_ref[...] = jnp.where(column == 0, rate_sum, jnp.where(column == 1, bias_sum, jnp.where(column == 2, skip_sum, 0.0)))
+    relative(groups, place_ref[1], heads // groups, col_ref, rel_ref)
+    tot_ref[...] = rel_ref[...].T[:PAD]
+
+
+def third_kernel(
+    place_ref, x_ref, g_ref, cum_ref, step_ref, src_ref, db0_ref, dc0_ref, y0_ref, dx0_ref, y1_ref, dx1_ref,
+    y_ref, dx_ref, db_ref, dc_ref,
+):
+    c = place_ref[0] & 1
+    half = x_ref.shape[1] // 2
+    for which, ys, dxs in ((c, y0_ref, dx0_ref), (1 - c, y1_ref, dx1_ref)):
+        at = pl.ds(pl.multiple_of(which * half, half), half)
+        y_ref[:, at] = ys[...]
+        dx_ref[:, at] = dxs[...]
+    db_ref[...], dc_ref[...] = projected(
+        1 - c, src_ref, x_ref, g_ref, cum_ref[...], step_ref[...], db0_ref[...], dc0_ref[...]
+    )
 
 
 def call(kernel, outs, args, scratch=(), flops=0, scalar=False, off_chip=False):
@@ -270,21 +403,18 @@
 
 
 def gathered(value, axis):
-    place, bit = lax.axis_index(axis), 1
+    bit = 1
     while bit < lax.axis_size(axis):
-        other = swap(value, axis, bit)
-        low = (place & bit) == 0
-        value = jnp.concatenate([jnp.where(low, value, other), jnp.where(low, other, value)], axis=0)
+        value = jnp.concatenate([value, swap(value, axis, bit)], axis=1)
         bit *= 2
     return value
 
 
 def owned_sum(value, axis):
-    place, bit = lax.axis_index(axis), lax.axis_size(axis) // 2
+    bit = lax.axis_size(axis) // 2
     while bit:
-        lower, upper = jnp.split(value, 2, axis=0)
-        low = (place & bit) == 0
-        value = jnp.where(low, lower, upper) + swap(jnp.where(low, upper, lower), axis, bit)
+        mine, theirs = jnp.split(value, 2, axis=1)
+        value = mine + swap(theirs, axis, bit)
         bit //= 2
     return value
 
@@ -311,24 +441,6 @@
     def decay(v):
         return v[..., size : size + 1, :]
 
-    if planned(n):
-        x1, y1 = (place & 2) != 0, (place & 4) != 0
-        bent = x1 != y1
-        (f_a, f_b), (r_a, r_b) = total[0], total[1]
-        own_a, own_b = jnp.where(y1, r_a, f_a), jnp.where(y1, f_b, r_b)
-        xa = swap(own_a, "ctx", 2)
-        yb = swap(jnp.where(y1, r_b, f_b), "ctx", 4)
-        late = swap(jnp.where(y1, jnp.where(x1, r_b, f_a), jnp.where(x1, r_a, f_b)), "ctx", 2)
-        diag = swap(f_b[size:], "ctx", 6)
-        first, second = jnp.where(x1, xa, own_a), jnp.where(x1, own_a, xa)
-        row = jnp.where(y1, state(first) + decay(first) * state(second), state(second) + decay(second) * state(first))
-        ya = swap(row, "ctx", 4)
-        both = state(own_b) + decay(own_b) * diag[:1] * state(yb)
-        onward = jnp.concatenate([jnp.where(bent, both, state(yb)), jnp.where(bent, own_b[size:], yb[size:])], axis=0)
-        xb = swap(onward, "ctx", 2)
-        far = jnp.stack([jnp.where(bent, ya, state(late) + decay(late) * ya), state(xb) + decay(xb) * state(yb)])
-        near = jnp.where(bent, jnp.stack([state(xa), state(late)]), 0.0)
-        return jnp.where(y1, far, near), jnp.where(y1, near, far)
     fwd, bwd = total[0], total[1]
     ahead = behind = jnp.zeros_like(state(fwd))
     ahead_decay = behind_decay = jnp.ones_like(decay(fwd))
@@ -353,30 +465,8 @@
     return layer(x[0], b[0], r[0], raw[0], rate, bias, skip, g[0])
 
 
-def layer(x, b, r, raw, rate, bias, skip, g):
-    heads, count = raw.shape
-    total, size = x.shape[1], b.shape[1]
-    half = total // 2
-    part = half // 2
-    shape = jax.ShapeDtypeStruct
-    par = gathered(jnp.stack([rate, bias, skip], axis=1), "dp")
-    core = lax.axis_index("ctx") & 1
-    odd = core == 1
-    c = core.astype(jnp.int32).reshape(1)
-    message = shape((2, 2, size + PAD, part), F32)
-    small = shape((heads, count), F32)
-    wide = shape((count, total), F32)
-    square = shape((count, size), F32)
-    mixed = shape((count, count), F32)
-    args = (x, g, b, r, raw)
-    x, g, b, r, raw = call(
-        prep_kernel, tuple(shape(v.shape, v.dtype) for v in args), args,
-        scratch=[pltpu.SemaphoreType.DMA((len(args),))], off_chip=True,
-    )
-    own, oth, cum, step = call(
-        ends_kernel, (message, message, small, small), (c, x, g, b, r, raw, par), flops=10**9, scalar=True
-    )
-    mate = swap(oth, "ctx", 1)
+def spread_generally(own, mate, size):
+    odd = (lax.axis_index("ctx") & 1) == 1
     s_o, g_o, a_o = own[0, :, :size], own[1, :, :size], own[0, :, size:]
     s_p, g_p, a_p = mate[0, :, :size], mate[1, :, :size], mate[0, :, size:]
     fwd = jnp.where(odd, a_o[:, :1] * s_p + s_o, a_p[:, :1] * s_o + s_p)
@@ -384,6 +474,62 @@
     decay = a_o * a_p
     chip = jnp.stack([jnp.concatenate([fwd, decay], axis=1), jnp.concatenate([bwd, decay], axis=1)])
     ahead, behind = chip_carries(chip, size)
+    through = jnp.where(odd, a_p[:, :1], a_o[:, :1]) * ahead + jnp.where(odd, s_p, s_o)
+    theirs = jnp.stack([jnp.where(odd, ahead, through), jnp.where(odd, g_o + a_o[:, :1] * behind, behind)])
+    mine = jnp.stack([jnp.where(odd, through, ahead), jnp.where(odd, behind, g_p + a_p[:, :1] * behind)])
+    return mine, theirs
+
+
+def spread_planned(place, own, mate, size):
+    part = own.shape[-1]
+    message = jax.ShapeDtypeStruct((size + PAD, part), F32)
+    row = jax.ShapeDtypeStruct((size, part), F32)
+    ends = jax.ShapeDtypeStruct((PAD, part), F32)
+    both = jax.ShapeDtypeStruct((2, 2, size, part), F32)
+    to_xa, to_yb, to_late, to_diag, kept = call(
+        totals_kernel, (message, message, message, ends, message), (place, own, mate), scalar=True
+    )
+    diag = swap(to_diag, "ctx", 6)
+    xa = swap(to_xa, "ctx", 2)
+    yb = swap(to_yb, "ctx", 4)
+    late = swap(to_late, "ctx", 2)
+    (to_ya,) = call(row_kernel, (row,), (place, to_xa, xa), scalar=True)
+    ya = swap(to_ya, "ctx", 4)
+    (to_xb,) = call(onward_kernel, (message,), (place, kept, diag, yb), scalar=True)
+    xb = swap(to_xb, "ctx", 2)
+    return call(reach_kernel, (both, both), (place, own, mate, xa, yb, late, ya, xb), scalar=True)
+
+
+def layer(x, b, r, raw, rate, bias, skip, g):
+    heads, count = raw.shape
+    total, size = x.shape[1], b.shape[1]
+    half = total // 2
+    part = half // 2
+    groups = lax.axis_size("dp")
+    shape = jax.ShapeDtypeStruct
+    place = jnp.stack([lax.axis_index("ctx"), lax.axis_index("dp")]).astype(jnp.int32)
+    got = gathered(jnp.stack([rate, bias, skip]), "dp")
+    message = shape((2, 2, size + PAD, part), F32)
+    small = shape((heads, count), F32)
+    wide = shape((count, total), F32)
+    square = shape((count, size), F32)
+    mixed = shape((count, count), F32)
+    columns = shape((heads, LANES), F32)
+    args = (x, g, b, r, raw)
+    x, g, b, r, raw = call(
+        prep_kernel, tuple(shape(v.shape, v.dtype) for v in args), args,
+        scratch=[pltpu.SemaphoreType.DMA((len(args),))], off_chip=True,
+    )
+    own, oth, cum, step, par = call(
+        functools.partial(ends_kernel, groups),
+        (message, message, small, small, columns), (place, x, g, b, r, raw, got),
+        scratch=[pltpu.VMEM((heads, LANES), F32)], flops=10**9, scalar=True,
+    )
+    mate = swap(oth, "ctx", 1)
+    if planned(lax.axis_size("ctx")):
+        mine, theirs = spread_planned(place, own, mate, size)
+    else:
+        mine, theirs = spread_generally(own, mate, size)
     gram, gram_t = call(gram_kernel, (mixed, mixed), (b, r), flops=10**7)
     inner, dxin, db0, dc0 = call(
         inside_kernel,
@@ -392,24 +538,26 @@
         scratch=[pltpu.VMEM((count, LANES), F32), pltpu.VMEM((count, count), F32)],
         flops=10**9,
     )
-    through = jnp.where(odd, a_p[:, :1], a_o[:, :1]) * ahead + jnp.where(odd, s_p, s_o)
-    theirs = jnp.where(odd, ahead, through), jnp.where(odd, g_o + a_o[:, :1] * behind, behind)
-    rest = swap(jnp.stack(theirs), "ctx", 1)
-    mine = jnp.stack([jnp.where(odd, through, ahead), jnp.where(odd, behind, g_p + a_p[:, :1] * behind)])
-    ready = (c, x, g, b, r, raw, par, inner, dxin)
+    rest = swap(theirs, "ctx", 1)
+    ready = (place, x, g, b, r, raw, par, inner, dxin)
     halved = shape((count, half), BF16)
     whole = shape((count, total), BF16)
-    y0, dx0, db1, dc1, uv, sums = call(
+    y0, dx0, uv, sums, db1, dc1 = call(
         first_kernel,
-        (halved, halved, square, square, shape((2 * count, heads), F32), shape((3 * PAD, heads), F32)),
-        (*ready, db0, dc0, mine), flops=10**9, scalar=True,
-    )
-    y, dx, db, dc, draw, tot = call(
-        second_kernel, (whole, whole, square, square, small, shape((heads, LANES), F32)),
-        (*ready, db1, dc1, rest, y0, dx0, uv, sums), flops=10**9, scalar=True,
-    )
-    owned = owned_sum(total_sum(tot[:, :3], "ctx"), "dp")
-    return (y[None], dx[None], db[None], dc[None], draw[None], owned[:, 0], owned[:, 1], owned[:, 2])
+        (halved, halved, shape((2 * count, heads), F32), shape((3 * PAD, heads), F32), square, square),
+        (*ready, mine, cum, step, db0, dc0), flops=10**9, scalar=True,
+    )
+    y1, dx1, draw, tot = call(
+        functools.partial(second_kernel, groups), (halved, halved, small, shape((PAD, heads), F32)),
+        (*ready, rest, uv, sums),
+        scratch=[pltpu.VMEM((heads, LANES), F32), pltpu.VMEM((heads, LANES), F32)], flops=10**9, scalar=True,
+    )
+    owned = owned_sum(total_sum(tot, "ctx"), "dp")
+    y, dx, db, dc = call(
+        third_kernel, (whole, whole, square, square),
+        (place, x, g, cum, step, rest, db1, dc1, y0, dx0, y1, dx1), flops=10**9, scalar=True,
+    )
+    return (y[None], dx[None], db[None], dc[None], draw[None], owned[0], owned[1], owned[2])
 
 
 def solution(mesh):

time: 76.7 us -> 73.9 us (0.963)
  Pallas kernels: 17.3 us -> 23.7 us
  other arithmetic: 6.91 us -> 1.66 us
  waiting for transfers between devices: 28.9 us -> 25.2 us
  starting transfers between devices: 20.7 us -> 21.7 us
  local copies, waits for them, and re-layouts: 1.62 us -> 0.69 us
    pallas_call x6 -> x11, Pallas kernels: 17.3 us -> 23.7 us  [call(): pl.pallas_call(kernel, out_shape=outs, in_specs=specs, out_specs=tuple([v...]
    select_n x13 -> x0, other arithmetic: 5.12 us -> none  [the longest x1 1.45 us: layer(): fwd = jnp.where(odd, a_o[:, :1] * s_p + s_o, a_p[:, :1] * s_o + s_p)]
    ppermute x15, waiting for transfers between devices: 28.9 us -> 25.2 us  [swap(): lax.ppermute(value, axis, [(i, i ^ bit) for i in range(lax.axis_size(axis...]
    ppermute x15, starting transfers between devices: 20.7 us -> 21.7 us  [swap(): lax.ppermute(value, axis, [(i, i ^ bit) for i in range(lax.axis_size(axis...]
    concatenate x3 -> x2, other arithmetic: 0.04 us -> 0.84 us  [gathered(): value = jnp.concatenate([value, swap(value, axis, bit)], axis=1)]
    mul x2 -> x0, other arithmetic: 0.77 us -> none  [the longest x1 0.77 us: layer(): decay = a_o * a_p]
  transfers between devices with their start and end apart: 15 -> 15, of which waited for: 13 -> 11; matrix products, arithmetic and copies ran while one was open for 0% -> 0% of each run, Pallas kernels for 16% -> 23%
where the time goes in v3:
time: 73.9 us; the launch traced here: 73.8 us
  waiting for transfers between devices  25.2 us (34%)
  Pallas kernels  23.7 us (32%)
  starting transfers between devices  21.7 us (29%)
  other arithmetic  1.66 us (2%)
  between operations  0.76 us (1%)
    ppermute x15, waiting for transfers between devices, swap(): lax.ppermute(value, axis, [(i, i ^ bit) for i in range(lax.axis_size(axis...  25.2 us
    pallas_call x11, Pallas kernels, call(): pl.pallas_call(kernel, out_shape=outs, in_specs=specs, out_specs=tuple([v...  23.7 us
    ppermute x15, starting transfers between devices, swap(): lax.ppermute(value, axis, [(i, i ^ bit) for i in range(lax.axis_size(axis...  21.7 us
  transfers between devices with their start and end apart: 15, of which 11 were waited for; matrix products, arithmetic and copies ran while one was open for 0% of the time, Pallas kernels for 23%

profile of v3, /device:TPU:0, one launch (start us, length us, event | category | flops | bytes accessed | tf_op | source)
XLA Modules:
  0.0 73.8 jit_solution(914129487703825743)
XLA Ops:
  0.7 0.7 pad_maximum_fusion
  1.4 3.1 %collective-permute-start = (f32[3,16]{1,0:T(4,128)S(1)}, f32[3,16]{1,0:T(4,128)S(1)}, u32[]{:S(2)}, u32[]{:S(2)}) collective-permute-start(f32[3,16]{1,0:T(4,128)S(1)} %pad_maximum_fusion), channel_id=1, source_target_pairs={{0,8},{8,0},{16,24},{24,16},{1,9},{9,1},{17,25},{25,17},{2,10},{10... | collective-permute-start | bytes 584 | tf_op jit(solution)/shard_map/ppermute | solution.py:402
  4.6 1.5 %collective-permute-done = f32[3,16]{1,0:T(4,128)S(1)} collective-permute-done((f32[3,16]{1,0:T(4,128)S(1)}, f32[3,16]{1,0:T(4,128)S(1)}, u32[]{:S(2)}, u32[]{:S(2)}) %collective-permute-start) | collective-permute-done | bytes 224 | tf_op jit(solution)/shard_map/ppermute | solution.py:402
  6.1 0.8 %pad_maximum_fusion.1 = f32[3,32]{1,0:T(4,128)S(1)} fusion(f32[3,16]{1,0:T(4,128)S(1)} %collective-permute-done, f32[1,16]{1,0:T(1,128)} %bitcast.27, f32[1,16]{1,0:T(1,128)} %bitcast.30, f32[1,16]{1,0:T(1,128)} %bitcast.33), kind=kLoop, calls=%fused_computation.3 | loop fusion | flops 288 | bytes 768 | tf_op jit(solution)/shard_map/concatenate | solution.py:408
  6.8 3.0 %collective-permute-start.1 = (f32[3,32]{1,0:T(4,128)S(1)}, f32[3,32]{1,0:T(4,128)S(1)}, u32[]{:S(2)}, u32[]{:S(2)}) collective-permute-start(f32[3,32]{1,0:T(4,128)S(1)} %pad_maximum_fusion.1), channel_id=1, source_target_pairs={{0,16},{8,24},{16,0},{24,8},{1,17},{9,25},{17,1},{25,9},{2,18},{10... | collective-permute-start | bytes 1160 | tf_op jit(solution)/shard_map/ppermute | solution.py:402
  9.9 1.2 %shard_map.143 = (bf16[128,2048]{1,0:T(8,128)(2,1)S(1)}, bf16[128,2048]{1,0:T(8,128)(2,1)S(1)}, bf16[128,128]{1,0:T(8,128)(2,1)S(1)}, bf16[128,128]{1,0:T(8,128)(2,1)S(1)}, f32[64,128]{1,0:T(8,128)S(1)}) custom-call(bf16[128,2048]{1,0:T(8,128)(2,1)} %bitcast.21, bf16[128,2048]{1,0:T(8,128)(2,1)} %bitcast.22, bf16[128,128]{1,0:T(8,128)(2,1)} %bitcast.23, ...), custom_call_target="tpu_custom_call" | custom-call | bytes 2293760 | tf_op jit(solution)/shard_map/pallas_call | solution.py:390
  11.5 2.5 %shard_map.144 = (f32[2,2,136,512]{3,2,1,0:T(8,128)S(1)}, f32[2,2,136,512]{3,2,1,0:T(8,128)S(1)}, f32[64,128]{1,0:T(8,128)S(1)}, f32[64,128]{1,0:T(8,128)S(1)}, f32[64,128]{1,0:T(8,128)S(1)}) custom-call(s32[2]{0:T(128)S(1)} %pad_add_fusion.place_ref, bf16[128,2048]{1,0:T(8,128)(2,1)S(1)} %get-tuple-element.45.x_ref, ...), custom_call_target="tpu_custom_call" | custom-call | flops 1000000000 | bytes 3474184 | tf_op jit(solution)/shard_map/pallas_call | solution.py:390
  14.1 2.7 %collective-permute-done.2.mate_ref = f32[2,2,136,512]{3,2,1,0:T(8,128)S(1)} collective-permute-done((f32[2,2,136,512]{3,2,1,0:T(8,128)S(1)}, f32[2,2,136,512]{3,2,1,0:T(8,128)S(1)}, u32[]{:S(2)}, u32[]{:S(2)}) %collective-permute-start.2) | collective-permute-done | bytes 1114144 | tf_op jit(solution)/shard_map/ppermute | solution.py:402
  16.8 0.7 shard_map.145
  17.5 1.9 %collective-permute-start.4 = (f32[136,512]{1,0:T(8,128)S(1)}, f32[136,512]{1,0:T(8,128)S(1)}, u32[]{:S(2)}, u32[]{:S(2)}) collective-permute-start(f32[136,512]{1,0:T(8,128)S(1)} %get-tuple-element.55), channel_id=1, source_target_pairs={{0,4},{1,5},{2,6},{3,7},{4,0},{5,1},{6,2},{7,3},{8,12},{9,13},{10,... | collective-permute-start | bytes 835592 | tf_op jit(solution)/shard_map/ppermute | solution.py:402
  19.4 1.5 %collective-permute-start.3 = (f32[136,512]{1,0:T(8,128)S(1)}, f32[136,512]{1,0:T(8,128)S(1)}, u32[]{:S(2)}, u32[]{:S(2)}) collective-permute-start(f32[136,512]{1,0:T(8,128)S(1)} %get-tuple-element.54.sent_ref), channel_id=1, source_target_pairs={{0,2},{1,3},{2,0},{3,1},{4,6},{5,7},{6,4},{7,5},{8,10},{9,11},{10,... | collective-permute-start | bytes 835592 | tf_op jit(solution)/shard_map/ppermute | solution.py:402
  21.0 1.8 %collective-permute-start.5 = (f32[136,512]{1,0:T(8,128)S(1)}, f32[136,512]{1,0:T(8,128)S(1)}, u32[]{:S(2)}, u32[]{:S(2)}) collective-permute-start(f32[136,512]{1,0:T(8,128)S(1)} %get-tuple-element.56), channel_id=1, source_target_pairs={{0,2},{1,3},{2,0},{3,1},{4,6},{5,7},{6,4},{7,5},{8,10},{9,11},{10,... | collective-permute-start | bytes 835592 | tf_op jit(solution)/shard_map/ppermute | solution.py:402
  22.9 6.0 %collective-permute-done.7.diag_ref = f32[8,512]{1,0:T(8,128)S(1)} collective-permute-done((f32[8,512]{1,0:T(8,128)S(1)}, f32[8,512]{1,0:T(8,128)S(1)}, u32[]{:S(2)}, u32[]{:S(2)}) %collective-permute-start.7) | collective-permute-done | bytes 16416 | tf_op jit(solution)/shard_map/ppermute | solution.py:402
  28.9 0.6 shard_map.147
  29.5 1.9 %collective-permute-start.8 = (f32[136,512]{1,0:T(8,128)S(1)}, f32[136,512]{1,0:T(8,128)S(1)}, u32[]{:S(2)}, u32[]{:S(2)}) collective-permute-start(f32[136,512]{1,0:T(8,128)S(1)} %shard_map.147), channel_id=1, source_target_pairs={{0,2},{1,3},{2,0},{3,1},{4,6},{5,7},{6,4},{7,5},{8,10},{9,11},{10,... | collective-permute-start | bytes 835592 | tf_op jit(solution)/shard_map/ppermute | solution.py:402
  31.4 0.6 shard_map.146
  32.0 1.6 %collective-permute-start.6 = (f32[128,512]{1,0:T(8,128)S(1)}, f32[128,512]{1,0:T(8,128)S(1)}, u32[]{:S(2)}, u32[]{:S(2)}) collective-permute-start(f32[128,512]{1,0:T(8,128)S(1)} %shard_map.146), channel_id=1, source_target_pairs={{0,4},{1,5},{2,6},{3,7},{4,0},{5,1},{6,2},{7,3},{8,12},{9,13},{10,... | collective-permute-start | bytes 786440 | tf_op jit(solution)/shard_map/ppermute | solution.py:402
  33.5 1.7 %collective-permute-done.5.late_ref = f32[136,512]{1,0:T(8,128)S(1)} collective-permute-done((f32[136,512]{1,0:T(8,128)S(1)}, f32[136,512]{1,0:T(8,128)S(1)}, u32[]{:S(2)}, u32[]{:S(2)}) %collective-permute-start.5) | collective-permute-done | bytes 278560 | tf_op jit(solution)/shard_map/ppermute | solution.py:402
  35.3 3.1 %collective-permute-done.6.ya_ref = f32[128,512]{1,0:T(8,128)S(1)} collective-permute-done((f32[128,512]{1,0:T(8,128)S(1)}, f32[128,512]{1,0:T(8,128)S(1)}, u32[]{:S(2)}, u32[]{:S(2)}) %collective-permute-start.6) | collective-permute-done | bytes 262176 | tf_op jit(solution)/shard_map/ppermute | solution.py:402
  38.4 1.7 %collective-permute-done.8.xb_ref = f32[136,512]{1,0:T(8,128)S(1)} collective-permute-done((f32[136,512]{1,0:T(8,128)S(1)}, f32[136,512]{1,0:T(8,128)S(1)}, u32[]{:S(2)}, u32[]{:S(2)}) %collective-permute-start.8) | collective-permute-done | bytes 278560 | tf_op jit(solution)/shard_map/ppermute | solution.py:402
  40.1 0.8 %shard_map.148 = (f32[2,2,128,512]{3,2,1,0:T(8,128)S(1)}, f32[2,2,128,512]{3,2,1,0:T(8,128)S(1)}) custom-call(s32[2]{0:T(128)S(1)} %pad_add_fusion.place_ref, f32[2,2,136,512]{3,2,1,0:T(8,128)S(1)} %get-tuple-element.52.own_ref, f32[2,2,136,512]{3,2,1,0:T(8,128)S(1)} %collective-permute-done.2.mate_ref, f32[136,512]{1,0:T(8,128)S(1)} %collective-permute-done.3.xa_ref, ...), custom_call_target="tpu_custom_call" | custom-call | bytes 5701640 | tf_op jit(solution)/shard_map/pallas_call | solution.py:390
  41.2 8.6 %shard_map.150 = (f32[128,2048]{1,0:T(8,128)S(1)}, f32[128,2048]{1,0:T(8,128)S(1)}, f32[128,128]{1,0:T(8,128)S(1)}, f32[128,128]{1,0:T(8,128)S(1)}) custom-call(bf16[128,2048]{1,0:T(8,128)(2,1)S(1)} %get-tuple-element.45.x_ref, bf16[128,2048]{1,0:T(8,128)(2,1)S(1)} %get-tuple-element.46.g_ref, bf16[128,128]{1,0:T(8,128)(2,1)S(1)} %get-tuple-element.47.b_ref, ...), custom_call_target="tpu_custom_call" | custom-call | flops 1000000000 | bytes 3538944 | tf_op jit(solution)/shard_map/pallas_call | solution.py:390
  49.8 2.9 %shard_map.151 = (bf16[128,1024]{1,0:T(8,128)(2,1)S(1)}, bf16[128,1024]{1,0:T(8,128)(2,1)S(1)}, f32[256,64]{1,0:T(8,128)S(1)}, f32[24,64]{1,0:T(8,128)S(1)}, f32...) custom-call(s32[2]{0:T(128)S(1)} %pad_add_fusion.place_ref, bf16[128,2048]{1,0:T(8,128)(2,1)S(1)} %get-tuple-element.45.x_ref, ...), custom_call_target="tpu_custom_call" | custom-call | flops 1000000000 | bytes 5249032 | tf_op jit(solution)/shard_map/pallas_call | solution.py:390
  52.8 3.2 %shard_map.152 = (bf16[128,1024]{1,0:T(8,128)(2,1)S(1)}, bf16[128,1024]{1,0:T(8,128)(2,1)S(1)}, f32[64,128]{1,0:T(8,128)}, f32[8,64]{1,0:T(8,128)S(1)}) custom-call(s32[2]{0:T(128)S(1)} %pad_add_fusion.place_ref, bf16[128,2048]{1,0:T(8,128)(2,1)S(1)} %get-tuple-element.45.x_ref, bf16[128,2048]{1,0:T(8,128)(2,1)S(1)} %get-tuple-element.46.g_ref, ...), custom_call_target="tpu_custom_call" | custom-call | flops 1000000000 | bytes 4956168 | tf_op jit(solution)/shard_map/pallas_call | solution.py:390
  56.4 0.8 %collective-permute-done.10 = f32[8,64]{1,0:T(8,128)S(1)} collective-permute-done((f32[8,64]{1,0:T(8,128)S(1)}, f32[8,64]{1,0:T(8,128)S(1)}, u32[]{:S(2)}, u32[]{:S(2)}) %collective-permute-start.10) | collective-permute-done | bytes 2080 | tf_op jit(solution)/shard_map/ppermute | solution.py:402
  57.2 1.5 %collective-permute-start.11 = (f32[8,64]{1,0:T(8,128)S(1)}, f32[8,64]{1,0:T(8,128)S(1)}, u32[]{:S(2)}, u32[]{:S(2)}) collective-permute-start(f32[8,64]{1,0:T(8,128)S(1)} %add.15), channel_id=1, source_target_pairs={{0,2},{1,3},{2,0},{3,1},{4,6},{5,7},{6,4},{7,5},{8,10},{9,11},{10,... | collective-permute-start | bytes 6152 | tf_op jit(solution)/shard_map/ppermute | solution.py:402
  58.7 2.1 %collective-permute-done.11 = f32[8,64]{1,0:T(8,128)S(1)} collective-permute-done((f32[8,64]{1,0:T(8,128)S(1)}, f32[8,64]{1,0:T(8,128)S(1)}, u32[]{:S(2)}, u32[]{:S(2)}) %collective-permute-start.11) | collective-permute-done | bytes 2080 | tf_op jit(solution)/shard_map/ppermute | solution.py:402
  61.2 3.2 %collective-permute-done.12 = f32[8,64]{1,0:T(8,128)S(1)} collective-permute-done((f32[8,64]{1,0:T(8,128)S(1)}, f32[8,64]{1,0:T(8,128)S(1)}, u32[]{:S(2)}, u32[]{:S(2)}) %collective-permute-start.12) | collective-permute-done | bytes 2080 | tf_op jit(solution)/shard_map/ppermute | solution.py:402
  64.5 2.6 %collective-permute-start.13 = (f32[8,32]{1,0:T(8,128)S(1)}, f32[8,32]{1,0:T(8,128)S(1)}, u32[]{:S(2)}, u32[]{:S(2)}) collective-permute-start(f32[8,32]{1,0:T(8,128)S(1)} %split.13), channel_id=1, source_target_pairs={{0,16},{8,24},{16,0},{24,8},{1,17},{9,25},{17,1},{25,9},{2,18},{10... | collective-permute-start | bytes 3080 | tf_op jit(solution)/shard_map/ppermute | solution.py:402
  67.1 1.9 %collective-permute-done.13 = f32[8,32]{1,0:T(8,128)S(1)} collective-permute-done((f32[8,32]{1,0:T(8,128)S(1)}, f32[8,32]{1,0:T(8,128)S(1)}, u32[]{:S(2)}, u32[]{:S(2)}) %collective-permute-start.13) | collective-permute-done | bytes 1056 | tf_op jit(solution)/shard_map/ppermute | solution.py:402
  69.1 1.6 %collective-permute-start.14 = (f32[8,16]{1,0:T(8,128)S(1)}, f32[8,16]{1,0:T(8,128)S(1)}, u32[]{:S(2)}, u32[]{:S(2)}) collective-permute-start(f32[8,16]{1,0:T(8,128)S(1)} %split.15), channel_id=1, source_target_pairs={{0,8},{8,0},{16,24},{24,16},{1,9},{9,1},{17,25},{25,17},{2,10},{10... | collective-permute-start | bytes 1544 | tf_op jit(solution)/shard_map/ppermute | solution.py:402
  70.7 2.5 %shard_map.153 = (bf16[128,2048]{1,0:T(8,128)(2,1)}, bf16[128,2048]{1,0:T(8,128)(2,1)}, f32[128,128]{1,0:T(8,128)}, f32[128,128]{1,0:T(8,128)}) custom-call(s32[2]{0:T(128)S(1)} %pad_add_fusion.place_ref, bf16[128,2048]{1,0:T(8,128)(2,1)S(1)} %get-tuple-element.45.x_ref, bf16[128,2048]{1,0:T(8,128)(2,1)S(1)} %get-tuple-element.46.g_ref, ...), custom_call_target="tpu_custom_call" | custom-call | flops 1000000000 | bytes 4521992 | tf_op jit(solution)/shard_map/pallas_call | solution.py:390
  (27 shorter events, 2.5 us)
Async XLA Ops:
  0.6 10.8 %copy-start = (f32[16]{0:T(128)S(1)}, f32[16]{0:T(128)}, u32[]{:S(2)}) copy-start(f32[16]{0:T(128)} %param.14) | copy-start | bytes 196
  0.6 10.8 %copy-start.1 = (f32[16]{0:T(128)S(1)}, f32[16]{0:T(128)}, u32[]{:S(2)}) copy-start(f32[16]{0:T(128)} %param.13) | copy-start | bytes 196
  0.7 10.8 %copy-start.2 = (f32[16]{0:T(128)S(1)}, f32[16]{0:T(128)}, u32[]{:S(2)}) copy-start(f32[16]{0:T(128)} %param.12) | copy-start | bytes 196
  1.4 4.7 %collective-permute-start = (f32[3,16]{1,0:T(4,128)S(1)}, f32[3,16]{1,0:T(4,128)S(1)}, u32[]{:S(2)}, u32[]{:S(2)}) collective-permute-start(f32[3,16]{1,0:T(4,128)S(1)} %pad_maximum_fusion), channel_id=1, source_target_pairs={{0,8},{8,0},{16,24},{24,16},{1,9},{9,1},{17,25},{25,17},{2,10},{10... | collective-permute-start | bytes 584 | tf_op jit(solution)/shard_map/ppermute | solution.py:402
  6.8 4.6 %collective-permute-start.1 = (f32[3,32]{1,0:T(4,128)S(1)}, f32[3,32]{1,0:T(4,128)S(1)}, u32[]{:S(2)}, u32[]{:S(2)}) collective-permute-start(f32[3,32]{1,0:T(4,128)S(1)} %pad_maximum_fusion.1), channel_id=1, source_target_pairs={{0,16},{8,24},{16,0},{24,8},{1,17},{9,25},{17,1},{25,9},{2,18},{10... | collective-permute-start | bytes 1160 | tf_op jit(solution)/shard_map/ppermute | solution.py:402
  14.0 2.8 %collective-permute-start.2 = (f32[2,2,136,512]{3,2,1,0:T(8,128)S(1)}, f32[2,2,136,512]{3,2,1,0:T(8,128)S(1)}, u32[]{:S(2)}, u32[]{:S(2)}) collective-permute-start(f32[2,2,136,512]{3,2,1,0:T(8,128)S(1)} %get-tuple-element.53), channel_id=1, source_target_pairs={{0,1},{1,0},{2,3},{3,2},{4,5},{5,4},{6,7},{7,6},{8,9},{9,8},{10,11... | collective-permute-start | bytes 3342344 | tf_op jit(solution)/shard_map/ppermute | solution.py:402
  17.5 11.4 %collective-permute-start.4 = (f32[136,512]{1,0:T(8,128)S(1)}, f32[136,512]{1,0:T(8,128)S(1)}, u32[]{:S(2)}, u32[]{:S(2)}) collective-permute-start(f32[136,512]{1,0:T(8,128)S(1)} %get-tuple-element.55), channel_id=1, source_target_pairs={{0,4},{1,5},{2,6},{3,7},{4,0},{5,1},{6,2},{7,3},{8,12},{9,13},{10,... | collective-permute-start | bytes 835592 | tf_op jit(solution)/shard_map/ppermute | solution.py:402
  19.4 12.0 %collective-permute-start.3 = (f32[136,512]{1,0:T(8,128)S(1)}, f32[136,512]{1,0:T(8,128)S(1)}, u32[]{:S(2)}, u32[]{:S(2)}) collective-permute-start(f32[136,512]{1,0:T(8,128)S(1)} %get-tuple-element.54.sent_ref), channel_id=1, source_target_pairs={{0,2},{1,3},{2,0},{3,1},{4,6},{5,7},{6,4},{7,5},{8,10},{9,11},{10,... | collective-permute-start | bytes 835592 | tf_op jit(solution)/shard_map/ppermute | solution.py:402
  20.9 8.0 %collective-permute-start.7 = (f32[8,512]{1,0:T(8,128)S(1)}, f32[8,512]{1,0:T(8,128)S(1)}, u32[]{:S(2)}, u32[]{:S(2)}) collective-permute-start(f32[8,512]{1,0:T(8,128)S(1)} %get-tuple-element.58), channel_id=1, source_target_pairs={{0,6},{1,7},{2,4},{3,5},{4,2},{5,3},{6,0},{7,1},{8,14},{9,15},{10,... | collective-permute-start | bytes 49160 | tf_op jit(solution)/shard_map/ppermute | solution.py:402
  21.0 14.2 %collective-permute-start.5 = (f32[136,512]{1,0:T(8,128)S(1)}, f32[136,512]{1,0:T(8,128)S(1)}, u32[]{:S(2)}, u32[]{:S(2)}) collective-permute-start(f32[136,512]{1,0:T(8,128)S(1)} %get-tuple-element.56), channel_id=1, source_target_pairs={{0,2},{1,3},{2,0},{3,1},{4,6},{5,7},{6,4},{7,5},{8,10},{9,11},{10,... | collective-permute-start | bytes 835592 | tf_op jit(solution)/shard_map/ppermute | solution.py:402
  29.5 10.7 %collective-permute-start.8 = (f32[136,512]{1,0:T(8,128)S(1)}, f32[136,512]{1,0:T(8,128)S(1)}, u32[]{:S(2)}, u32[]{:S(2)}) collective-permute-start(f32[136,512]{1,0:T(8,128)S(1)} %shard_map.147), channel_id=1, source_target_pairs={{0,2},{1,3},{2,0},{3,1},{4,6},{5,7},{6,4},{7,5},{8,10},{9,11},{10,... | collective-permute-start | bytes 835592 | tf_op jit(solution)/shard_map/ppermute | solution.py:402
  32.0 6.4 %collective-permute-start.6 = (f32[128,512]{1,0:T(8,128)S(1)}, f32[128,512]{1,0:T(8,128)S(1)}, u32[]{:S(2)}, u32[]{:S(2)}) collective-permute-start(f32[128,512]{1,0:T(8,128)S(1)} %shard_map.146), channel_id=1, source_target_pairs={{0,4},{1,5},{2,6},{3,7},{4,0},{5,1},{6,2},{7,3},{8,12},{9,13},{10,... | collective-permute-start | bytes 786440 | tf_op jit(solution)/shard_map/ppermute | solution.py:402
  40.9 11.8 %collective-permute-start.9 = (f32[2,2,128,512]{3,2,1,0:T(8,128)S(1)}, f32[2,2,128,512]{3,2,1,0:T(8,128)S(1)}, u32[]{:S(2)}, u32[]{:S(2)}) collective-permute-start(f32[2,2,128,512]{3,2,1,0:T(8,128)S(1)} %get-tuple-element.59), channel_id=1, source_target_pairs={{0,1},{1,0},{2,3},{3,2},{4,5},{5,4},{6,7},{7,6},{8,9},{9,8},{10,11... | collective-permute-start | bytes 3145736 | tf_op jit(solution)/shard_map/ppermute | solution.py:402
  55.9 1.3 %collective-permute-start.10 = (f32[8,64]{1,0:T(8,128)S(1)}, f32[8,64]{1,0:T(8,128)S(1)}, u32[]{:S(2)}, u32[]{:S(2)}) collective-permute-start(f32[8,64]{1,0:T(8,128)S(1)} %get-tuple-element.81), channel_id=1, source_target_pairs={{0,1},{1,0},{2,3},{3,2},{4,5},{5,4},{6,7},{7,6},{8,9},{9,8},{10,11... | collective-permute-start | bytes 6152 | tf_op jit(solution)/shard_map/ppermute | solution.py:402
  57.2 3.6 %collective-permute-start.11 = (f32[8,64]{1,0:T(8,128)S(1)}, f32[8,64]{1,0:T(8,128)S(1)}, u32[]{:S(2)}, u32[]{:S(2)}) collective-permute-start(f32[8,64]{1,0:T(8,128)S(1)} %add.15), channel_id=1, source_target_pairs={{0,2},{1,3},{2,0},{3,1},{4,6},{5,7},{6,4},{7,5},{8,10},{9,11},{10,... | collective-permute-start | bytes 6152 | tf_op jit(solution)/shard_map/ppermute | solution.py:402
  60.8 3.6 %collective-permute-start.12 = (f32[8,64]{1,0:T(8,128)S(1)}, f32[8,64]{1,0:T(8,128)S(1)}, u32[]{:S(2)}, u32[]{:S(2)}) collective-permute-start(f32[8,64]{1,0:T(8,128)S(1)} %add.16), channel_id=1, source_target_pairs={{0,4},{1,5},{2,6},{3,7},{4,0},{5,1},{6,2},{7,3},{8,12},{9,13},{10,... | collective-permute-start | bytes 6152 | tf_op jit(solution)/shard_map/ppermute | solution.py:402
  64.5 4.5 %collective-permute-start.13 = (f32[8,32]{1,0:T(8,128)S(1)}, f32[8,32]{1,0:T(8,128)S(1)}, u32[]{:S(2)}, u32[]{:S(2)}) collective-permute-start(f32[8,32]{1,0:T(8,128)S(1)} %split.13), channel_id=1, source_target_pairs={{0,16},{8,24},{16,0},{24,8},{1,17},{9,25},{17,1},{25,9},{2,18},{10... | collective-permute-start | bytes 3080 | tf_op jit(solution)/shard_map/ppermute | solution.py:402
  69.1 4.1 %collective-permute-start.14 = (f32[8,16]{1,0:T(8,128)S(1)}, f32[8,16]{1,0:T(8,128)S(1)}, u32[]{:S(2)}, u32[]{:S(2)}) collective-permute-start(f32[8,16]{1,0:T(8,128)S(1)} %split.15), channel_id=1, source_target_pairs={{0,8},{8,0},{16,24},{24,16},{1,9},{9,1},{17,25},{25,17},{2,10},{10... | collective-permute-start | bytes 1544 | tf_op jit(solution)/shard_map/ppermute | solution.py:402

commit v4 on v3

--- a/solution.py
+++ b/solution.py
@@ -73,12 +73,12 @@
 
 
 def ends_kernel(
-    groups, place_ref, x_ref, g_ref, b_ref, r_ref, raw_ref, got_ref, own_ref, oth_ref, cum_ref, step_ref, par_ref, mixed_ref,
+    groups, x_ref, g_ref, b_ref, r_ref, raw_ref, got_ref, own_ref, oth_ref, cum_ref, step_ref, par_ref, mixed_ref,
 ):
     heads, count = raw_ref.shape
     rows = got_ref.shape[0]
     mixed_ref[...] = jnp.concatenate([got_ref[...], jnp.zeros((LANES - rows, heads), F32)], axis=0).T
-    relative(groups, place_ref[1], heads // groups, mixed_ref, par_ref)
+    relative(groups, lax.axis_index("dp"), heads // groups, mixed_ref, par_ref)
     total = x_ref.shape[1]
     half = total // 2
     width = total // heads
@@ -92,7 +92,7 @@
     ct = r_ref[...].astype(F32).T.astype(BF16)
     bt2 = jnp.concatenate([bt, bt], axis=1)
     ct2 = jnp.concatenate([ct, ct], axis=1)
-    c = place_ref[0] & 1
+    c = lax.axis_index("ctx") & 1
     size = b_ref.shape[1]
     for which, out in ((1 - c, oth_ref), (c, own_ref)):
         for k in range(2):
@@ -109,16 +109,8 @@
             out[1, k, size:] = last
 
 
-def gram_kernel(b_ref, r_ref, gram_ref, gram_t_ref):
-    b, r = b_ref[...], r_ref[...]
-    row = lax.broadcasted_iota(jnp.int32, gram_ref.shape, 0)
-    col = lax.broadcasted_iota(jnp.int32, gram_ref.shape, 1)
-    gram_ref[...] = jnp.where(row >= col, mm(r, b, NT), 0.0)
-    gram_t_ref[...] = jnp.where(row <= col, mm(b, r, NT), 0.0)
-
-
-def totals_kernel(place_ref, own_ref, mate_ref, xa_ref, yb_ref, late_ref, diag_ref, kept_ref):
-    place = place_ref[0]
+def totals_kernel(own_ref, mate_ref, xa_ref, yb_ref, late_ref, diag_ref, kept_ref):
+    place = lax.axis_index("ctx")
     odd, x1, y1 = (place & 1) != 0, (place >> 1) & 1, (place >> 2) & 1
     size = own_ref.shape[2] - PAD
 
@@ -155,8 +147,8 @@
         all_totals(own_ref, mate_ref)
 
 
-def row_kernel(place_ref, sent_ref, xa_ref, row_ref):
-    place = place_ref[0]
+def row_kernel(sent_ref, xa_ref, row_ref):
+    place = lax.axis_index("ctx")
     x1, y1 = (place >> 1) & 1, (place >> 2) & 1
     size = row_ref.shape[0]
 
@@ -169,8 +161,8 @@
         row_ref[...] = xa_ref[:size] + xa_ref[size : size + 1] * sent_ref[:size]
 
 
-def onward_kernel(place_ref, kept_ref, diag_ref, yb_ref, xb_ref):
-    place = place_ref[0]
+def onward_kernel(kept_ref, diag_ref, yb_ref, xb_ref):
+    place = lax.axis_index("ctx")
     x1, y1 = (place >> 1) & 1, (place >> 2) & 1
     size = xb_ref.shape[0] - PAD
 
@@ -184,8 +176,8 @@
         xb_ref[...] = yb_ref[...]
 
 
-def reach_kernel(place_ref, own_ref, mate_ref, xa_ref, yb_ref, late_ref, ya_ref, xb_ref, mine_ref, rest_ref):
-    place = place_ref[0]
+def reach_kernel(own_ref, mate_ref, xa_ref, yb_ref, late_ref, ya_ref, xb_ref, mine_ref, rest_ref):
+    place = lax.axis_index("ctx")
     odd, x1, y1 = (place & 1) != 0, (place >> 1) & 1, (place >> 2) & 1
     size = ya_ref.shape[0]
 
@@ -215,23 +207,31 @@
         spread_to(own_ref, mate_ref, mine_ref, rest_ref)
 
 
-def inside_kernel(x_ref, g_ref, b_ref, r_ref, cum_ref, step_ref, gram_ref, gram_t_ref, inner_ref, dxin_ref, db_ref, dc_ref, cumt_ref, dgram_ref):
+def inside_kernel(own, last, x_ref, g_ref, b_ref, r_ref, cum_ref, step_ref, *refs):
     heads, count = cum_ref.shape
-    total = x_ref.shape[1]
-    width = total // heads
+    if last:
+        dgram0_ref, inner_ref, dxin_ref, db_ref, dc_ref, cumt_ref, dgram_ref = refs
+    else:
+        inner_ref, dxin_ref, dgram_ref, cumt_ref = refs
+    half = inner_ref.shape[1]
+    width = 2 * half // heads
     pack = LANES // width
+    core = lax.axis_index("ctx") & 1
+    base = (core if own else 1 - core) * (half // LANES)
     t_row = lax.broadcasted_iota(jnp.int32, (count, count), 0)
     t_col = lax.broadcasted_iota(jnp.int32, (count, count), 1)
     b, r = b_ref[...], r_ref[...]
-    gram, gram_t = gram_ref[...], gram_t_ref[...]
-    cum_all = cum_ref[...]
-    cumt_ref[...] = jnp.concatenate([cum_all, jnp.zeros((LANES - heads, count), F32)], axis=0).T
+    gram = jnp.where(t_row >= t_col, mm(r, b, NT), 0.0)
+    gram_t = jnp.where(t_row <= t_col, mm(b, r, NT), 0.0)
+    cumt_ref[...] = jnp.concatenate([cum_ref[...], jnp.zeros((LANES - heads, count), F32)], axis=0).T
     step_t = step_ref[...].T
-    dgram_ref[...] = jnp.zeros_like(dgram_ref)
+    dgram_ref[...] = dgram0_ref[...] if last else jnp.zeros_like(dgram_ref)
     lane = lax.broadcasted_iota(jnp.int32, (count, LANES), 1)
 
-    def group(j, _):
+    def group(k, _):
+        j = base + k
         at = pl.multiple_of(j * LANES, LANES)
+        out = pl.ds(pl.multiple_of(k * LANES, LANES), LANES)
         x4 = x_ref[:, pl.ds(at, LANES)]
         g4 = g_ref[:, pl.ds(at, LANES)]
         cols = pltpu.roll(cumt_ref[...], LANES - j * pack, 1)
@@ -257,18 +257,19 @@
             xs.append(xm)
             gs.append(gm)
         dgram_ref[...] = dgram
-        inner_ref[:, pl.ds(at, LANES)] = mm(jnp.concatenate(his + los, axis=1), jnp.concatenate(xs + xs, axis=0))
+        inner_ref[:, out] = mm(jnp.concatenate(his + los, axis=1), jnp.concatenate(xs + xs, axis=0))
         hot = spread(heads, width, at, LANES)
         back = mm(jnp.concatenate(thi + tlo, axis=1), jnp.concatenate(gs + gs, axis=0))
-        dxin_ref[:, pl.ds(at, LANES)] = back * expand(step_t, hot)
+        dxin_ref[:, out] = back * expand(step_t, hot)
         return 0
 
-    lax.fori_loop(0, heads // pack, group, 0)
-    dgram = jnp.where(t_row >= t_col, dgram_ref[...], 0.0)
-    hi, lo = split(dgram)
-    dc_ref[...] = mm(jnp.concatenate([hi, lo], axis=1), jnp.concatenate([b, b], axis=0))
-    hi, lo = split(dgram.T)
-    db_ref[...] = mm(jnp.concatenate([hi, lo], axis=1), jnp.concatenate([r, r], axis=0))
+    lax.fori_loop(0, half // LANES, group, 0)
+    if last:
+        dgram = jnp.where(t_row >= t_col, dgram_ref[...], 0.0)
+        hi, lo = split(dgram)
+        dc_ref[...] = mm(jnp.concatenate([hi, lo], axis=1), jnp.concatenate([b, b], axis=0))
+        hi, lo = split(dgram.T)
+        db_ref[...] = mm(jnp.concatenate([hi, lo], axis=1), jnp.concatenate([r, r], axis=0))
 
 
 def lanes_of(heads, total, which):
@@ -294,10 +295,10 @@
         g = g_ref[:, here].astype(F32)
         grow_x, tail_x, skip_x = expand(grow, hot), expand(tail, hot), expand(skip, hot)[0:1]
         before, later = src[0, k], src[1, k]
-        flow = inner_ref[:, here] + grow_x * mm(r2, jnp.concatenate(split(before), axis=0))
+        flow = inner_ref[:, out] + grow_x * mm(r2, jnp.concatenate(split(before), axis=0))
         y_ref[:, out] = (flow + skip_x * x).astype(BF16)
         reach = tail_x * mm(b2, jnp.concatenate(split(later), axis=0))
-        back = dxin_ref[:, here] + reach
+        back = dxin_ref[:, out] + reach
         dx_ref[:, out] = (back + skip_x * g).astype(BF16)
         uv_hi, uv_lo = split(jnp.concatenate([g * flow, x * back], axis=0))
         uv = uv + mm(uv_hi, hot, NT) + mm(uv_lo, hot, NT)
@@ -323,10 +324,10 @@
 
 
 def first_kernel(
-    place_ref, x_ref, g_ref, b_ref, r_ref, raw_ref, par_ref, inner_ref, dxin_ref, src_ref, cum_ref, step_ref,
+    x_ref, g_ref, b_ref, r_ref, raw_ref, par_ref, inner_ref, dxin_ref, src_ref, cum_ref, step_ref,
     db0_ref, dc0_ref, y_ref, dx_ref, uv_ref, sums_ref, db_ref, dc_ref,
 ):
-    c = place_ref[0] & 1
+    c = lax.axis_index("ctx") & 1
     uv, sums = jnp.zeros(uv_ref.shape, F32), jnp.zeros(sums_ref.shape, F32)
     uv_ref[...], sums_ref[...], _ = carried(
         c, src_ref, x_ref, g_ref, b_ref, r_ref, raw_ref[...], par_ref[...], inner_ref, dxin_ref, uv, sums, y_ref, dx_ref
@@ -337,11 +338,11 @@
 
 
 def second_kernel(
-    groups, place_ref, x_ref, g_ref, b_ref, r_ref, raw_ref, par_ref, inner_ref, dxin_ref, src_ref,
+    groups, x_ref, g_ref, b_ref, r_ref, raw_ref, par_ref, inner_ref, dxin_ref, src_ref,
     uv0_ref, sums0_ref, y_ref, dx_ref, draw_ref, tot_ref, col_ref, rel_ref,
 ):
     heads, count = raw_ref.shape
-    other = 1 - (place_ref[0] & 1)
+    other = 1 - (lax.axis_index("ctx") & 1)
     uv, sums, (z, step, scale, logdecay, cum, upper) = carried(
         other, src_ref, x_ref, g_ref, b_ref, r_ref, raw_ref[...], par_ref[...], inner_ref, dxin_ref,
         uv0_ref[...], sums0_ref[...], y_ref, dx_ref,
@@ -360,15 +361,15 @@
     rate_sum = jnp.sum(dlog * logdecay, axis=1, keepdims=True)
     bias_sum = jnp.sum(draw, axis=1, keepdims=True)
     col_ref[...] = jnp.where(column == 0, rate_sum, jnp.where(column == 1, bias_sum, jnp.where(column == 2, skip_sum, 0.0)))
-    relative(groups, place_ref[1], heads // groups, col_ref, rel_ref)
+    relative(groups, lax.axis_index("dp"), heads // groups, col_ref, rel_ref)
     tot_ref[...] = rel_ref[...].T[:PAD]
 
 
 def third_kernel(
-    place_ref, x_ref, g_ref, cum_ref, step_ref, src_ref, db0_ref, dc0_ref, y0_ref, dx0_ref, y1_ref, dx1_ref,
+    x_ref, g_ref, cum_ref, step_ref, src_ref, db0_ref, dc0_ref, y0_ref, dx0_ref, y1_ref, dx1_ref,
     y_ref, dx_ref, db_ref, dc_ref,
 ):
-    c = place_ref[0] & 1
+    c = lax.axis_index("ctx") & 1
     half = x_ref.shape[1] // 2
     for which, ys, dxs in ((c, y0_ref, dx0_ref), (1 - c, y1_ref, dx1_ref)):
         at = pl.ds(pl.multiple_of(which * half, half), half)
@@ -379,13 +380,11 @@
     )
 
 
-def call(kernel, outs, args, scratch=(), flops=0, scalar=False, off_chip=False):
+def call(kernel, outs, args, scratch=(), flops=0, off_chip=False):
     if off_chip:
         args = tuple(pltpu.with_memory_space_constraint(a, pltpu.HBM) for a in args)
     vmem = pl.BlockSpec(memory_space=pltpu.VMEM)
     specs = [pl.BlockSpec(memory_space=pltpu.HBM) if off_chip else vmem] * len(args)
-    if scalar:
-        specs[0] = pl.BlockSpec(memory_space=pltpu.SMEM)
     size = sum(a.size * a.dtype.itemsize for a in (*args, *outs))
     return pl.pallas_call(
         kernel,
@@ -480,24 +479,22 @@
     return mine, theirs
 
 
-def spread_planned(place, own, mate, size):
+def spread_planned(own, mate, size):
     part = own.shape[-1]
     message = jax.ShapeDtypeStruct((size + PAD, part), F32)
     row = jax.ShapeDtypeStruct((size, part), F32)
     ends = jax.ShapeDtypeStruct((PAD, part), F32)
     both = jax.ShapeDtypeStruct((2, 2, size, part), F32)
-    to_xa, to_yb, to_late, to_diag, kept = call(
-        totals_kernel, (message, message, message, ends, message), (place, own, mate), scalar=True
-    )
+    to_xa, to_yb, to_late, to_diag, kept = call(totals_kernel, (message, message, message, ends, message), (own, mate))
     diag = swap(to_diag, "ctx", 6)
     xa = swap(to_xa, "ctx", 2)
     yb = swap(to_yb, "ctx", 4)
     late = swap(to_late, "ctx", 2)
-    (to_ya,) = call(row_kernel, (row,), (place, to_xa, xa), scalar=True)
+    (to_ya,) = call(row_kernel, (row,), (to_xa, xa))
     ya = swap(to_ya, "ctx", 4)
-    (to_xb,) = call(onward_kernel, (message,), (place, kept, diag, yb), scalar=True)
+    (to_xb,) = call(onward_kernel, (message,), (kept, diag, yb))
     xb = swap(to_xb, "ctx", 2)
-    return call(reach_kernel, (both, both), (place, own, mate, xa, yb, late, ya, xb), scalar=True)
+    return call(reach_kernel, (both, both), (own, mate, xa, yb, late, ya, xb))
 
 
 def layer(x, b, r, raw, rate, bias, skip, g):
@@ -507,11 +504,9 @@
     part = half // 2
     groups = lax.axis_size("dp")
     shape = jax.ShapeDtypeStruct
-    place = jnp.stack([lax.axis_index("ctx"), lax.axis_index("dp")]).astype(jnp.int32)
     got = gathered(jnp.stack([rate, bias, skip]), "dp")
     message = shape((2, 2, size + PAD, part), F32)
     small = shape((heads, count), F32)
-    wide = shape((count, total), F32)
     square = shape((count, size), F32)
     mixed = shape((count, count), F32)
     columns = shape((heads, LANES), F32)
@@ -522,40 +517,42 @@
     )
     own, oth, cum, step, par = call(
         functools.partial(ends_kernel, groups),
-        (message, message, small, small, columns), (place, x, g, b, r, raw, got),
-        scratch=[pltpu.VMEM((heads, LANES), F32)], flops=10**9, scalar=True,
+        (message, message, small, small, columns), (x, g, b, r, raw, got),
+        scratch=[pltpu.VMEM((heads, LANES), F32)], flops=10**9,
     )
     mate = swap(oth, "ctx", 1)
     if planned(lax.axis_size("ctx")):
-        mine, theirs = spread_planned(place, own, mate, size)
+        mine, theirs = spread_planned(own, mate, size)
     else:
         mine, theirs = spread_generally(own, mate, size)
-    gram, gram_t = call(gram_kernel, (mixed, mixed), (b, r), flops=10**7)
-    inner, dxin, db0, dc0 = call(
-        inside_kernel,
-        (wide, wide, square, square),
-        (x, g, b, r, cum, step, gram, gram_t),
-        scratch=[pltpu.VMEM((count, LANES), F32), pltpu.VMEM((count, count), F32)],
-        flops=10**9,
+    halves = shape((count, half), F32)
+    inner0, dxin0, dgram = call(
+        functools.partial(inside_kernel, True, False), (halves, halves, mixed), (x, g, b, r, cum, step),
+        scratch=[pltpu.VMEM((count, LANES), F32)], flops=10**9,
+    )
+    inner1, dxin1, db0, dc0 = call(
+        functools.partial(inside_kernel, False, True), (halves, halves, square, square),
+        (x, g, b, r, cum, step, dgram),
+        scratch=[pltpu.VMEM((count, LANES), F32), pltpu.VMEM((count, count), F32)], flops=10**9,
     )
     rest = swap(theirs, "ctx", 1)
-    ready = (place, x, g, b, r, raw, par, inner, dxin)
+    ready = (x, g, b, r, raw, par)
     halved = shape((count, half), BF16)
     whole = shape((count, total), BF16)
     y0, dx0, uv, sums, db1, dc1 = call(
         first_kernel,
         (halved, halved, shape((2 * count, heads), F32), shape((3 * PAD, heads), F32), square, square),
-        (*ready, mine, cum, step, db0, dc0), flops=10**9, scalar=True,
+        (*ready, inner0, dxin0, mine, cum, step, db0, dc0), flops=10**9,
     )
     y1, dx1, draw, tot = call(
         functools.partial(second_kernel, groups), (halved, halved, small, shape((PAD, heads), F32)),
-        (*ready, rest, uv, sums),
-        scratch=[pltpu.VMEM((heads, LANES), F32), pltpu.VMEM((heads, LANES), F32)], flops=10**9, scalar=True,
+        (*ready, inner1, dxin1, rest, uv, sums),
+        scratch=[pltpu.VMEM((heads, LANES), F32), pltpu.VMEM((heads, LANES), F32)], flops=10**9,
     )
     owned = owned_sum(total_sum(tot, "ctx"), "dp")
     y, dx, db, dc = call(
         third_kernel, (whole, whole, square, square),
-        (place, x, g, cum, step, rest, db1, dc1, y0, dx0, y1, dx1), flops=10**9, scalar=True,
+        (x, g, cum, step, rest, db1, dc1, y0, dx0, y1, dx1), flops=10**9,
     )
     return (y[None], dx[None], db[None], dc[None], draw[None], owned[0], owned[1], owned[2])
 

time: 73.9 us -> 70.8 us (0.958)
  Pallas kernels: 23.7 us -> 19.5 us
  waiting for transfers between devices: 25.2 us -> 26.5 us
    pallas_call x11, Pallas kernels: 23.7 us -> 19.5 us  [call(): pl.pallas_call(kernel, out_shape=outs, in_specs=specs, out_specs=tuple([v...]
    ppermute x15, waiting for transfers between devices: 25.2 us -> 26.5 us  [swap(): lax.ppermute(value, axis, [(i, i ^ bit) for i in range(lax.axis_size(axis...]
  transfers between devices with their start and end apart: 15 -> 15, of which waited for: 11 -> 12; matrix products, arithmetic and copies ran while one was open for 0% -> 0% of each run, Pallas kernels for 23% -> 21%
where the time goes in v4:
time: 70.8 us; the launch traced here: 70.6 us
  waiting for transfers between devices  26.5 us (37%)
  starting transfers between devices  21.6 us (31%)
  Pallas kernels  19.5 us (28%)
  other arithmetic  1.58 us (2%)
  between operations  0.75 us (1%)
    ppermute x15, waiting for transfers between devices, swap(): lax.ppermute(value, axis, [(i, i ^ bit) for i in range(lax.axis_size(axis...  26.5 us
    ppermute x15, starting transfers between devices, swap(): lax.ppermute(value, axis, [(i, i ^ bit) for i in range(lax.axis_size(axis...  21.6 us
    pallas_call x11, Pallas kernels, call(): pl.pallas_call(kernel, out_shape=outs, in_specs=specs, out_specs=tuple([v...  19.5 us
  transfers between devices with their start and end apart: 15, of which 12 were waited for; matrix products, arithmetic and copies ran while one was open for 0% of the time, Pallas kernels for 21%

profile of v4, /device:TPU:0, one launch (start us, length us, event | category | flops | bytes accessed | tf_op | source)
XLA Modules:
  0.0 70.6 jit_solution(17960470280972483792)
XLA Ops:
  0.7 0.7 %pad_maximum_fusion = f32[3,16]{1,0:T(4,128)S(1)} fusion(f32[1,16]{1,0:T(1,128)} %bitcast.24, f32[1,16]{1,0:T(1,128)} %bitcast.27, f32[1,16]{1,0:T(1,128)} %bitcast.30), kind=kLoop, calls=%fused_computation.2 | loop fusion | flops 96 | bytes 384 | tf_op jit(solution)/shard_map/stack | solution.py:507
  1.4 3.1 %collective-permute-start = (f32[3,16]{1,0:T(4,128)S(1)}, f32[3,16]{1,0:T(4,128)S(1)}, u32[]{:S(2)}, u32[]{:S(2)}) collective-permute-start(f32[3,16]{1,0:T(4,128)S(1)} %pad_maximum_fusion), channel_id=1, source_target_pairs={{0,8},{8,0},{16,24},{24,16},{1,9},{9,1},{17,25},{25,17},{2,10},{10... | collective-permute-start | bytes 584 | tf_op jit(solution)/shard_map/ppermute | solution.py:401
  4.5 1.6 %collective-permute-done = f32[3,16]{1,0:T(4,128)S(1)} collective-permute-done((f32[3,16]{1,0:T(4,128)S(1)}, f32[3,16]{1,0:T(4,128)S(1)}, u32[]{:S(2)}, u32[]{:S(2)}) %collective-permute-start) | collective-permute-done | bytes 224 | tf_op jit(solution)/shard_map/ppermute | solution.py:401
  6.1 0.8 %pad_maximum_fusion.1 = f32[3,32]{1,0:T(4,128)S(1)} fusion(f32[3,16]{1,0:T(4,128)S(1)} %collective-permute-done, f32[1,16]{1,0:T(1,128)} %bitcast.25, f32[1,16]{1,0:T(1,128)} %bitcast.28, f32[1,16]{1,0:T(1,128)} %bitcast.31), kind=kLoop, calls=%fused_computation.3 | loop fusion | flops 288 | bytes 768 | tf_op jit(solution)/shard_map/concatenate | solution.py:407
  6.8 3.0 %collective-permute-start.1 = (f32[3,32]{1,0:T(4,128)S(1)}, f32[3,32]{1,0:T(4,128)S(1)}, u32[]{:S(2)}, u32[]{:S(2)}) collective-permute-start(f32[3,32]{1,0:T(4,128)S(1)} %pad_maximum_fusion.1), channel_id=1, source_target_pairs={{0,16},{8,24},{16,0},{24,8},{1,17},{9,25},{17,1},{25,9},{2,18},{10... | collective-permute-start | bytes 1160 | tf_op jit(solution)/shard_map/ppermute | solution.py:401
  9.9 1.2 %shard_map.143 = (bf16[128,2048]{1,0:T(8,128)(2,1)S(1)}, bf16[128,2048]{1,0:T(8,128)(2,1)S(1)}, bf16[128,128]{1,0:T(8,128)(2,1)S(1)}, bf16[128,128]{1,0:T(8,128)(2,1)S(1)}, f32[64,128]{1,0:T(8,128)S(1)}) custom-call(bf16[128,2048]{1,0:T(8,128)(2,1)} %bitcast.19, bf16[128,2048]{1,0:T(8,128)(2,1)} %bitcast.20, bf16[128,128]{1,0:T(8,128)(2,1)} %bitcast.21, ...), custom_call_target="tpu_custom_call" | custom-call | bytes 2293760 | tf_op jit(solution)/shard_map/pallas_call | solution.py:389
  11.5 1.9 %shard_map.144 = (f32[2,2,136,512]{3,2,1,0:T(8,128)S(1)}, f32[2,2,136,512]{3,2,1,0:T(8,128)S(1)}, f32[64,128]{1,0:T(8,128)S(1)}, f32[64,128]{1,0:T(8,128)S(1)}, f32[64,128]{1,0:T(8,128)S(1)}) custom-call(bf16[128,2048]{1,0:T(8,128)(2,1)S(1)} %get-tuple-element.46.x_ref, bf16[128,2048]{1,0:T(8,128)(2,1)S(1)} %get-tuple-element.47.g_ref, ...), custom_call_target="tpu_custom_call" | custom-call | flops 1000000000 | bytes 3474176 | tf_op jit(solution)/shard_map/pallas_call | solution.py:389
  13.5 2.7 %collective-permute-done.2.mate_ref = f32[2,2,136,512]{3,2,1,0:T(8,128)S(1)} collective-permute-done((f32[2,2,136,512]{3,2,1,0:T(8,128)S(1)}, f32[2,2,136,512]{3,2,1,0:T(8,128)S(1)}, u32[]{:S(2)}, u32[]{:S(2)}) %collective-permute-start.2) | collective-permute-done | bytes 1114144 | tf_op jit(solution)/shard_map/ppermute | solution.py:401
  16.4 1.9 %collective-permute-start.4 = (f32[136,512]{1,0:T(8,128)S(1)}, f32[136,512]{1,0:T(8,128)S(1)}, u32[]{:S(2)}, u32[]{:S(2)}) collective-permute-start(f32[136,512]{1,0:T(8,128)S(1)} %get-tuple-element.56), channel_id=1, source_target_pairs={{0,4},{1,5},{2,6},{3,7},{4,0},{5,1},{6,2},{7,3},{8,12},{9,13},{10,... | collective-permute-start | bytes 835592 | tf_op jit(solution)/shard_map/ppermute | solution.py:401
  18.3 1.5 %collective-permute-start.3 = (f32[136,512]{1,0:T(8,128)S(1)}, f32[136,512]{1,0:T(8,128)S(1)}, u32[]{:S(2)}, u32[]{:S(2)}) collective-permute-start(f32[136,512]{1,0:T(8,128)S(1)} %get-tuple-element.55.sent_ref), channel_id=1, source_target_pairs={{0,2},{1,3},{2,0},{3,1},{4,6},{5,7},{6,4},{7,5},{8,10},{9,11},{10,... | collective-permute-start | bytes 835592 | tf_op jit(solution)/shard_map/ppermute | solution.py:401
  19.9 1.8 %collective-permute-start.5 = (f32[136,512]{1,0:T(8,128)S(1)}, f32[136,512]{1,0:T(8,128)S(1)}, u32[]{:S(2)}, u32[]{:S(2)}) collective-permute-start(f32[136,512]{1,0:T(8,128)S(1)} %get-tuple-element.57), channel_id=1, source_target_pairs={{0,2},{1,3},{2,0},{3,1},{4,6},{5,7},{6,4},{7,5},{8,10},{9,11},{10,... | collective-permute-start | bytes 835592 | tf_op jit(solution)/shard_map/ppermute | solution.py:401
  21.8 6.0 %collective-permute-done.7.diag_ref = f32[8,512]{1,0:T(8,128)S(1)} collective-permute-done((f32[8,512]{1,0:T(8,128)S(1)}, f32[8,512]{1,0:T(8,128)S(1)}, u32[]{:S(2)}, u32[]{:S(2)}) %collective-permute-start.7) | collective-permute-done | bytes 16416 | tf_op jit(solution)/shard_map/ppermute | solution.py:401
  27.8 1.9 %collective-permute-start.8 = (f32[136,512]{1,0:T(8,128)S(1)}, f32[136,512]{1,0:T(8,128)S(1)}, u32[]{:S(2)}, u32[]{:S(2)}) collective-permute-start(f32[136,512]{1,0:T(8,128)S(1)} %shard_map.147), channel_id=1, source_target_pairs={{0,2},{1,3},{2,0},{3,1},{4,6},{5,7},{6,4},{7,5},{8,10},{9,11},{10,... | collective-permute-start | bytes 835592 | tf_op jit(solution)/shard_map/ppermute | solution.py:401
  29.8 1.6 %collective-permute-start.6 = (f32[128,512]{1,0:T(8,128)S(1)}, f32[128,512]{1,0:T(8,128)S(1)}, u32[]{:S(2)}, u32[]{:S(2)}) collective-permute-start(f32[128,512]{1,0:T(8,128)S(1)} %shard_map.146), channel_id=1, source_target_pairs={{0,4},{1,5},{2,6},{3,7},{4,0},{5,1},{6,2},{7,3},{8,12},{9,13},{10,... | collective-permute-start | bytes 786440 | tf_op jit(solution)/shard_map/ppermute | solution.py:401
  31.3 2.8 %collective-permute-done.5.late_ref = f32[136,512]{1,0:T(8,128)S(1)} collective-permute-done((f32[136,512]{1,0:T(8,128)S(1)}, f32[136,512]{1,0:T(8,128)S(1)}, u32[]{:S(2)}, u32[]{:S(2)}) %collective-permute-start.5) | collective-permute-done | bytes 278560 | tf_op jit(solution)/shard_map/ppermute | solution.py:401
  34.2 2.1 %collective-permute-done.6.ya_ref = f32[128,512]{1,0:T(8,128)S(1)} collective-permute-done((f32[128,512]{1,0:T(8,128)S(1)}, f32[128,512]{1,0:T(8,128)S(1)}, u32[]{:S(2)}, u32[]{:S(2)}) %collective-permute-start.6) | collective-permute-done | bytes 262176 | tf_op jit(solution)/shard_map/ppermute | solution.py:401
  36.2 2.8 %collective-permute-done.8.xb_ref = f32[136,512]{1,0:T(8,128)S(1)} collective-permute-done((f32[136,512]{1,0:T(8,128)S(1)}, f32[136,512]{1,0:T(8,128)S(1)}, u32[]{:S(2)}, u32[]{:S(2)}) %collective-permute-start.8) | collective-permute-done | bytes 278560 | tf_op jit(solution)/shard_map/ppermute | solution.py:401
  39.4 4.3 %shard_map.149 = (f32[128,1024]{1,0:T(8,128)S(1)}, f32[128,1024]{1,0:T(8,128)S(1)}, f32[128,128]{1,0:T(8,128)S(1)}) custom-call(bf16[128,2048]{1,0:T(8,128)(2,1)S(1)} %get-tuple-element.46.x_ref, bf16[128,2048]{1,0:T(8,128)(2,1)S(1)} %get-tuple-element.47.g_ref, bf16[128,128]{1,0:T(8,128)(2,1)S(1)} %get-tuple-element.48.b_ref, ...), custom_call_target="tpu_custom_call" | custom-call | flops 1000000000 | bytes 2293760 | tf_op jit(solution)/shard_map/pallas_call | solution.py:389
  43.7 4.6 %shard_map.150 = (f32[128,1024]{1,0:T(8,128)S(1)}, f32[128,1024]{1,0:T(8,128)S(1)}, f32[128,128]{1,0:T(8,128)S(1)}, f32[128,128]{1,0:T(8,128)S(1)}) custom-call(bf16[128,2048]{1,0:T(8,128)(2,1)S(1)} %get-tuple-element.46.x_ref, bf16[128,2048]{1,0:T(8,128)(2,1)S(1)} %get-tuple-element.47.g_ref, bf16[128,128]{1,0:T(8,128)(2,1)S(1)} %get-tuple-element.48.b_ref, ...), custom_call_target="tpu_custom_call" | custom-call | flops 1000000000 | bytes 2424832 | tf_op jit(solution)/shard_map/pallas_call | solution.py:389
  48.3 2.4 %shard_map.151 = (bf16[128,1024]{1,0:T(8,128)(2,1)S(1)}, bf16[128,1024]{1,0:T(8,128)(2,1)S(1)}, f32[256,64]{1,0:T(8,128)S(1)}, f32[24,64]{1,0:T(8,128)S(1)}, f32...) custom-call(bf16[128,2048]{1,0:T(8,128)(2,1)S(1)} %get-tuple-element.46.x_ref, ...), custom_call_target="tpu_custom_call" | custom-call | flops 1000000000 | bytes 4200448 | tf_op jit(solution)/shard_map/pallas_call | solution.py:389
  50.7 2.6 %shard_map.152 = (bf16[128,1024]{1,0:T(8,128)(2,1)S(1)}, bf16[128,1024]{1,0:T(8,128)(2,1)S(1)}, f32[64,128]{1,0:T(8,128)}, f32[8,64]{1,0:T(8,128)S(1)}) custom-call(bf16[128,2048]{1,0:T(8,128)(2,1)S(1)} %get-tuple-element.46.x_ref, bf16[128,2048]{1,0:T(8,128)(2,1)S(1)} %get-tuple-element.47.g_ref, bf16[128,128]{1,0:T(8,128)(2,1)S(1)} %get-tuple-element.48.b_ref, ...), custom_call_target="tpu_custom_call" | custom-call | flops 1000000000 | bytes 3907584 | tf_op jit(solution)/shard_map/pallas_call | solution.py:389
  53.3 0.5 collective-permute-start.10
  53.8 0.8 %collective-permute-done.10 = f32[8,64]{1,0:T(8,128)S(1)} collective-permute-done((f32[8,64]{1,0:T(8,128)S(1)}, f32[8,64]{1,0:T(8,128)S(1)}, u32[]{:S(2)}, u32[]{:S(2)}) %collective-permute-start.10) | collective-permute-done | bytes 2080 | tf_op jit(solution)/shard_map/ppermute | solution.py:401
  54.6 1.5 %collective-permute-start.11 = (f32[8,64]{1,0:T(8,128)S(1)}, f32[8,64]{1,0:T(8,128)S(1)}, u32[]{:S(2)}, u32[]{:S(2)}) collective-permute-start(f32[8,64]{1,0:T(8,128)S(1)} %add.15), channel_id=1, source_target_pairs={{0,2},{1,3},{2,0},{3,1},{4,6},{5,7},{6,4},{7,5},{8,10},{9,11},{10,... | collective-permute-start | bytes 6152 | tf_op jit(solution)/shard_map/ppermute | solution.py:401
  56.1 2.1 %collective-permute-done.11 = f32[8,64]{1,0:T(8,128)S(1)} collective-permute-done((f32[8,64]{1,0:T(8,128)S(1)}, f32[8,64]{1,0:T(8,128)S(1)}, u32[]{:S(2)}, u32[]{:S(2)}) %collective-permute-start.11) | collective-permute-done | bytes 2080 | tf_op jit(solution)/shard_map/ppermute | solution.py:401
  58.2 0.4 collective-permute-start.12
  58.6 3.3 %collective-permute-done.12 = f32[8,64]{1,0:T(8,128)S(1)} collective-permute-done((f32[8,64]{1,0:T(8,128)S(1)}, f32[8,64]{1,0:T(8,128)S(1)}, u32[]{:S(2)}, u32[]{:S(2)}) %collective-permute-start.12) | collective-permute-done | bytes 2080 | tf_op jit(solution)/shard_map/ppermute | solution.py:401
  61.9 2.6 %collective-permute-start.13 = (f32[8,32]{1,0:T(8,128)S(1)}, f32[8,32]{1,0:T(8,128)S(1)}, u32[]{:S(2)}, u32[]{:S(2)}) collective-permute-start(f32[8,32]{1,0:T(8,128)S(1)} %split.13), channel_id=1, source_target_pairs={{0,16},{8,24},{16,0},{24,8},{1,17},{9,25},{17,1},{25,9},{2,18},{10... | collective-permute-start | bytes 3080 | tf_op jit(solution)/shard_map/ppermute | solution.py:401
  64.5 1.9 %collective-permute-done.13 = f32[8,32]{1,0:T(8,128)S(1)} collective-permute-done((f32[8,32]{1,0:T(8,128)S(1)}, f32[8,32]{1,0:T(8,128)S(1)}, u32[]{:S(2)}, u32[]{:S(2)}) %collective-permute-start.13) | collective-permute-done | bytes 1056 | tf_op jit(solution)/shard_map/ppermute | solution.py:401
  66.5 1.6 %collective-permute-start.14 = (f32[8,16]{1,0:T(8,128)S(1)}, f32[8,16]{1,0:T(8,128)S(1)}, u32[]{:S(2)}, u32[]{:S(2)}) collective-permute-start(f32[8,16]{1,0:T(8,128)S(1)} %split.15), channel_id=1, source_target_pairs={{0,8},{8,0},{16,24},{24,16},{1,9},{9,1},{17,25},{25,17},{2,10},{10... | collective-permute-start | bytes 1544 | tf_op jit(solution)/shard_map/ppermute | solution.py:401
  68.1 2.0 %shard_map.153 = (bf16[128,2048]{1,0:T(8,128)(2,1)}, bf16[128,2048]{1,0:T(8,128)(2,1)}, f32[128,128]{1,0:T(8,128)}, f32[128,128]{1,0:T(8,128)}) custom-call(bf16[128,2048]{1,0:T(8,128)(2,1)S(1)} %get-tuple-element.46.x_ref, bf16[128,2048]{1,0:T(8,128)(2,1)S(1)} %get-tuple-element.47.g_ref, f32[64,128]{1,0:T(8,128)S(1)} %get-tuple-element.51.cum_ref, ...), custom_call_target="tpu_custom_call" | custom-call | flops 1000000000 | bytes 4521984 | tf_op jit(solution)/shard_map/pallas_call | solution.py:389
  70.1 0.5 slice_bitcast_fusion
  (26 shorter events, 1.3 us)
Async XLA Ops:
  0.6 10.8 %copy-start = (f32[16]{0:T(128)S(1)}, f32[16]{0:T(128)}, u32[]{:S(2)}) copy-start(f32[16]{0:T(128)} %param.14) | copy-start | bytes 196
  0.6 10.8 %copy-start.1 = (f32[16]{0:T(128)S(1)}, f32[16]{0:T(128)}, u32[]{:S(2)}) copy-start(f32[16]{0:T(128)} %param.13) | copy-start | bytes 196
  0.7 10.8 %copy-start.2 = (f32[16]{0:T(128)S(1)}, f32[16]{0:T(128)}, u32[]{:S(2)}) copy-start(f32[16]{0:T(128)} %param.12) | copy-start | bytes 196
  1.4 4.7 %collective-permute-start = (f32[3,16]{1,0:T(4,128)S(1)}, f32[3,16]{1,0:T(4,128)S(1)}, u32[]{:S(2)}, u32[]{:S(2)}) collective-permute-start(f32[3,16]{1,0:T(4,128)S(1)} %pad_maximum_fusion), channel_id=1, source_target_pairs={{0,8},{8,0},{16,24},{24,16},{1,9},{9,1},{17,25},{25,17},{2,10},{10... | collective-permute-start | bytes 584 | tf_op jit(solution)/shard_map/ppermute | solution.py:401
  6.8 4.6 %collective-permute-start.1 = (f32[3,32]{1,0:T(4,128)S(1)}, f32[3,32]{1,0:T(4,128)S(1)}, u32[]{:S(2)}, u32[]{:S(2)}) collective-permute-start(f32[3,32]{1,0:T(4,128)S(1)} %pad_maximum_fusion.1), channel_id=1, source_target_pairs={{0,16},{8,24},{16,0},{24,8},{1,17},{9,25},{17,1},{25,9},{2,18},{10... | collective-permute-start | bytes 1160 | tf_op jit(solution)/shard_map/ppermute | solution.py:401
  13.4 2.8 %collective-permute-start.2 = (f32[2,2,136,512]{3,2,1,0:T(8,128)S(1)}, f32[2,2,136,512]{3,2,1,0:T(8,128)S(1)}, u32[]{:S(2)}, u32[]{:S(2)}) collective-permute-start(f32[2,2,136,512]{3,2,1,0:T(8,128)S(1)} %get-tuple-element.54), channel_id=1, source_target_pairs={{0,1},{1,0},{2,3},{3,2},{4,5},{5,4},{6,7},{7,6},{8,9},{9,8},{10,11... | collective-permute-start | bytes 3342344 | tf_op jit(solution)/shard_map/ppermute | solution.py:401
  16.4 11.4 %collective-permute-start.4 = (f32[136,512]{1,0:T(8,128)S(1)}, f32[136,512]{1,0:T(8,128)S(1)}, u32[]{:S(2)}, u32[]{:S(2)}) collective-permute-start(f32[136,512]{1,0:T(8,128)S(1)} %get-tuple-element.56), channel_id=1, source_target_pairs={{0,4},{1,5},{2,6},{3,7},{4,0},{5,1},{6,2},{7,3},{8,12},{9,13},{10,... | collective-permute-start | bytes 835592 | tf_op jit(solution)/shard_map/ppermute | solution.py:401
  18.3 11.4 %collective-permute-start.3 = (f32[136,512]{1,0:T(8,128)S(1)}, f32[136,512]{1,0:T(8,128)S(1)}, u32[]{:S(2)}, u32[]{:S(2)}) collective-permute-start(f32[136,512]{1,0:T(8,128)S(1)} %get-tuple-element.55.sent_ref), channel_id=1, source_target_pairs={{0,2},{1,3},{2,0},{3,1},{4,6},{5,7},{6,4},{7,5},{8,10},{9,11},{10,... | collective-permute-start | bytes 835592 | tf_op jit(solution)/shard_map/ppermute | solution.py:401
  19.8 8.0 %collective-permute-start.7 = (f32[8,512]{1,0:T(8,128)S(1)}, f32[8,512]{1,0:T(8,128)S(1)}, u32[]{:S(2)}, u32[]{:S(2)}) collective-permute-start(f32[8,512]{1,0:T(8,128)S(1)} %get-tuple-element.59), channel_id=1, source_target_pairs={{0,6},{1,7},{2,4},{3,5},{4,2},{5,3},{6,0},{7,1},{8,14},{9,15},{10,... | collective-permute-start | bytes 49160 | tf_op jit(solution)/shard_map/ppermute | solution.py:401
  19.9 14.2 %collective-permute-start.5 = (f32[136,512]{1,0:T(8,128)S(1)}, f32[136,512]{1,0:T(8,128)S(1)}, u32[]{:S(2)}, u32[]{:S(2)}) collective-permute-start(f32[136,512]{1,0:T(8,128)S(1)} %get-tuple-element.57), channel_id=1, source_target_pairs={{0,2},{1,3},{2,0},{3,1},{4,6},{5,7},{6,4},{7,5},{8,10},{9,11},{10,... | collective-permute-start | bytes 835592 | tf_op jit(solution)/shard_map/ppermute | solution.py:401
  27.8 11.2 %collective-permute-start.8 = (f32[136,512]{1,0:T(8,128)S(1)}, f32[136,512]{1,0:T(8,128)S(1)}, u32[]{:S(2)}, u32[]{:S(2)}) collective-permute-start(f32[136,512]{1,0:T(8,128)S(1)} %shard_map.147), channel_id=1, source_target_pairs={{0,2},{1,3},{2,0},{3,1},{4,6},{5,7},{6,4},{7,5},{8,10},{9,11},{10,... | collective-permute-start | bytes 835592 | tf_op jit(solution)/shard_map/ppermute | solution.py:401
  29.8 6.4 %collective-permute-start.6 = (f32[128,512]{1,0:T(8,128)S(1)}, f32[128,512]{1,0:T(8,128)S(1)}, u32[]{:S(2)}, u32[]{:S(2)}) collective-permute-start(f32[128,512]{1,0:T(8,128)S(1)} %shard_map.146), channel_id=1, source_target_pairs={{0,4},{1,5},{2,6},{3,7},{4,0},{5,1},{6,2},{7,3},{8,12},{9,13},{10,... | collective-permute-start | bytes 786440 | tf_op jit(solution)/shard_map/ppermute | solution.py:401
  39.3 11.4 %collective-permute-start.9 = (f32[2,2,128,512]{3,2,1,0:T(8,128)S(1)}, f32[2,2,128,512]{3,2,1,0:T(8,128)S(1)}, u32[]{:S(2)}, u32[]{:S(2)}) collective-permute-start(f32[2,2,128,512]{3,2,1,0:T(8,128)S(1)} %get-tuple-element.60), channel_id=1, source_target_pairs={{0,1},{1,0},{2,3},{3,2},{4,5},{5,4},{6,7},{7,6},{8,9},{9,8},{10,11... | collective-permute-start | bytes 3145736 | tf_op jit(solution)/shard_map/ppermute | solution.py:401
  53.3 1.3 %collective-permute-start.10 = (f32[8,64]{1,0:T(8,128)S(1)}, f32[8,64]{1,0:T(8,128)S(1)}, u32[]{:S(2)}, u32[]{:S(2)}) collective-permute-start(f32[8,64]{1,0:T(8,128)S(1)} %get-tuple-element.83), channel_id=1, source_target_pairs={{0,1},{1,0},{2,3},{3,2},{4,5},{5,4},{6,7},{7,6},{8,9},{9,8},{10,11... | collective-permute-start | bytes 6152 | tf_op jit(solution)/shard_map/ppermute | solution.py:401
  54.6 3.6 %collective-permute-start.11 = (f32[8,64]{1,0:T(8,128)S(1)}, f32[8,64]{1,0:T(8,128)S(1)}, u32[]{:S(2)}, u32[]{:S(2)}) collective-permute-start(f32[8,64]{1,0:T(8,128)S(1)} %add.15), channel_id=1, source_target_pairs={{0,2},{1,3},{2,0},{3,1},{4,6},{5,7},{6,4},{7,5},{8,10},{9,11},{10,... | collective-permute-start | bytes 6152 | tf_op jit(solution)/shard_map/ppermute | solution.py:401
  58.2 3.6 %collective-permute-start.12 = (f32[8,64]{1,0:T(8,128)S(1)}, f32[8,64]{1,0:T(8,128)S(1)}, u32[]{:S(2)}, u32[]{:S(2)}) collective-permute-start(f32[8,64]{1,0:T(8,128)S(1)} %add.16), channel_id=1, source_target_pairs={{0,4},{1,5},{2,6},{3,7},{4,0},{5,1},{6,2},{7,3},{8,12},{9,13},{10,... | collective-permute-start | bytes 6152 | tf_op jit(solution)/shard_map/ppermute | solution.py:401
  61.9 4.5 %collective-permute-start.13 = (f32[8,32]{1,0:T(8,128)S(1)}, f32[8,32]{1,0:T(8,128)S(1)}, u32[]{:S(2)}, u32[]{:S(2)}) collective-permute-start(f32[8,32]{1,0:T(8,128)S(1)} %split.13), channel_id=1, source_target_pairs={{0,16},{8,24},{16,0},{24,8},{1,17},{9,25},{17,1},{25,9},{2,18},{10... | collective-permute-start | bytes 3080 | tf_op jit(solution)/shard_map/ppermute | solution.py:401
  66.5 3.6 %collective-permute-start.14 = (f32[8,16]{1,0:T(8,128)S(1)}, f32[8,16]{1,0:T(8,128)S(1)}, u32[]{:S(2)}, u32[]{:S(2)}) collective-permute-start(f32[8,16]{1,0:T(8,128)S(1)} %split.15), channel_id=1, source_target_pairs={{0,8},{8,0},{16,24},{24,16},{1,9},{9,1},{17,25},{25,17},{2,10},{10... | collective-permute-start | bytes 1544 | tf_op jit(solution)/shard_map/ppermute | solution.py:401
